TPU v7x, 128 devices: a whole 4x4x4 slice. The times are simulated.
128 devices in a mesh: frame: 8 (over x, y_lo), band: 16 (over y_hi, z, core).
Axes of the slice: x: 4, y: 4 (y_hi: 2, y_lo: 2; y = y_hi * 2 + y_lo), z: 4, core: 2. Of those that a mesh axis runs over, the one named last changes fastest.
Arguments:
- features: bfloat16 [24, 64, 128, 128], P('frame', 'band'), may hold values from -6 to 6
- frame_pairs: int32 [24, 2], P('frame'), may hold values from 0 to 23, as said below
- conv_weight: float32 [4, 2, 2, 3, 3], replicated, may hold values from -1.5 to 1.5
- conv_bias: float32 [4, 2], replicated, may hold values from -1 to 1
Outputs:
- flows: float32 [24, 2, 2, 64, 128], P('frame', None, None, 'band')
Inputs may be any that keep to these rules, and one draw needn't show every extreme that they name: `frame_pairs`: each pair names two different frames.
All inputs are finite; a program needn't handle non-finite values.
Results may differ from a plain program's by a relative error of at most 0.0003.
Values may be sent and summed in bfloat16 or wider, within the bound.
No kernel may reach another device: no remote copies, remote signals or barrier semaphores. Data moves between devices by JAX's collectives and lax.ppermute only.
A program may use at most 128 MiB of HBM per device.

v0:
```python
import functools
import itertools
import math

import jax
import jax.numpy as jnp
from jax import lax
from jax.experimental import pallas as pl
from jax.experimental.pallas import tpu as pltpu
from jax.sharding import Mesh
from jax.sharding import PartitionSpec as P

score_gain = 2.5
AXES = ("fx", "fy", "bh", "bz", "bc")
SIZES = (4, 2, 2, 4, 2)
VMEM = pl.BlockSpec(memory_space=pltpu.VMEM)
SMEM = pl.BlockSpec(memory_space=pltpu.SMEM)
NT = (((1,), (1,)), ((), ()))


def flat(coords):
    index = 0
    for value, size in zip(coords, SIZES):
        index = index * size + value
    return index


def hop(value, move):
    route = []
    for coords in itertools.product(*(range(size) for size in SIZES)):
        target = move(*coords)
        if target is not None:
            route.append((flat(coords), flat(target)))
    return lax.ppermute(value, AXES, route)


def flip_y(x, y, h, z, c):
    return x, 1 - y, h, z, c


def flip_a(x, y, h, z, c):
    return x ^ 1, y, h, z, c


def flip_b(x, y, h, z, c):
    return 3 - x, y, h, z, c


def flip_h(x, y, h, z, c):
    return x, y, 1 - h, z, c


def flip_c(x, y, h, z, c):
    return x, y, h, z, 1 - c


def flip_za(x, y, h, z, c):
    return x, y, h, z ^ 1, c


def flip_zb(x, y, h, z, c):
    return x, y, h, 3 - z, c


def ring(x, y, h, z, c):
    return x, y, h, (z + 1 - 2 * c) % SIZES[3], c


def back(x, y, h, z, c):
    return x, y, h, (z - 1 + 2 * c) % SIZES[3], c


def by_core(first, second):
    def move(*coords):
        return (second if coords[4] else first)(*coords)

    return move


def next_chip(x, y, h, z, c):
    band = (h * SIZES[3] + z) * SIZES[4] + c + 2 * c - 1
    return x, y, band // (SIZES[3] * SIZES[4]) % SIZES[2], band // SIZES[4] % SIZES[3], band % SIZES[4]


def gray(x):
    return (x ^ (x >> 1)) & 1, x >> 1


def pick_kernel(table_ref, *refs, counts):
    pieces = [refs[4 * v : 4 * v + 4] for v in range(len(counts))]
    outs = refs[4 * len(counts) :]
    me_x, me_y, core = lax.axis_index("fx"), lax.axis_index("fy"), lax.axis_index("bc")
    me_a, me_b = gray(me_x)
    frames = sum(counts)
    for slot in range(outs[0].shape[0]):
        for side in range(2):
            frame = table_ref[slot, side]
            which, group = frame % frames, frame // frames
            to_a, to_b = gray(group // 2)
            fa, fb, fy = to_a ^ me_a, to_b ^ me_b, (group % 2) ^ me_y
            other = core == 1
            first = (jnp.where(other, fb, fy), jnp.where(other, fy, fa), jnp.where(other, fa, fb))
            low_frame = 0
            for v, bits in enumerate((first, (fa, fb, fy))):
                count = counts[v]
                place = bits[0] + 2 * bits[1] + 4 * bits[2]
                mine = (which >= low_frame) & (which < low_frame + count)
                for m, (low, span) in enumerate(((0, 1), (1, 1), (2, 2), (4, 4))):

                    @pl.when(mine & (place >= low) & (place < low + span))
                    def _():
                        outs[side][slot] = pieces[v][m][(place - low) * count + which - low_frame]

                low_frame += count


def pick(table, held, counts):
    block = held[0][0].shape[1:]
    pieces = [piece for have in held for piece in have]
    shape = jax.ShapeDtypeStruct((table.shape[0],) + block, pieces[0].dtype)
    return pl.pallas_call(
        functools.partial(pick_kernel, counts=counts),
        out_shape=[shape, shape],
        in_specs=[SMEM] + [VMEM] * len(pieces),
        out_specs=[VMEM, VMEM],
        compiler_params=pltpu.CompilerParams(vmem_limit_bytes=12 << 20),
    )(table, *pieces)


def targets(refs, p, scale, rhs, start, cells):
    for j, ref in enumerate(refs):
        b = ref[p].astype(jnp.float32) * scale
        hi = b.astype(jnp.bfloat16)
        lo = (b - hi.astype(jnp.float32)).astype(jnp.bfloat16)
        rhs[(start + j) * cells : (start + j + 1) * cells, :] = jnp.concatenate([hi, lo], axis=1)


def places(cells, width):
    h, z, core = lax.axis_index("bh"), lax.axis_index("bz"), lax.axis_index("bc")
    src_place = [(h, core), (1 - h, core), (h, 1 - core), (1 - h, 1 - core)]
    src_band = [(hh * SIZES[3] + z) * SIZES[4] + cc for hh, cc in src_place]
    step = 1 - 2 * core
    tgt_z = [z, (z - step) % SIZES[3], (z + step) % SIZES[3], (z + 2) % SIZES[3]]
    tgt_band = [(h * SIZES[3] + zz) * SIZES[4] + core for zz in tgt_z]
    tgt_slot = [jnp.where(zz == z, 0, jnp.where(zz == 3 - z, 1, jnp.where(zz == (z ^ 1), 2, 3))) for zz in tgt_z]
    row = lambda band: (band * (cells // width)).astype(jnp.float32) - 27.5
    return [row(band) for band in src_band], [row(band) for band in tgt_band], tgt_slot


def chosen(values, index):
    return functools.reduce(lambda x, j: jnp.where(index == j, values[j], x), range(1, len(values)), values[0])


def block(sources, b, yj, src_rows, sums, cols, cells, width, shifts=None):
    band_rows = cells // width
    groups = width // 8
    a = jnp.concatenate(sources, axis=0)
    s = lax.dot_general(jnp.concatenate([a, a], axis=1), b, NT, preferred_element_type=jnp.float32)
    put, cols_first = cols
    for i in range(len(sources)):
        tt = [None] * band_rows
        uu = [None] * band_rows
        xx = [None] * band_rows
        for q in range(band_rows):
            ps = [None] * band_rows
            qs = [None] * band_rows
            for k in range(groups):
                r0 = i * cells + q * width + k * 8
                t = [s[r0 : r0 + 8, c * width : (c + 1) * width] for c in range(band_rows)]
                rows = slice(r0, r0 + 8)
                if shifts is None:
                    w = [jnp.exp2(x) for x in t]
                    v = w
                else:
                    m = shifts[0][rows, :]
                    w = [jnp.exp2(x - m) for x in t]
                    v = [jnp.exp2(x - shifts[1](c)) for c, x in enumerate(t)]
                a1 = w[0]
                b1 = w[0]
                for c in range(1, band_rows):
                    a1 = a1 + w[c]
                    b1 = b1 + a1
                sums(rows, a1, yj * a1 - b1)
                for c in range(band_rows):
                    ps[c] = v[c] if k == 0 else ps[c] + v[c]
                    qs[c] = ps[c] if k == 0 else qs[c] + ps[c]
            for c in range(band_rows):
                tt[c] = ps[c] if q == 0 else tt[c] + ps[c]
                uu[c] = tt[c] if q == 0 else uu[c] + tt[c]
                xx[c] = qs[c] if q == 0 else xx[c] + qs[c]
        for c in range(band_rows):
            put(slice(c * width, (c + 1) * width), i == 0 and cols_first, (tt[c], xx[c], src_rows[i] * tt[c] - uu[c]))


def early_kernel(*refs, nsrc, ntgt, cells, width):
    src, tgt = refs[:nsrc], refs[nsrc : nsrc + ntgt]
    acc, accy, g0, gq, gy, rhs = refs[nsrc + ntgt :]
    src_rows, tgt_rows, _ = places(cells, width)
    scale = score_gain / math.sqrt(src[0].shape[-1]) * math.log2(math.e)

    def one(p, jb, first):
        def sums(rows, total, rowed):
            acc[p, rows, :] = total if first else acc[p, rows, :] + total
            accy[p, rows, :] = rowed if first else accy[p, rows, :] + rowed

        def put(lanes, new, values):
            for ref, value in zip((g0, gq, gy), values):
                ref[p, jb, :, lanes] = value if new else ref[p, jb, :, lanes] + value

        b = rhs[jb * cells : (jb + 1) * cells, :]
        block([ref[p] for ref in src], b, tgt_rows[jb], src_rows, sums, (put, True), cells, width)

    def pair(p, carry):
        targets(tgt, p, scale, rhs, 0, cells)
        one(p, 0, True)

        for jb in range(1, ntgt):
            one(p, jb, False)
        return carry

    lax.fori_loop(0, src[0].shape[0], pair, 0)


def late_kernel(*refs, nsrc, ntgt, cells, width):
    src, tgt = refs[:nsrc], refs[nsrc : nsrc + ntgt]
    acc_in, accy_in, g0_in, gq_in, gy_in, fwd_keep, fwd_send, rev_keep, rev_send, rev, rhs, acc, accy, g0, gq, gy, shift_r, shift_c = refs[
        nsrc + ntgt :
    ]
    fwd = [(fwd_keep, 0), (fwd_keep, 1), (fwd_send, 0), (fwd_send, 1)]
    band_rows = cells // width
    src_rows, tgt_rows, tgt_slot = places(cells, width)
    scale = score_gain / math.sqrt(src[0].shape[-1]) * math.log2(math.e)
    early = g0_in.shape[1]
    lane = lax.broadcasted_iota(jnp.int32, (16, width), 1)
    row16 = lax.broadcasted_iota(jnp.int32, (16, width), 0)
    ramp = (2 * lane - (width - 1)).astype(jnp.float32)
    pick_rows = jnp.where(row16 == 0, 1.0, jnp.where(row16 == 1, ramp, 0.0)).astype(jnp.bfloat16)
    pick_rows = jnp.concatenate([pick_rows, pick_rows], axis=1)
    sub = lax.broadcasted_iota(jnp.int32, (8, width), 0).astype(jnp.float32)

    def safe(x):
        return jnp.all((x > 2.0**-90) & (x < 2.0**110))

    def lanes(ref, sl):
        x = ref[sl, :]
        hi = x.astype(jnp.bfloat16)
        lo = (x - hi.astype(jnp.float32)).astype(jnp.bfloat16)
        return lax.dot_general(pick_rows, jnp.concatenate([hi, lo], axis=1), NT, preferred_element_type=jnp.float32)

    def emit(p, cols_of, tops):
        ok = None
        for i in range(nsrc):
            sl = slice(i * cells, (i + 1) * cells)
            one = lanes(acc, sl)
            two = lanes(accy, sl)
            good = safe(one[0:1])
            ok = good if ok is None else ok & good
            ref, at = fwd[i]
            for r in range(band_rows):
                cs = slice(r * width, (r + 1) * width)
                ref[at, p, band_rows + r : band_rows + r + 1, :] = one[0:1, cs]
                ref[at, p, 2 * band_rows + r : 2 * band_rows + r + 1, :] = one[1:2, cs] * (1.0 / width)
                ref[at, p, 3 * band_rows + r : 3 * band_rows + r + 1, :] = two[0:1, cs] * (1.0 / 32)
                top = jnp.zeros((1, width), jnp.float32)
                if tops:
                    m = shift_r[i * cells + r * width : i * cells + (r + 1) * width, :]
                    top = jnp.transpose(m)[0:1, :]
                ref[at, p, r : r + 1, :] = top
        for j in range(ntgt):
            for r in range(band_rows):
                cs = slice(r * width, (r + 1) * width)
                t, xq, ty = cols_of(j, cs)
                tot = jnp.sum(t, axis=0, keepdims=True)
                ok = ok & safe(tot)
                slot = tgt_slot[j]
                x = (129.0 + 2.0 * sub) * t - 16.0 * xq
                rev[slot, p, band_rows + r : band_rows + r + 1, :] = tot
                rev[slot, p, 2 * band_rows + r : 2 * band_rows + r + 1, :] = jnp.sum(x, axis=0, keepdims=True) * (1.0 / width)
                rev[slot, p, 3 * band_rows + r : 3 * band_rows + r + 1, :] = jnp.sum(ty, axis=0, keepdims=True) * (1.0 / 32)
                rev[slot, p, r : r + 1, :] = shift_c[j, 0:1, cs] if tops else jnp.zeros((1, width), jnp.float32)
        return ok

    def put(jb):
        def inner(lane_slice, new, values):
            for ref, value in zip((g0, gq, gy), values):
                ref[jb, :, lane_slice] = value if new else ref[jb, :, lane_slice] + value

        return inner

    def pair(p, carry):
        targets(tgt[early:], p, scale, rhs, early, cells)
        sources = [ref[p] for ref in src]
        for jb in range(early, ntgt):

            def sums(rows, total, rowed):
                acc[rows, :] = (acc_in[p, rows, :] if jb == early else acc[rows, :]) + total
                accy[rows, :] = (accy_in[p, rows, :] if jb == early else accy[rows, :]) + rowed

            b = rhs[jb * cells : (jb + 1) * cells, :]
            block(sources, b, tgt_rows[jb], src_rows, sums, (put(jb), True), cells, width)

        def cols_of(j, cs):
            if j >= early:
                return g0[j, :, cs], gq[j, :, cs], gy[j, :, cs]
            return g0_in[p, j, :, cs], gq_in[p, j, :, cs], gy_in[p, j, :, cs]

        ok = emit(p, cols_of, False)

        @pl.when(jnp.logical_not(ok))
        def _():
            targets(tgt[:early], p, scale, rhs, 0, cells)
            shift_r[...] = jnp.full_like(shift_r, -1e30)
            shift_c[...] = jnp.full_like(shift_c, -1e30)

            def tops(jb, c):
                b = rhs[pl.ds(pl.multiple_of(jb * cells, cells), cells), :]
                for i in range(nsrc):

                    def part(q, c2):
                        a = src[i][p, pl.ds(pl.multiple_of(q * width, width), width), :]
                        s = lax.dot_general(jnp.concatenate([a, a], axis=1), b, NT, preferred_element_type=jnp.float32)
                        sl = pl.ds(pl.multiple_of(i * cells + q * width, width), width)
                        m = shift_r[sl, :]
                        for c3 in range(band_rows):
                            m = jnp.maximum(m, s[:, c3 * width : (c3 + 1) * width])
                        shift_r[sl, :] = m
                        t = shift_c[jb]
                        shift_c[jb] = jnp.maximum(t, jnp.broadcast_to(jnp.max(s, axis=0, keepdims=True), t.shape))
                        return c2

                    lax.fori_loop(0, band_rows, part, 0)
                return c

            lax.fori_loop(0, ntgt, tops, 0)

            def level(n, c):
                sl = pl.ds(pl.multiple_of(n * width, width), width)
                m = shift_r[sl, :]
                shift_r[sl, :] = jnp.broadcast_to(jnp.max(m, axis=1, keepdims=True), m.shape)
                return c

            lax.fori_loop(0, nsrc * band_rows, level, 0)
            acc[...] = jnp.zeros_like(acc)
            accy[...] = jnp.zeros_like(accy)

            def again(jb, c):
                def more(rows, total, rowed):
                    acc[rows, :] = acc[rows, :] + total
                    accy[rows, :] = accy[rows, :] + rowed

                shifts = (shift_r, lambda c4: shift_c[jb, :, c4 * width : (c4 + 1) * width])
                b = rhs[pl.ds(pl.multiple_of(jb * cells, cells), cells), :]
                block(sources, b, chosen(tgt_rows, jb), src_rows, more, (put(jb), True), cells, width, shifts)
                return c

            lax.fori_loop(0, ntgt, again, 0)
            emit(p, lambda j, cs: (g0[j, :, cs], gq[j, :, cs], gy[j, :, cs]), True)

        return carry

    lax.fori_loop(0, src[0].shape[0], pair, 0)
    rev_keep[...] = rev[0:2]
    rev_send[...] = rev[2:4]


def cost(pairs, blocks):
    return pl.CostEstimate(
        flops=134_000_000 * pairs * blocks, bytes_accessed=100_000 * pairs * blocks, transcendentals=262_144 * pairs * blocks
    )


def match_early(src, tgt):
    pairs, cells, chans = src[0].shape
    width = 128
    nsrc, ntgt = len(src), len(tgt)
    rows = jax.ShapeDtypeStruct((pairs, nsrc * cells, width), jnp.float32)
    cols = jax.ShapeDtypeStruct((pairs, ntgt, 8, cells), jnp.float32)
    return pl.pallas_call(
        functools.partial(early_kernel, nsrc=nsrc, ntgt=ntgt, cells=cells, width=width),
        out_shape=[rows, rows, cols, cols, cols],
        in_specs=[VMEM] * (nsrc + ntgt),
        out_specs=[VMEM] * 5,
        scratch_shapes=[pltpu.VMEM((ntgt * cells, 2 * chans), jnp.bfloat16)],
        compiler_params=pltpu.CompilerParams(vmem_limit_bytes=16 << 20),
        cost_estimate=cost(pairs, nsrc * ntgt),
    )(*src, *tgt)


def match_late(src, tgt, early):
    pairs, cells, chans = src[0].shape
    width = 128
    nsrc, ntgt = len(src), len(tgt)
    stats = jax.ShapeDtypeStruct((2, pairs, 4 * cells // width, width), jnp.float32)
    return pl.pallas_call(
        functools.partial(late_kernel, nsrc=nsrc, ntgt=ntgt, cells=cells, width=width),
        out_shape=[stats] * 4,
        in_specs=[VMEM] * (nsrc + ntgt + 5),
        out_specs=[VMEM] * 4,
        scratch_shapes=[
            pltpu.VMEM((4,) + stats.shape[1:], jnp.float32),
            pltpu.VMEM((ntgt * cells, 2 * chans), jnp.bfloat16),
            pltpu.VMEM((nsrc * cells, width), jnp.float32),
            pltpu.VMEM((nsrc * cells, width), jnp.float32),
            pltpu.VMEM((ntgt, 8, cells), jnp.float32),
            pltpu.VMEM((ntgt, 8, cells), jnp.float32),
            pltpu.VMEM((ntgt, 8, cells), jnp.float32),
            pltpu.VMEM((nsrc * cells, width), jnp.float32),
            pltpu.VMEM((ntgt, 8, cells), jnp.float32),
        ],
        compiler_params=pltpu.CompilerParams(vmem_limit_bytes=24 << 20),
        cost_estimate=cost(pairs, 2 * nsrc),
    )(*src, *tgt, *early)


def joined(left, right, band_rows):
    part = lambda x, k: x[k * band_rows : (k + 1) * band_rows]
    top = jnp.maximum(part(left, 0), part(right, 0))
    scale_l = jnp.exp2(part(left, 0) - top)
    scale_r = jnp.exp2(part(right, 0) - top)
    return [top] + [part(left, k) * scale_l + part(right, k) * scale_r for k in range(1, 4)]


def half_kernel(fwd, fwd_in, rev, rev_in, *outs, band_rows):
    for way, (own, other) in enumerate(((fwd, fwd_in), (rev, rev_in))):
        for side in range(2):
            for p in range(own.shape[1]):
                for k, value in enumerate(joined(own[side, p], other[side, p], band_rows)):
                    outs[2 * way + side][p, k * band_rows : (k + 1) * band_rows] = value


def half(fwd, fwd_in, rev, rev_in, band_rows):
    shape = jax.ShapeDtypeStruct(fwd.shape[1:], jnp.float32)
    return pl.pallas_call(
        functools.partial(half_kernel, band_rows=band_rows),
        out_shape=[shape] * 4,
        in_specs=[VMEM] * 4,
        out_specs=[VMEM] * 4,
        compiler_params=pltpu.CompilerParams(vmem_limit_bytes=4 << 20),
    )(fwd, fwd_in, rev, rev_in)


def merge_kernel(fwd, fwd_in, rev, rev_in, out, *, band_rows, width):
    band = (lax.axis_index("bh") * SIZES[3] + lax.axis_index("bz")) * SIZES[4] + lax.axis_index("bc")
    col = (2 * lax.broadcasted_iota(jnp.int32, (band_rows, width), 1) - (width - 1)).astype(jnp.float32) * (1.0 / width)
    row = lax.broadcasted_iota(jnp.int32, (band_rows, width), 0) + band * band_rows
    row = (2 * row - 63).astype(jnp.float32) * (1.0 / 64)
    for p in range(out.shape[0]):
        for way, (own, other) in enumerate(((fwd, fwd_in), (rev, rev_in))):
            _, total, cols, rows = joined(own[p], other[p], band_rows)
            out[p, way, 0] = cols / total - col
            out[p, way, 1] = rows / total - row


def merge(fwd, fwd_in, rev, rev_in, band_rows, width):
    return pl.pallas_call(
        functools.partial(merge_kernel, band_rows=band_rows, width=width),
        out_shape=jax.ShapeDtypeStruct((fwd.shape[0], 2, 2, band_rows, width), jnp.float32),
        in_specs=[VMEM] * 4,
        out_specs=VMEM,
        compiler_params=pltpu.CompilerParams(vmem_limit_bytes=4 << 20),
    )(fwd, fwd_in, rev, rev_in)


def refine_kernel(weight, bias, chip, own, core, out, *cur, layers):
    pairs, ways, comps, band_rows, width = own.shape
    high = 16
    total = pairs * ways * high
    band = (lax.axis_index("bh") * SIZES[3] + lax.axis_index("bz")) * SIZES[4] + lax.axis_index("bc")
    last = SIZES[2] * SIZES[3] * SIZES[4] - 1
    odd = lax.axis_index("bc") == 1
    for i in range(comps):
        for p in range(pairs):
            for d in range(ways):
                base = (p * ways + d) * high
                near, far = core[p, d, i], chip[p, d, i]
                cur[i][base : base + band_rows] = jnp.where(odd, near, far)
                cur[i][base + band_rows : base + 2 * band_rows] = own[p, d, i]
                cur[i][base + 2 * band_rows : base + 3 * band_rows] = jnp.where(odd, far, near)
                cur[i][base + 3 * band_rows : base + high] = jnp.zeros((high - 3 * band_rows, width), jnp.float32)
    row = lax.broadcasted_iota(jnp.int32, (total, width), 0) & (high - 1)
    lane = lax.broadcasted_iota(jnp.int32, (total, width), 1)
    low = jnp.where(band == 0, band_rows, 0)
    top = jnp.where(band == last, 2 * band_rows, 3 * band_rows)
    inside = ((row >= low) & (row < top)).astype(jnp.float32)
    keep_left = (lane > 0).astype(jnp.float32)
    keep_right = (lane < width - 1).astype(jnp.float32)
    for layer in range(layers):
        taps = []
        for i in range(comps):
            act = jnp.tanh(2.0 * cur[i][...]) * inside
            taps.append((pltpu.roll(act, 1, 1) * keep_left, act, pltpu.roll(act, width - 1, 1) * keep_right))
        for o in range(comps):
            lines = []
            for r in range(3):
                line = None
                for i in range(comps):
                    for c in range(3):
                        term = taps[i][c] * weight[(((layer * comps + o) * comps + i) * 3 + r) * 3 + c]
                        line = term if line is None else line + term
                lines.append(line)
            grown = pltpu.roll(lines[0], 1, 0) + lines[1] + pltpu.roll(lines[2], total - 1, 0)
            cur[o][...] = cur[o][...] + (grown + bias[layer * comps + o])
    for i in range(comps):
        for p in range(pairs):
            for d in range(ways):
                base = (p * ways + d) * high + band_rows
                out[p, d, i] = cur[i][base : base + band_rows]


def refine(weight, bias, chip, own, core):
    pairs, ways, comps, _, width = own.shape
    return pl.pallas_call(
        functools.partial(refine_kernel, layers=weight.shape[0]),
        out_shape=jax.ShapeDtypeStruct(own.shape, jnp.float32),
        in_specs=[SMEM, SMEM, VMEM, VMEM, VMEM],
        out_specs=VMEM,
        scratch_shapes=[pltpu.VMEM((pairs * ways * 16, width), jnp.float32)] * comps,
        compiler_params=pltpu.CompilerParams(vmem_limit_bytes=4 << 20),
    )(weight.reshape(-1), bias.reshape(-1), chip, own, core)


def gather_frames(blocks):
    orders = (
        (by_core(flip_y, flip_b), by_core(flip_a, flip_y), by_core(flip_b, flip_a)),
        (flip_a, flip_b, flip_y),
    )
    held = [[block] for block in blocks]
    for stage in range(3):
        send = [have[0] if len(have) == 1 else jnp.concatenate(have, axis=0) for have in held]
        got = [hop(part, order[stage]) for part, order in zip(send, orders)]
        got = lax.optimization_barrier(got)
        for have, piece in zip(held, got):
            have.append(piece)
    return held


def matched(src0, tgt0):
    src1 = hop(src0, flip_h)
    tgt1 = hop(tgt0, ring)
    src2 = hop(src0, flip_c)
    tgt2 = hop(tgt0, back)
    tgt1, src1, src2 = lax.optimization_barrier((tgt1, src1, src2))
    tgt3 = hop(tgt1, ring)
    src3 = hop(src1, flip_c)
    src = (src0, src1, src2, src3)
    early = match_early(src, (tgt0, tgt1))
    return match_late(src, (tgt0, tgt1, tgt2, tgt3), early)


def shards(features, frame_pairs, conv_weight, conv_bias):
    frames, band_rows, width, chans = features.shape
    cells = band_rows * width
    flat_features = features.reshape(frames, cells, chans)
    counts = (frames - 1, 1)
    held = gather_frames([flat_features[:-1], flat_features[-1:]])
    src0, tgt0 = pick(frame_pairs, held, counts)
    fwd_keep, fwd_send, rev_keep, rev_send = matched(src0, tgt0)
    fwd0, fwd1, rev0, rev1 = half(fwd_keep, hop(fwd_send, flip_c), rev_keep, hop(rev_send, flip_za), band_rows)
    flows = merge(fwd0, hop(fwd1, flip_h), rev0, hop(rev1, flip_zb), band_rows, width)
    chip = hop(flows, next_chip)
    core = hop(flows, flip_c)
    return refine(conv_weight, conv_bias, chip, flows, core)


def solution(mesh):
    finer = Mesh(mesh.devices.reshape(SIZES), AXES)
    frame, band = AXES[:2], AXES[2:]
    placed = (P(frame, band, None, None), P(frame, None), P(), P())
    return jax.shard_map(
        shards,
        mesh=finer,
        in_specs=placed,
        out_specs=P(frame, None, None, band, None),
        check_vma=False,
    )
```

profile of v0, /device:TPU:0, one launch (start us, length us, event | category | flops | bytes accessed | tf_op | source)
XLA Modules:
  0.0 162.6 jit_solution(16052872551326147503)
XLA Ops:
  0.0 1.0 slice.12
  1.0 1.8 %collective-permute-start = (bf16[2,512,128]{2,1,0:T(8,128)(2,1)S(1)}, bf16[2,512,128]{2,1,0:T(8,128)(2,1)S(1)}, u32[]{:S(2)}, u32[]{:S(2)}) collective-permute-start(bf16[2,512,128]{2,1,0:T(8,128)(2,1)S(1)} %bitcast.2), channel_id=1, source_target_pairs={{0,16},{1,97},{2,18},{3,99},{4,20},{5,101},{6,22},{7,103},{8,24},{... | collective-permute-start | bytes 786440 | tf_op jit(solution)/shard_map/ppermute | solution.py:34
  2.8 0.9 slice.14
  3.7 1.6 collective-permute-start.1
  5.2 4.6 %collective-permute-done.1.refs_5_ = bf16[1,512,128]{2,1,0:T(8,128)(2,1)S(1)} collective-permute-done((bf16[1,512,128]{2,1,0:T(8,128)(2,1)S(1)}, bf16[1,512,128]{2,1,0:T(8,128)(2,1)S(1)}, u32[]{:S(2)}, u32[]{:S(2)}) %collective-permute-start.1) | collective-permute-done | bytes 131104 | tf_op jit(solution)/shard_map/ppermute | solution.py:34
  9.9 0.4 collective-permute-start.2
  10.4 2.2 %collective-permute-start.3 = (bf16[2,512,128]{2,1,0:T(8,128)(2,1)S(1)}, bf16[2,512,128]{2,1,0:T(8,128)(2,1)S(1)}, u32[]{:S(2)}, u32[]{:S(2)}) collective-permute-start(bf16[2,512,128]{2,1,0:T(8,128)(2,1)S(1)} %pad_maximum_fusion.3), channel_id=1, source_target_pairs={{0,96},{1,97},{2,98},{3,99},{4,100},{5,101},{6,102},{7,103},{8,104... | collective-permute-start | bytes 786440 | tf_op jit(solution)/shard_map/ppermute | solution.py:34
  12.6 7.1 %collective-permute-done.3.refs_6_ = bf16[2,512,128]{2,1,0:T(8,128)(2,1)S(1)} collective-permute-done((bf16[2,512,128]{2,1,0:T(8,128)(2,1)S(1)}, bf16[2,512,128]{2,1,0:T(8,128)(2,1)S(1)}, u32[]{:S(2)}, u32[]{:S(2)}) %collective-permute-start.3) | collective-permute-done | bytes 262176 | tf_op jit(solution)/shard_map/ppermute | solution.py:34
  19.7 1.1 pad_maximum_fusion
  20.8 1.5 collective-permute-start.4
  22.3 0.8 pad_maximum_fusion.2
  23.1 0.4 collective-permute-start.5
  23.6 10.9 %collective-permute-done.5.refs_7_ = bf16[4,512,128]{2,1,0:T(8,128)(2,1)S(1)} collective-permute-done((bf16[4,512,128]{2,1,0:T(8,128)(2,1)}, bf16[4,512,128]{2,1,0:T(8,128)(2,1)S(1)}, u32[]{:S(2)}, u32[]{:S(2)}) %collective-permute-start.5) | collective-permute-done | bytes 524320 | tf_op jit(solution)/shard_map/ppermute | solution.py:34
  34.6 2.4 %collective-permute-done.4.refs_3_ = bf16[8,512,128]{2,1,0:T(8,128)(2,1)S(1)} collective-permute-done((bf16[8,512,128]{2,1,0:T(8,128)(2,1)}, bf16[8,512,128]{2,1,0:T(8,128)(2,1)S(1)}, u32[]{:S(2)}, u32[]{:S(2)}) %collective-permute-start.4) | collective-permute-done | bytes 1048608 | tf_op jit(solution)/shard_map/ppermute | solution.py:34
  37.0 1.1 shard_map.46
  38.1 2.1 %collective-permute-start.6 = (bf16[3,512,128]{2,1,0:T(8,128)(2,1)S(1)}, bf16[3,512,128]{2,1,0:T(8,128)(2,1)S(1)}, u32[]{:S(2)}, u32[]{:S(2)}) collective-permute-start(bf16[3,512,128]{2,1,0:T(8,128)(2,1)S(1)} %get-tuple-element.36.refs_4_), channel_id=1, source_target_pairs={{0,2},{1,7},{2,4},{3,1},{4,6},{5,3},{6,0},{7,5},{8,10},{9,15},{10,... | collective-permute-start | bytes 1179656 | tf_op jit(solution)/shard_map/ppermute | solution.py:34
  40.2 3.2 %collective-permute-start.7 = (bf16[3,512,128]{2,1,0:T(8,128)(2,1)S(1)}, bf16[3,512,128]{2,1,0:T(8,128)(2,1)S(1)}, u32[]{:S(2)}, u32[]{:S(2)}) collective-permute-start(bf16[3,512,128]{2,1,0:T(8,128)(2,1)S(1)} %get-tuple-element.35.refs_0_), channel_id=1, source_target_pairs={{0,8},{1,9},{2,10},{3,11},{4,12},{5,13},{6,14},{7,15},{8,0},{9,1},... | collective-permute-start | bytes 1179656 | tf_op jit(solution)/shard_map/ppermute | solution.py:34
  43.4 4.7 %collective-permute-done.6.refs_5_ = bf16[3,512,128]{2,1,0:T(8,128)(2,1)S(1)} collective-permute-done((bf16[3,512,128]{2,1,0:T(8,128)(2,1)S(1)}, bf16[3,512,128]{2,1,0:T(8,128)(2,1)S(1)}, u32[]{:S(2)}, u32[]{:S(2)}) %collective-permute-start.6) | collective-permute-done | bytes 393248 | tf_op jit(solution)/shard_map/ppermute | solution.py:34
  48.1 3.5 %collective-permute-done.7.refs_1_ = bf16[3,512,128]{2,1,0:T(8,128)(2,1)S(1)} collective-permute-done((bf16[3,512,128]{2,1,0:T(8,128)(2,1)S(1)}, bf16[3,512,128]{2,1,0:T(8,128)(2,1)S(1)}, u32[]{:S(2)}, u32[]{:S(2)}) %collective-permute-start.7) | collective-permute-done | bytes 393248 | tf_op jit(solution)/shard_map/ppermute | solution.py:34
  51.5 0.4 collective-permute-start.10
  52.0 1.6 collective-permute-start.11
  53.6 6.1 %shard_map.47 = (f32[3,2048,128]{2,1,0:T(8,128)S(1)}, f32[3,2048,128]{2,1,0:T(8,128)S(1)}, f32[3,2,8,512]{3,2,1,0:T(8,128)S(1)}, f32[3,2,8,512]{3,2,1,0:T(8,128)S(1)}, f32[3,2,8,512]{3,2,1,0:T(8,128)S(1)}) custom-call(bf16[3,512,128]{2,1,0:T(8,128)(2,1)S(1)} %get-tuple-element.35.refs_0_, bf16[3,512,128]{2,1,0:T(8,128)(2,1)S(1)} %collective-permute-done.7.refs_1_, ...), custom_call_target="tpu_custom_call" | custom-call | flops 3216000000 | bytes 2400000 | tf_op jit(solution)/shard_map/pallas_call | solution.py:378
  59.7 3.4 %collective-permute-done.10.refs_6_ = bf16[3,512,128]{2,1,0:T(8,128)(2,1)S(1)} collective-permute-done((bf16[3,512,128]{2,1,0:T(8,128)(2,1)S(1)}, bf16[3,512,128]{2,1,0:T(8,128)(2,1)S(1)}, u32[]{:S(2)}, u32[]{:S(2)}) %collective-permute-start.10) | collective-permute-done | bytes 393248 | tf_op jit(solution)/shard_map/ppermute | solution.py:34
  63.1 1.2 collective-permute-done.11.refs_7_
  64.3 76.6 %shard_map.48 = (f32[2,3,16,128]{3,2,1,0:T(8,128)S(1)}, f32[2,3,16,128]{3,2,1,0:T(8,128)S(1)}, f32[2,3,16,128]{3,2,1,0:T(8,128)S(1)}, f32[2,3,16,128]{3,2,1,0:T(8,128)S(1)}) custom-call(bf16[3,512,128]{2,1,0:T(8,128)(2,1)S(1)} %get-tuple-element.35.refs_0_, bf16[3,512,128]{2,1,0:T(8,128)(2,1)S(1)} %collective-permute-done.7.refs_1_, ...), custom_call_target="tpu_custom_call" | custom-call | flops 3216000000 | bytes 2400000 | tf_op jit(solution)/shard_map/pallas_call | solution.py:394
  141.1 1.1 collective-permute-done.12.fwd_in
  142.2 3.0 %collective-permute-done.13.rev_in = f32[2,3,16,128]{3,2,1,0:T(8,128)S(1)} collective-permute-done((f32[2,3,16,128]{3,2,1,0:T(8,128)S(1)}, f32[2,3,16,128]{3,2,1,0:T(8,128)S(1)}, u32[]{:S(2)}, u32[]{:S(2)}) %collective-permute-start.13) | collective-permute-done | bytes 49184 | tf_op jit(solution)/shard_map/ppermute | solution.py:34
  145.2 3.3 %collective-permute-start.14 = (f32[3,16,128]{2,1,0:T(8,128)S(1)}, f32[3,16,128]{2,1,0:T(8,128)S(1)}, u32[]{:S(2)}, u32[]{:S(2)}) collective-permute-start(f32[3,16,128]{2,1,0:T(8,128)S(1)} %get-tuple-element.50), channel_id=1, source_target_pairs={{0,8},{1,9},{2,10},{3,11},{4,12},{5,13},{6,14},{7,15},{8,0},{9,1},... | collective-permute-start | bytes 73736 | tf_op jit(solution)/shard_map/ppermute | solution.py:34
  148.5 2.1 %collective-permute-done.14.fwd_in = f32[3,16,128]{2,1,0:T(8,128)S(1)} collective-permute-done((f32[3,16,128]{2,1,0:T(8,128)S(1)}, f32[3,16,128]{2,1,0:T(8,128)S(1)}, u32[]{:S(2)}, u32[]{:S(2)}) %collective-permute-start.14) | collective-permute-done | bytes 24608 | tf_op jit(solution)/shard_map/ppermute | solution.py:34
  150.6 2.9 %collective-permute-done.15.rev_in = f32[3,16,128]{2,1,0:T(8,128)S(1)} collective-permute-done((f32[3,16,128]{2,1,0:T(8,128)S(1)}, f32[3,16,128]{2,1,0:T(8,128)S(1)}, u32[]{:S(2)}, u32[]{:S(2)}) %collective-permute-start.15) | collective-permute-done | bytes 24608 | tf_op jit(solution)/shard_map/ppermute | solution.py:34
  154.3 6.2 %collective-permute-done.16.chip = f32[3,2,2,4,128]{4,3,2,1,0:T(4,128)S(1)} collective-permute-done((f32[3,2,2,4,128]{4,3,2,1,0:T(4,128)S(1)}, f32[3,2,2,4,128]{4,3,2,1,0:T(4,128)S(1)}, u32[]{:S(2)}, u32[]{:S(2)}) %collective-permute-start.16) | collective-permute-done | bytes 24608 | tf_op jit(solution)/shard_map/ppermute | solution.py:34
  160.5 2.0 %shard_map.51 = f32[3,2,2,4,128]{4,3,2,1,0:T(4,128)} custom-call(f32[144]{0:T(256)S(1)} %reshape.9.weight, f32[8]{0:T(128)S(1)} %reshape.10.bias, f32[3,2,2,4,128]{4,3,2,1,0:T(4,128)S(1)} %collective-permute-done.16.chip, f32[3,2,2,4,128]{4,3,2,1,0:T(4,128)S(1)} %shard_map.50.own, f32[3,2,2,4,128]{4,3,2,1,0:T(4,128)S(1)} %collective-permute-done.17.core), custom_call_target="tpu_custom_call" | custom-call | tf_op jit(solution)/shard_map/pallas_call | solution.py:512
  (27 shorter events, 1.1 us)
Async XLA Ops:
  0.0 23.6 %copy-start.1 = (s32[3,2]{0,1:T(2,128)S(1)}, s32[3,2]{0,1:T(2,128)}, u32[]{:S(2)}) copy-start(s32[3,2]{0,1:T(2,128)} %param.5) | copy-start | bytes 76
  1.0 8.9 %collective-permute-start = (bf16[2,512,128]{2,1,0:T(8,128)(2,1)S(1)}, bf16[2,512,128]{2,1,0:T(8,128)(2,1)S(1)}, u32[]{:S(2)}, u32[]{:S(2)}) collective-permute-start(bf16[2,512,128]{2,1,0:T(8,128)(2,1)S(1)} %bitcast.2), channel_id=1, source_target_pairs={{0,16},{1,97},{2,18},{3,99},{4,20},{5,101},{6,22},{7,103},{8,24},{... | collective-permute-start | bytes 786440 | tf_op jit(solution)/shard_map/ppermute | solution.py:34
  3.7 6.2 %collective-permute-start.1 = (bf16[1,512,128]{2,1,0:T(8,128)(2,1)S(1)}, bf16[1,512,128]{2,1,0:T(8,128)(2,1)S(1)}, u32[]{:S(2)}, u32[]{:S(2)}) collective-permute-start(bf16[1,512,128]{2,1,0:T(8,128)(2,1)S(1)} %bitcast.6), channel_id=1, source_target_pairs={{0,32},{1,33},{2,34},{3,35},{4,36},{5,37},{6,38},{7,39},{8,40},{9,... | collective-permute-start | bytes 393224 | tf_op jit(solution)/shard_map/ppermute | solution.py:34
  9.9 9.7 %collective-permute-start.2 = (bf16[4,512,128]{2,1,0:T(8,128)(2,1)S(1)}, bf16[4,512,128]{2,1,0:T(8,128)(2,1)S(1)}, u32[]{:S(2)}, u32[]{:S(2)}) collective-permute-start(bf16[4,512,128]{2,1,0:T(8,128)(2,1)S(1)} %pad_maximum_fusion.1), channel_id=1, source_target_pairs={{0,32},{1,17},{2,34},{3,19},{4,36},{5,21},{6,38},{7,23},{8,40},{9,... | collective-permute-start | bytes 1572872 | tf_op jit(solution)/shard_map/ppermute | solution.py:34
  10.4 9.3 %collective-permute-start.3 = (bf16[2,512,128]{2,1,0:T(8,128)(2,1)S(1)}, bf16[2,512,128]{2,1,0:T(8,128)(2,1)S(1)}, u32[]{:S(2)}, u32[]{:S(2)}) collective-permute-start(bf16[2,512,128]{2,1,0:T(8,128)(2,1)S(1)} %pad_maximum_fusion.3), channel_id=1, source_target_pairs={{0,96},{1,97},{2,98},{3,99},{4,100},{5,101},{6,102},{7,103},{8,104... | collective-permute-start | bytes 786440 | tf_op jit(solution)/shard_map/ppermute | solution.py:34
  20.8 16.2 %collective-permute-start.4 = (bf16[8,512,128]{2,1,0:T(8,128)(2,1)}, bf16[8,512,128]{2,1,0:T(8,128)(2,1)S(1)}, u32[]{:S(2)}, u32[]{:S(2)}) collective-permute-start(bf16[8,512,128]{2,1,0:T(8,128)(2,1)} %pad_maximum_fusion), channel_id=1, source_target_pairs={{0,96},{1,33},{2,98},{3,35},{4,100},{5,37},{6,102},{7,39},{8,104},... | collective-permute-start | bytes 3145736 | tf_op jit(solution)/shard_map/ppermute | solution.py:34
  23.1 11.5 %collective-permute-start.5 = (bf16[4,512,128]{2,1,0:T(8,128)(2,1)}, bf16[4,512,128]{2,1,0:T(8,128)(2,1)S(1)}, u32[]{:S(2)}, u32[]{:S(2)}) collective-permute-start(bf16[4,512,128]{2,1,0:T(8,128)(2,1)} %pad_maximum_fusion.2), channel_id=1, source_target_pairs={{0,16},{1,17},{2,18},{3,19},{4,20},{5,21},{6,22},{7,23},{8,24},{9,... | collective-permute-start | bytes 1572872 | tf_op jit(solution)/shard_map/ppermute | solution.py:34
  38.1 10.0 %collective-permute-start.6 = (bf16[3,512,128]{2,1,0:T(8,128)(2,1)S(1)}, bf16[3,512,128]{2,1,0:T(8,128)(2,1)S(1)}, u32[]{:S(2)}, u32[]{:S(2)}) collective-permute-start(bf16[3,512,128]{2,1,0:T(8,128)(2,1)S(1)} %get-tuple-element.36.refs_4_), channel_id=1, source_target_pairs={{0,2},{1,7},{2,4},{3,1},{4,6},{5,3},{6,0},{7,5},{8,10},{9,15},{10,... | collective-permute-start | bytes 1179656 | tf_op jit(solution)/shard_map/ppermute | solution.py:34
  40.2 11.3 %collective-permute-start.7 = (bf16[3,512,128]{2,1,0:T(8,128)(2,1)S(1)}, bf16[3,512,128]{2,1,0:T(8,128)(2,1)S(1)}, u32[]{:S(2)}, u32[]{:S(2)}) collective-permute-start(bf16[3,512,128]{2,1,0:T(8,128)(2,1)S(1)} %get-tuple-element.35.refs_0_), channel_id=1, source_target_pairs={{0,8},{1,9},{2,10},{3,11},{4,12},{5,13},{6,14},{7,15},{8,0},{9,1},... | collective-permute-start | bytes 1179656 | tf_op jit(solution)/shard_map/ppermute | solution.py:34
  43.4 8.2 %collective-permute-start.8 = (bf16[3,512,128]{2,1,0:T(8,128)(2,1)S(1)}, bf16[3,512,128]{2,1,0:T(8,128)(2,1)S(1)}, u32[]{:S(2)}, u32[]{:S(2)}) collective-permute-start(bf16[3,512,128]{2,1,0:T(8,128)(2,1)S(1)} %get-tuple-element.35.refs_0_), channel_id=1, source_target_pairs={{0,1},{1,0},{2,3},{3,2},{4,5},{5,4},{6,7},{7,6},{8,9},{9,8},{10,11... | collective-permute-start | bytes 1179656 | tf_op jit(solution)/shard_map/ppermute | solution.py:34
  51.5 2.0 %collective-permute-start.9 = (bf16[3,512,128]{2,1,0:T(8,128)(2,1)S(1)}, bf16[3,512,128]{2,1,0:T(8,128)(2,1)S(1)}, u32[]{:S(2)}, u32[]{:S(2)}) collective-permute-start(bf16[3,512,128]{2,1,0:T(8,128)(2,1)S(1)} %collective-permute-done.7.refs_1_), channel_id=1, source_target_pairs={{0,1},{1,0},{2,3},{3,2},{4,5},{5,4},{6,7},{7,6},{8,9},{9,8},{10,11... | collective-permute-start | bytes 1179656 | tf_op jit(solution)/shard_map/ppermute | solution.py:34
  51.5 11.5 %collective-permute-start.10 = (bf16[3,512,128]{2,1,0:T(8,128)(2,1)S(1)}, bf16[3,512,128]{2,1,0:T(8,128)(2,1)S(1)}, u32[]{:S(2)}, u32[]{:S(2)}) collective-permute-start(bf16[3,512,128]{2,1,0:T(8,128)(2,1)S(1)} %get-tuple-element.36.refs_4_), channel_id=1, source_target_pairs={{0,6},{1,3},{2,0},{3,5},{4,2},{5,7},{6,4},{7,1},{8,14},{9,11},{10,... | collective-permute-start | bytes 1179656 | tf_op jit(solution)/shard_map/ppermute | solution.py:34
  52.0 12.3 %collective-permute-start.11 = (bf16[3,512,128]{2,1,0:T(8,128)(2,1)S(1)}, bf16[3,512,128]{2,1,0:T(8,128)(2,1)S(1)}, u32[]{:S(2)}, u32[]{:S(2)}) collective-permute-start(bf16[3,512,128]{2,1,0:T(8,128)(2,1)S(1)} %collective-permute-done.6.refs_5_), channel_id=1, source_target_pairs={{0,2},{1,7},{2,4},{3,1},{4,6},{5,3},{6,0},{7,5},{8,10},{9,15},{10,... | collective-permute-start | bytes 1179656 | tf_op jit(solution)/shard_map/ppermute | solution.py:34
  64.3 89.5 %copy-start = (f32[4,2,2,3,3]{0,2,4,3,1:T(2,128)S(1)}, f32[4,2,2,3,3]{0,2,4,3,1:T(2,128)}, u32[]{:S(2)}) copy-start(f32[4,2,2,3,3]{0,2,4,3,1:T(2,128)} %param.6) | copy-start | bytes 1732
  64.3 89.8 %copy-start.2 = (f32[4,2]{0,1:T(2,128)S(1)}, f32[4,2]{0,1:T(2,128)}, u32[]{:S(2)}) copy-start(f32[4,2]{0,1:T(2,128)} %param.7) | copy-start | bytes 100
  140.9 1.3 collective-permute-start.12
  141.0 4.2 %collective-permute-start.13 = (f32[2,3,16,128]{3,2,1,0:T(8,128)S(1)}, f32[2,3,16,128]{3,2,1,0:T(8,128)S(1)}, u32[]{:S(2)}, u32[]{:S(2)}) collective-permute-start(f32[2,3,16,128]{3,2,1,0:T(8,128)S(1)} %get-tuple-element.48), channel_id=1, source_target_pairs={{0,2},{1,3},{2,0},{3,1},{4,6},{5,7},{6,4},{7,5},{8,10},{9,11},{10,... | collective-permute-start | bytes 147464 | tf_op jit(solution)/shard_map/ppermute | solution.py:34
  145.2 5.4 %collective-permute-start.14 = (f32[3,16,128]{2,1,0:T(8,128)S(1)}, f32[3,16,128]{2,1,0:T(8,128)S(1)}, u32[]{:S(2)}, u32[]{:S(2)}) collective-permute-start(f32[3,16,128]{2,1,0:T(8,128)S(1)} %get-tuple-element.50), channel_id=1, source_target_pairs={{0,8},{1,9},{2,10},{3,11},{4,12},{5,13},{6,14},{7,15},{8,0},{9,1},... | collective-permute-start | bytes 73736 | tf_op jit(solution)/shard_map/ppermute | solution.py:34
  148.5 5.0 %collective-permute-start.15 = (f32[3,16,128]{2,1,0:T(8,128)S(1)}, f32[3,16,128]{2,1,0:T(8,128)S(1)}, u32[]{:S(2)}, u32[]{:S(2)}) collective-permute-start(f32[3,16,128]{2,1,0:T(8,128)S(1)} %get-tuple-element.52), channel_id=1, source_target_pairs={{0,6},{1,7},{2,4},{3,5},{4,2},{5,3},{6,0},{7,1},{8,14},{9,15},{10,... | collective-permute-start | bytes 73736 | tf_op jit(solution)/shard_map/ppermute | solution.py:34
  153.6 6.9 %collective-permute-start.16 = (f32[3,2,2,4,128]{4,3,2,1,0:T(4,128)S(1)}, f32[3,2,2,4,128]{4,3,2,1,0:T(4,128)S(1)}, u32[]{:S(2)}, u32[]{:S(2)}) collective-permute-start(f32[3,2,2,4,128]{4,3,2,1,0:T(4,128)S(1)} %shard_map.50.own), channel_id=1, source_target_pairs={{0,15},{1,2},{2,1},{3,4},{4,3},{5,6},{6,5},{7,8},{8,7},{9,10},{10,... | collective-permute-start | bytes 73736 | tf_op jit(solution)/shard_map/ppermute | solution.py:34
  153.7 6.9 %collective-permute-start.17 = (f32[3,2,2,4,128]{4,3,2,1,0:T(4,128)S(1)}, f32[3,2,2,4,128]{4,3,2,1,0:T(4,128)S(1)}, u32[]{:S(2)}, u32[]{:S(2)}) collective-permute-start(f32[3,2,2,4,128]{4,3,2,1,0:T(4,128)S(1)} %shard_map.50.own), channel_id=1, source_target_pairs={{0,1},{1,0},{2,3},{3,2},{4,5},{5,4},{6,7},{7,6},{8,9},{9,8},{10,11... | collective-permute-start | bytes 73736 | tf_op jit(solution)/shard_map/ppermute | solution.py:34
where the time goes:
time: 163 us
  Pallas kernels  85.9 us (53%)
  waiting for transfers between devices  53.2 us (33%)
  starting transfers between devices  18.8 us (12%)
  local copies, waits for them, and re-layouts  2.5 us (2%)
  other arithmetic  2.01 us (1%)
    pallas_call x1, Pallas kernels, match_late(): pl.pallas_call(functools.partial(late_kernel, nsrc=nsrc, ntgt=ntgt, cells...  76.6 us
    ppermute x18, waiting for transfers between devices, hop(): return lax.ppermute(value, AXES, route)  53.2 us
    ppermute x18, starting transfers between devices, hop(): return lax.ppermute(value, AXES, route)  18.8 us
    pallas_call x1, Pallas kernels, match_early(): pl.pallas_call(functools.partial(early_kernel, nsrc=nsrc, ntgt=ntgt, cell...  6.13 us
  transfers between devices with their start and end apart: 18, of which 13 were waited for; matrix products, arithmetic and copies ran while one was open for 1% of the time, Pallas kernels for 4%

commit v1 on v0

--- a/solution.py
+++ b/solution.py
@@ -86,40 +86,80 @@
     return (x ^ (x >> 1)) & 1, x >> 1
 
 
-def pick_kernel(table_ref, *refs, counts):
-    pieces = [refs[4 * v : 4 * v + 4] for v in range(len(counts))]
-    outs = refs[4 * len(counts) :]
+def seat(frame, frames):
     me_x, me_y, core = lax.axis_index("fx"), lax.axis_index("fy"), lax.axis_index("bc")
     me_a, me_b = gray(me_x)
-    frames = sum(counts)
-    for slot in range(outs[0].shape[0]):
+    group = frame // frames
+    to_a, to_b = gray(group // 2)
+    fa, fb, fy = to_a ^ me_a, to_b ^ me_b, (group % 2) ^ me_y
+    other = core == 1
+    first = (jnp.where(other, fb, fy), jnp.where(other, fy, fa), jnp.where(other, fa, fb))
+    return (first, (fa, fb, fy)), frame % frames
+
+
+def copy_held(pieces, bits, which, frames, take, also=True):
+    place = bits[0] + 2 * bits[1]
+    for piece, low, span in zip(pieces, (0, 1, 2), (1, 1, 2)):
+
+        @pl.when((place >= low) & (place < low + span) & also)
+        def _():
+            take(piece[(place - low) * frames + which])
+
+
+def offer_kernel(*refs, parts):
+    tables, pieces, outs = refs[:parts], refs[parts : 4 * parts], refs[4 * parts :]
+    frames = pieces[0].shape[0]
+    for v in range(parts):
+        for slot in range(tables[v].shape[0]):
+            for side in range(2):
+                seats, which = seat(tables[v][slot, side], frames)
+
+                def take(value):
+                    outs[v][2 * slot + side] = value
+
+                copy_held(pieces[3 * v : 3 * v + 3], seats[v], which, frames, take)
+
+
+def offer(tables, held):
+    pieces = [piece for have in held for piece in have]
+    slots = 2 * tables[0].shape[0]
+    return pl.pallas_call(
+        functools.partial(offer_kernel, parts=len(held)),
+        out_shape=[jax.ShapeDtypeStruct((slots,) + have[0].shape[1:], have[0].dtype) for have in held],
+        in_specs=[SMEM] * len(held) + [VMEM] * len(pieces),
+        out_specs=[VMEM] * len(held),
+        compiler_params=pltpu.CompilerParams(vmem_limit_bytes=8 << 20),
+    )(*tables, *pieces)
+
+
+def pick_kernel(table, *refs, parts):
+    pieces, outs = refs[: 4 * parts], refs[4 * parts :]
+    frames = pieces[0].shape[0]
+    for slot in range(table.shape[0]):
         for side in range(2):
-            frame = table_ref[slot, side]
-            which, group = frame % frames, frame // frames
-            to_a, to_b = gray(group // 2)
-            fa, fb, fy = to_a ^ me_a, to_b ^ me_b, (group % 2) ^ me_y
-            other = core == 1
-            first = (jnp.where(other, fb, fy), jnp.where(other, fy, fa), jnp.where(other, fa, fb))
-            low_frame = 0
-            for v, bits in enumerate((first, (fa, fb, fy))):
-                count = counts[v]
-                place = bits[0] + 2 * bits[1] + 4 * bits[2]
-                mine = (which >= low_frame) & (which < low_frame + count)
-                for m, (low, span) in enumerate(((0, 1), (1, 1), (2, 2), (4, 4))):
-
-                    @pl.when(mine & (place >= low) & (place < low + span))
-                    def _():
-                        outs[side][slot] = pieces[v][m][(place - low) * count + which - low_frame]
-
-                low_frame += count
-
-
-def pick(table, held, counts):
-    block = held[0][0].shape[1:]
+            seats, which = seat(table[slot, side], frames)
+            start = 0
+            for v in range(parts):
+                count = pieces[4 * v].shape[1]
+
+                def take(value):
+                    outs[side][slot, start : start + count] = value
+
+                copy_held(pieces[4 * v : 4 * v + 3], seats[v], which, frames, take, seats[v][2] == 0)
+
+                @pl.when(seats[v][2] == 1)
+                def _():
+                    take(pieces[4 * v + 3][2 * slot + side])
+
+                start += count
+
+
+def pick(table, held):
     pieces = [piece for have in held for piece in have]
-    shape = jax.ShapeDtypeStruct((table.shape[0],) + block, pieces[0].dtype)
+    cells = sum(have[0].shape[1] for have in held)
+    shape = jax.ShapeDtypeStruct((table.shape[0], cells, pieces[0].shape[2]), pieces[0].dtype)
     return pl.pallas_call(
-        functools.partial(pick_kernel, counts=counts),
+        functools.partial(pick_kernel, parts=len(held)),
         out_shape=[shape, shape],
         in_specs=[SMEM] + [VMEM] * len(pieces),
         out_specs=[VMEM, VMEM],
@@ -408,7 +448,7 @@
             pltpu.VMEM((ntgt, 8, cells), jnp.float32),
         ],
         compiler_params=pltpu.CompilerParams(vmem_limit_bytes=24 << 20),
-        cost_estimate=cost(pairs, 2 * nsrc),
+        cost_estimate=cost(pairs, nsrc),
     )(*src, *tgt, *early)
 
 
@@ -519,19 +559,20 @@
     )(weight.reshape(-1), bias.reshape(-1), chip, own, core)
 
 
-def gather_frames(blocks):
+def gather_frames(blocks, table):
     orders = (
         (by_core(flip_y, flip_b), by_core(flip_a, flip_y), by_core(flip_b, flip_a)),
         (flip_a, flip_b, flip_y),
     )
-    held = [[block] for block in blocks]
-    for stage in range(3):
-        send = [have[0] if len(have) == 1 else jnp.concatenate(have, axis=0) for have in held]
-        got = [hop(part, order[stage]) for part, order in zip(send, orders)]
-        got = lax.optimization_barrier(got)
-        for have, piece in zip(held, got):
-            have.append(piece)
-    return held
+    first = lax.optimization_barrier([hop(block, order[0]) for block, order in zip(blocks, orders)])
+    held = [[block, piece] for block, piece in zip(blocks, first)]
+    send = [jnp.concatenate(have, axis=0) for have in held]
+    second = [hop(part, order[1]) for part, order in zip(send, orders)]
+    tables = [hop(table, order[2]) for order in orders]
+    second, tables = lax.optimization_barrier((second, tables))
+    held = [have + [piece] for have, piece in zip(held, second)]
+    sent = [hop(part, order[2]) for part, order in zip(offer(tables, held), orders)]
+    return pick(table, [have + [piece] for have, piece in zip(held, sent)])
 
 
 def matched(src0, tgt0):
@@ -539,11 +580,11 @@
     tgt1 = hop(tgt0, ring)
     src2 = hop(src0, flip_c)
     tgt2 = hop(tgt0, back)
-    tgt1, src1, src2 = lax.optimization_barrier((tgt1, src1, src2))
+    tgt1, src1, src2, tgt2 = lax.optimization_barrier((tgt1, src1, src2, tgt2))
     tgt3 = hop(tgt1, ring)
     src3 = hop(src1, flip_c)
     src = (src0, src1, src2, src3)
-    early = match_early(src, (tgt0, tgt1))
+    early = match_early(src, (tgt0, tgt1, tgt2))
     return match_late(src, (tgt0, tgt1, tgt2, tgt3), early)
 
 
@@ -551,9 +592,8 @@
     frames, band_rows, width, chans = features.shape
     cells = band_rows * width
     flat_features = features.reshape(frames, cells, chans)
-    counts = (frames - 1, 1)
-    held = gather_frames([flat_features[:-1], flat_features[-1:]])
-    src0, tgt0 = pick(frame_pairs, held, counts)
+    cut = cells * 11 // 16
+    src0, tgt0 = gather_frames([flat_features[:, :cut], flat_features[:, cut:]], frame_pairs)
     fwd_keep, fwd_send, rev_keep, rev_send = matched(src0, tgt0)
     fwd0, fwd1, rev0, rev1 = half(fwd_keep, hop(fwd_send, flip_c), rev_keep, hop(rev_send, flip_za), band_rows)
     flows = merge(fwd0, hop(fwd1, flip_h), rev0, hop(rev1, flip_zb), band_rows, width)

time: 163 us -> 156 us (0.957)
  waiting for transfers between devices: 53.2 us -> 41 us
  starting transfers between devices: 18.8 us -> 23.7 us
  other arithmetic: 2.01 us -> 0.07 us
    ppermute x18 -> x20, waiting for transfers between devices: 53.2 us -> 41 us  [hop(): return lax.ppermute(value, AXES, route)]
    ppermute x18 -> x20, starting transfers between devices: 18.8 us -> 23.7 us  [hop(): return lax.ppermute(value, AXES, route)]
    pallas_call x1, Pallas kernels: 6.13 us -> 9.07 us  [match_early(): pl.pallas_call(functools.partial(early_kernel, nsrc=nsrc, ntgt=ntgt, cell...]
    pallas_call x1, Pallas kernels: 76.6 us -> 74 us  [match_late(): pl.pallas_call(functools.partial(late_kernel, nsrc=nsrc, ntgt=ntgt, cells...]
    concatenate x4 -> x2, other arithmetic: 2.01 us -> 0.07 us  [gather_frames(): send = [jnp.concatenate(have, axis=0) for have in held]]
  transfers between devices with their start and end apart: 18 -> 20, of which waited for: 13 -> 14; matrix products, arithmetic and copies ran while one was open for 1% -> 1% of each run, Pallas kernels for 4% -> 6%
where the time goes in v1:
time: 156 us; the launch traced here: 155 us
  Pallas kernels  87.3 us (56%)
  waiting for transfers between devices  41 us (26%)
  starting transfers between devices  23.7 us (15%)
  local copies, waits for them, and re-layouts  3.16 us (2%)
    pallas_call x1, Pallas kernels, match_late(): pl.pallas_call(functools.partial(late_kernel, nsrc=nsrc, ntgt=ntgt, cells...  74 us
    ppermute x20, waiting for transfers between devices, hop(): return lax.ppermute(value, AXES, route)  41 us
    ppermute x20, starting transfers between devices, hop(): return lax.ppermute(value, AXES, route)  23.7 us
    pallas_call x1, Pallas kernels, match_early(): pl.pallas_call(functools.partial(early_kernel, nsrc=nsrc, ntgt=ntgt, cell...  9.07 us
  transfers between devices with their start and end apart: 20, of which 14 were waited for; matrix products, arithmetic and copies ran while one was open for 1% of the time, Pallas kernels for 6%

profile of v1, /device:TPU:0, one launch (start us, length us, event | category | flops | bytes accessed | tf_op | source)
XLA Modules:
  0.0 155.4 jit_solution(14968115692558491357)
XLA Ops:
  0.0 1.0 slice.8.refs_2_.refs_0_
  1.0 1.8 %collective-permute-start = (bf16[3,352,128]{2,1,0:T(8,128)(2,1)S(1)}, bf16[3,352,128]{2,1,0:T(8,128)(2,1)S(1)}, u32[]{:S(2)}, u32[]{:S(2)}) collective-permute-start(bf16[3,352,128]{2,1,0:T(8,128)(2,1)S(1)} %slice.8.refs_2_.refs_0_), channel_id=1, source_target_pairs={{0,16},{1,97},{2,18},{3,99},{4,20},{5,101},{6,22},{7,103},{8,24},{... | collective-permute-start | bytes 811016 | tf_op jit(solution)/shard_map/ppermute | solution.py:34
  2.7 0.9 slice.9.refs_5_.refs_4_
  3.7 1.6 %collective-permute-start.1 = (bf16[3,160,128]{2,1,0:T(8,128)(2,1)S(1)}, bf16[3,160,128]{2,1,0:T(8,128)(2,1)S(1)}, u32[]{:S(2)}, u32[]{:S(2)}) collective-permute-start(bf16[3,160,128]{2,1,0:T(8,128)(2,1)S(1)} %slice.9.refs_5_.refs_4_), channel_id=1, source_target_pairs={{0,32},{1,33},{2,34},{3,35},{4,36},{5,37},{6,38},{7,39},{8,40},{9,... | collective-permute-start | bytes 368648 | tf_op jit(solution)/shard_map/ppermute | solution.py:34
  5.2 4.5 %collective-permute-done.1.refs_6_.refs_5_ = bf16[3,160,128]{2,1,0:T(8,128)(2,1)S(1)} collective-permute-done((bf16[3,160,128]{2,1,0:T(8,128)(2,1)S(1)}, bf16[3,160,128]{2,1,0:T(8,128)(2,1)S(1)}, u32[]{:S(2)}, u32[]{:S(2)}) %collective-permute-start.1) | collective-permute-done | bytes 122912 | tf_op jit(solution)/shard_map/ppermute | solution.py:34
  9.7 0.5 collective-permute-start.2
  10.3 2.2 %collective-permute-start.3 = (bf16[6,160,128]{2,1,0:T(8,128)(2,1)S(1)}, bf16[6,160,128]{2,1,0:T(8,128)(2,1)S(1)}, u32[]{:S(2)}, u32[]{:S(2)}) collective-permute-start(bf16[6,160,128]{2,1,0:T(8,128)(2,1)S(1)} %pad_maximum_fusion.1), channel_id=1, source_target_pairs={{0,96},{1,97},{2,98},{3,99},{4,100},{5,101},{6,102},{7,103},{8,104... | collective-permute-start | bytes 737288 | tf_op jit(solution)/shard_map/ppermute | solution.py:34
  12.4 0.8 copy.13.table
  13.2 1.1 collective-permute-start.4
  14.3 1.5 collective-permute-start.5
  15.8 3.3 %collective-permute-done.4.refs_0_ = s32[3,2]{1,0:T(4,128)S(1)} collective-permute-done((s32[3,2]{1,0:T(4,128)S(1)}, s32[3,2]{1,0:T(4,128)S(1)}, u32[]{:S(2)}, u32[]{:S(2)}) %collective-permute-start.4) | collective-permute-done | bytes 56 | tf_op jit(solution)/shard_map/ppermute | solution.py:34
  19.2 1.1 shard_map.46
  20.3 1.8 %collective-permute-start.6 = (bf16[6,352,128]{2,1,0:T(8,128)(2,1)S(1)}, bf16[6,352,128]{2,1,0:T(8,128)(2,1)S(1)}, u32[]{:S(2)}, u32[]{:S(2)}) collective-permute-start(bf16[6,352,128]{2,1,0:T(8,128)(2,1)S(1)} %get-tuple-element.38), channel_id=1, source_target_pairs={{0,96},{1,33},{2,98},{3,35},{4,100},{5,37},{6,102},{7,39},{8,104},... | collective-permute-start | bytes 1622024 | tf_op jit(solution)/shard_map/ppermute | solution.py:34
  22.1 0.6 collective-permute-start.7
  22.7 5.6 %collective-permute-done.7.refs_7_ = bf16[6,160,128]{2,1,0:T(8,128)(2,1)S(1)} collective-permute-done((bf16[6,160,128]{2,1,0:T(8,128)(2,1)S(1)}, bf16[6,160,128]{2,1,0:T(8,128)(2,1)S(1)}, u32[]{:S(2)}, u32[]{:S(2)}) %collective-permute-start.7) | collective-permute-done | bytes 245792 | tf_op jit(solution)/shard_map/ppermute | solution.py:34
  28.3 2.7 %collective-permute-done.6.refs_3_ = bf16[6,352,128]{2,1,0:T(8,128)(2,1)S(1)} collective-permute-done((bf16[6,352,128]{2,1,0:T(8,128)(2,1)S(1)}, bf16[6,352,128]{2,1,0:T(8,128)(2,1)S(1)}, u32[]{:S(2)}, u32[]{:S(2)}) %collective-permute-start.6) | collective-permute-done | bytes 540704 | tf_op jit(solution)/shard_map/ppermute | solution.py:34
  31.0 1.1 shard_map.47
  32.1 4.2 %collective-permute-start.11 = (bf16[3,512,128]{2,1,0:T(8,128)(2,1)S(1)}, bf16[3,512,128]{2,1,0:T(8,128)(2,1)S(1)}, u32[]{:S(2)}, u32[]{:S(2)}) collective-permute-start(bf16[3,512,128]{2,1,0:T(8,128)(2,1)S(1)} %get-tuple-element.41.refs_4_), channel_id=1, source_target_pairs={{0,6},{1,3},{2,0},{3,5},{4,2},{5,7},{6,4},{7,1},{8,14},{9,11},{10,... | collective-permute-start | bytes 1179656 | tf_op jit(solution)/shard_map/ppermute | solution.py:34
  36.3 3.2 %collective-permute-start.9 = (bf16[3,512,128]{2,1,0:T(8,128)(2,1)S(1)}, bf16[3,512,128]{2,1,0:T(8,128)(2,1)S(1)}, u32[]{:S(2)}, u32[]{:S(2)}) collective-permute-start(bf16[3,512,128]{2,1,0:T(8,128)(2,1)S(1)} %get-tuple-element.40.refs_0_), channel_id=1, source_target_pairs={{0,8},{1,9},{2,10},{3,11},{4,12},{5,13},{6,14},{7,15},{8,0},{9,1},... | collective-permute-start | bytes 1179656 | tf_op jit(solution)/shard_map/ppermute | solution.py:34
  39.5 5.8 %collective-permute-done.11.refs_6_ = bf16[3,512,128]{2,1,0:T(8,128)(2,1)S(1)} collective-permute-done((bf16[3,512,128]{2,1,0:T(8,128)(2,1)S(1)}, bf16[3,512,128]{2,1,0:T(8,128)(2,1)S(1)}, u32[]{:S(2)}, u32[]{:S(2)}) %collective-permute-start.11) | collective-permute-done | bytes 393248 | tf_op jit(solution)/shard_map/ppermute | solution.py:34
  45.3 0.7 collective-permute-done.8.refs_5_
  46.0 3.0 %collective-permute-done.9.refs_1_ = bf16[3,512,128]{2,1,0:T(8,128)(2,1)S(1)} collective-permute-done((bf16[3,512,128]{2,1,0:T(8,128)(2,1)S(1)}, bf16[3,512,128]{2,1,0:T(8,128)(2,1)S(1)}, u32[]{:S(2)}, u32[]{:S(2)}) %collective-permute-start.9) | collective-permute-done | bytes 393248 | tf_op jit(solution)/shard_map/ppermute | solution.py:34
  49.0 1.7 %collective-permute-done.12.refs_3_ = bf16[3,512,128]{2,1,0:T(8,128)(2,1)S(1)} collective-permute-done((bf16[3,512,128]{2,1,0:T(8,128)(2,1)S(1)}, bf16[3,512,128]{2,1,0:T(8,128)(2,1)S(1)}, u32[]{:S(2)}, u32[]{:S(2)}) %collective-permute-start.12) | collective-permute-done | bytes 393248 | tf_op jit(solution)/shard_map/ppermute | solution.py:34
  50.7 9.1 %shard_map.48 = (f32[3,2048,128]{2,1,0:T(8,128)S(1)}, f32[3,2048,128]{2,1,0:T(8,128)S(1)}, f32[3,3,8,512]{3,2,1,0:T(8,128)S(1)}, f32[3,3,8,512]{3,2,1,0:T(8,128)S(1)}, f32[3,3,8,512]{3,2,1,0:T(8,128)S(1)}) custom-call(bf16[3,512,128]{2,1,0:T(8,128)(2,1)S(1)} %get-tuple-element.40.refs_0_, bf16[3,512,128]{2,1,0:T(8,128)(2,1)S(1)} %collective-permute-done.9.refs_1_, ...), custom_call_target="tpu_custom_call" | custom-call | flops 4824000000 | bytes 3600000 | tf_op jit(solution)/shard_map/pallas_call | solution.py:418
  59.8 74.0 %shard_map.49 = (f32[2,3,16,128]{3,2,1,0:T(8,128)S(1)}, f32[2,3,16,128]{3,2,1,0:T(8,128)S(1)}, f32[2,3,16,128]{3,2,1,0:T(8,128)S(1)}, f32[2,3,16,128]{3,2,1,0:T(8,128)S(1)}) custom-call(bf16[3,512,128]{2,1,0:T(8,128)(2,1)S(1)} %get-tuple-element.40.refs_0_, bf16[3,512,128]{2,1,0:T(8,128)(2,1)S(1)} %collective-permute-done.9.refs_1_, ...), custom_call_target="tpu_custom_call" | custom-call | flops 1608000000 | bytes 1200000 | tf_op jit(solution)/shard_map/pallas_call | solution.py:434
  134.0 1.1 collective-permute-done.14.fwd_in
  135.1 3.0 %collective-permute-done.15.rev_in = f32[2,3,16,128]{3,2,1,0:T(8,128)S(1)} collective-permute-done((f32[2,3,16,128]{3,2,1,0:T(8,128)S(1)}, f32[2,3,16,128]{3,2,1,0:T(8,128)S(1)}, u32[]{:S(2)}, u32[]{:S(2)}) %collective-permute-start.15) | collective-permute-done | bytes 49184 | tf_op jit(solution)/shard_map/ppermute | solution.py:34
  138.1 3.3 %collective-permute-start.16 = (f32[3,16,128]{2,1,0:T(8,128)S(1)}, f32[3,16,128]{2,1,0:T(8,128)S(1)}, u32[]{:S(2)}, u32[]{:S(2)}) collective-permute-start(f32[3,16,128]{2,1,0:T(8,128)S(1)} %get-tuple-element.56), channel_id=1, source_target_pairs={{0,8},{1,9},{2,10},{3,11},{4,12},{5,13},{6,14},{7,15},{8,0},{9,1},... | collective-permute-start | bytes 73736 | tf_op jit(solution)/shard_map/ppermute | solution.py:34
  141.4 1.7 %collective-permute-start.17 = (f32[3,16,128]{2,1,0:T(8,128)S(1)}, f32[3,16,128]{2,1,0:T(8,128)S(1)}, u32[]{:S(2)}, u32[]{:S(2)}) collective-permute-start(f32[3,16,128]{2,1,0:T(8,128)S(1)} %get-tuple-element.58), channel_id=1, source_target_pairs={{0,6},{1,7},{2,4},{3,5},{4,2},{5,3},{6,0},{7,1},{8,14},{9,15},{10,... | collective-permute-start | bytes 73736 | tf_op jit(solution)/shard_map/ppermute | solution.py:34
  143.5 2.9 %collective-permute-done.17.rev_in = f32[3,16,128]{2,1,0:T(8,128)S(1)} collective-permute-done((f32[3,16,128]{2,1,0:T(8,128)S(1)}, f32[3,16,128]{2,1,0:T(8,128)S(1)}, u32[]{:S(2)}, u32[]{:S(2)}) %collective-permute-start.17) | collective-permute-done | bytes 24608 | tf_op jit(solution)/shard_map/ppermute | solution.py:34
  147.1 6.2 %collective-permute-done.18.chip = f32[3,2,2,4,128]{4,3,2,1,0:T(4,128)S(1)} collective-permute-done((f32[3,2,2,4,128]{4,3,2,1,0:T(4,128)S(1)}, f32[3,2,2,4,128]{4,3,2,1,0:T(4,128)S(1)}, u32[]{:S(2)}, u32[]{:S(2)}) %collective-permute-start.18) | collective-permute-done | bytes 24608 | tf_op jit(solution)/shard_map/ppermute | solution.py:34
  153.4 2.0 %shard_map.52 = f32[3,2,2,4,128]{4,3,2,1,0:T(4,128)} custom-call(f32[144]{0:T(256)S(1)} %reshape.9.weight, f32[8]{0:T(128)S(1)} %reshape.10.bias, f32[3,2,2,4,128]{4,3,2,1,0:T(4,128)S(1)} %collective-permute-done.18.chip, f32[3,2,2,4,128]{4,3,2,1,0:T(4,128)S(1)} %shard_map.51.own, f32[3,2,2,4,128]{4,3,2,1,0:T(4,128)S(1)} %collective-permute-done.19.core), custom_call_target="tpu_custom_call" | custom-call | tf_op jit(solution)/shard_map/pallas_call | solution.py:552
  (28 shorter events, 1.6 us)
Async XLA Ops:
  1.0 8.7 %collective-permute-start = (bf16[3,352,128]{2,1,0:T(8,128)(2,1)S(1)}, bf16[3,352,128]{2,1,0:T(8,128)(2,1)S(1)}, u32[]{:S(2)}, u32[]{:S(2)}) collective-permute-start(bf16[3,352,128]{2,1,0:T(8,128)(2,1)S(1)} %slice.8.refs_2_.refs_0_), channel_id=1, source_target_pairs={{0,16},{1,97},{2,18},{3,99},{4,20},{5,101},{6,22},{7,103},{8,24},{... | collective-permute-start | bytes 811016 | tf_op jit(solution)/shard_map/ppermute | solution.py:34
  3.7 6.0 %collective-permute-start.1 = (bf16[3,160,128]{2,1,0:T(8,128)(2,1)S(1)}, bf16[3,160,128]{2,1,0:T(8,128)(2,1)S(1)}, u32[]{:S(2)}, u32[]{:S(2)}) collective-permute-start(bf16[3,160,128]{2,1,0:T(8,128)(2,1)S(1)} %slice.9.refs_5_.refs_4_), channel_id=1, source_target_pairs={{0,32},{1,33},{2,34},{3,35},{4,36},{5,37},{6,38},{7,39},{8,40},{9,... | collective-permute-start | bytes 368648 | tf_op jit(solution)/shard_map/ppermute | solution.py:34
  9.7 9.5 %collective-permute-start.2 = (bf16[6,352,128]{2,1,0:T(8,128)(2,1)S(1)}, bf16[6,352,128]{2,1,0:T(8,128)(2,1)S(1)}, u32[]{:S(2)}, u32[]{:S(2)}) collective-permute-start(bf16[6,352,128]{2,1,0:T(8,128)(2,1)S(1)} %pad_maximum_fusion), channel_id=1, source_target_pairs={{0,32},{1,17},{2,34},{3,19},{4,36},{5,21},{6,38},{7,23},{8,40},{9,... | collective-permute-start | bytes 1622024 | tf_op jit(solution)/shard_map/ppermute | solution.py:34
  10.3 8.9 %collective-permute-start.3 = (bf16[6,160,128]{2,1,0:T(8,128)(2,1)S(1)}, bf16[6,160,128]{2,1,0:T(8,128)(2,1)S(1)}, u32[]{:S(2)}, u32[]{:S(2)}) collective-permute-start(bf16[6,160,128]{2,1,0:T(8,128)(2,1)S(1)} %pad_maximum_fusion.1), channel_id=1, source_target_pairs={{0,96},{1,97},{2,98},{3,99},{4,100},{5,101},{6,102},{7,103},{8,104... | collective-permute-start | bytes 737288 | tf_op jit(solution)/shard_map/ppermute | solution.py:34
  13.2 5.9 %collective-permute-start.4 = (s32[3,2]{1,0:T(4,128)S(1)}, s32[3,2]{1,0:T(4,128)S(1)}, u32[]{:S(2)}, u32[]{:S(2)}) collective-permute-start(s32[3,2]{1,0:T(4,128)S(1)} %copy.13.table), channel_id=1, source_target_pairs={{0,96},{1,33},{2,98},{3,35},{4,100},{5,37},{6,102},{7,39},{8,104},... | collective-permute-start | bytes 80 | tf_op jit(solution)/shard_map/ppermute | solution.py:34
  14.3 4.8 %collective-permute-start.5 = (s32[3,2]{1,0:T(4,128)S(1)}, s32[3,2]{1,0:T(4,128)S(1)}, u32[]{:S(2)}, u32[]{:S(2)}) collective-permute-start(s32[3,2]{1,0:T(4,128)S(1)} %copy.13.table), channel_id=1, source_target_pairs={{0,16},{1,17},{2,18},{3,19},{4,20},{5,21},{6,22},{7,23},{8,24},{9,... | collective-permute-start | bytes 80 | tf_op jit(solution)/shard_map/ppermute | solution.py:34
  20.3 10.6 %collective-permute-start.6 = (bf16[6,352,128]{2,1,0:T(8,128)(2,1)S(1)}, bf16[6,352,128]{2,1,0:T(8,128)(2,1)S(1)}, u32[]{:S(2)}, u32[]{:S(2)}) collective-permute-start(bf16[6,352,128]{2,1,0:T(8,128)(2,1)S(1)} %get-tuple-element.38), channel_id=1, source_target_pairs={{0,96},{1,33},{2,98},{3,35},{4,100},{5,37},{6,102},{7,39},{8,104},... | collective-permute-start | bytes 1622024 | tf_op jit(solution)/shard_map/ppermute | solution.py:34
  22.1 6.2 %collective-permute-start.7 = (bf16[6,160,128]{2,1,0:T(8,128)(2,1)S(1)}, bf16[6,160,128]{2,1,0:T(8,128)(2,1)S(1)}, u32[]{:S(2)}, u32[]{:S(2)}) collective-permute-start(bf16[6,160,128]{2,1,0:T(8,128)(2,1)S(1)} %get-tuple-element.39), channel_id=1, source_target_pairs={{0,16},{1,17},{2,18},{3,19},{4,20},{5,21},{6,22},{7,23},{8,24},{9,... | collective-permute-start | bytes 737288 | tf_op jit(solution)/shard_map/ppermute | solution.py:34
  32.0 7.5 %collective-permute-start.10 = (bf16[3,512,128]{2,1,0:T(8,128)(2,1)S(1)}, bf16[3,512,128]{2,1,0:T(8,128)(2,1)S(1)}, u32[]{:S(2)}, u32[]{:S(2)}) collective-permute-start(bf16[3,512,128]{2,1,0:T(8,128)(2,1)S(1)} %get-tuple-element.40.refs_0_), channel_id=1, source_target_pairs={{0,1},{1,0},{2,3},{3,2},{4,5},{5,4},{6,7},{7,6},{8,9},{9,8},{10,11... | collective-permute-start | bytes 1179656 | tf_op jit(solution)/shard_map/ppermute | solution.py:34
  32.1 13.1 %collective-permute-start.11 = (bf16[3,512,128]{2,1,0:T(8,128)(2,1)S(1)}, bf16[3,512,128]{2,1,0:T(8,128)(2,1)S(1)}, u32[]{:S(2)}, u32[]{:S(2)}) collective-permute-start(bf16[3,512,128]{2,1,0:T(8,128)(2,1)S(1)} %get-tuple-element.41.refs_4_), channel_id=1, source_target_pairs={{0,6},{1,3},{2,0},{3,5},{4,2},{5,7},{6,4},{7,1},{8,14},{9,11},{10,... | collective-permute-start | bytes 1179656 | tf_op jit(solution)/shard_map/ppermute | solution.py:34
  36.3 9.7 %collective-permute-start.8 = (bf16[3,512,128]{2,1,0:T(8,128)(2,1)S(1)}, bf16[3,512,128]{2,1,0:T(8,128)(2,1)S(1)}, u32[]{:S(2)}, u32[]{:S(2)}) collective-permute-start(bf16[3,512,128]{2,1,0:T(8,128)(2,1)S(1)} %get-tuple-element.41.refs_4_), channel_id=1, source_target_pairs={{0,2},{1,7},{2,4},{3,1},{4,6},{5,3},{6,0},{7,5},{8,10},{9,15},{10,... | collective-permute-start | bytes 1179656 | tf_op jit(solution)/shard_map/ppermute | solution.py:34
  36.3 12.7 %collective-permute-start.9 = (bf16[3,512,128]{2,1,0:T(8,128)(2,1)S(1)}, bf16[3,512,128]{2,1,0:T(8,128)(2,1)S(1)}, u32[]{:S(2)}, u32[]{:S(2)}) collective-permute-start(bf16[3,512,128]{2,1,0:T(8,128)(2,1)S(1)} %get-tuple-element.40.refs_0_), channel_id=1, source_target_pairs={{0,8},{1,9},{2,10},{3,11},{4,12},{5,13},{6,14},{7,15},{8,0},{9,1},... | collective-permute-start | bytes 1179656 | tf_op jit(solution)/shard_map/ppermute | solution.py:34
  49.0 1.7 %collective-permute-start.12 = (bf16[3,512,128]{2,1,0:T(8,128)(2,1)S(1)}, bf16[3,512,128]{2,1,0:T(8,128)(2,1)S(1)}, u32[]{:S(2)}, u32[]{:S(2)}) collective-permute-start(bf16[3,512,128]{2,1,0:T(8,128)(2,1)S(1)} %collective-permute-done.9.refs_1_), channel_id=1, source_target_pairs={{0,1},{1,0},{2,3},{3,2},{4,5},{5,4},{6,7},{7,6},{8,9},{9,8},{10,11... | collective-permute-start | bytes 1179656 | tf_op jit(solution)/shard_map/ppermute | solution.py:34
  49.0 10.8 %collective-permute-start.13 = (bf16[3,512,128]{2,1,0:T(8,128)(2,1)S(1)}, bf16[3,512,128]{2,1,0:T(8,128)(2,1)S(1)}, u32[]{:S(2)}, u32[]{:S(2)}) collective-permute-start(bf16[3,512,128]{2,1,0:T(8,128)(2,1)S(1)} %collective-permute-done.8.refs_5_), channel_id=1, source_target_pairs={{0,2},{1,7},{2,4},{3,1},{4,6},{5,3},{6,0},{7,5},{8,10},{9,15},{10,... | collective-permute-start | bytes 1179656 | tf_op jit(solution)/shard_map/ppermute | solution.py:34
  59.8 86.8 %copy-start = (f32[4,2,2,3,3]{0,2,4,3,1:T(2,128)S(1)}, f32[4,2,2,3,3]{0,2,4,3,1:T(2,128)}, u32[]{:S(2)}) copy-start(f32[4,2,2,3,3]{0,2,4,3,1:T(2,128)} %param.6) | copy-start | bytes 1732
  59.8 87.2 %copy-start.1 = (f32[4,2]{0,1:T(2,128)S(1)}, f32[4,2]{0,1:T(2,128)}, u32[]{:S(2)}) copy-start(f32[4,2]{0,1:T(2,128)} %param.7) | copy-start | bytes 100
  133.8 1.3 collective-permute-start.14
  133.9 4.2 %collective-permute-start.15 = (f32[2,3,16,128]{3,2,1,0:T(8,128)S(1)}, f32[2,3,16,128]{3,2,1,0:T(8,128)S(1)}, u32[]{:S(2)}, u32[]{:S(2)}) collective-permute-start(f32[2,3,16,128]{3,2,1,0:T(8,128)S(1)} %get-tuple-element.54), channel_id=1, source_target_pairs={{0,2},{1,3},{2,0},{3,1},{4,6},{5,7},{6,4},{7,5},{8,10},{9,11},{10,... | collective-permute-start | bytes 147464 | tf_op jit(solution)/shard_map/ppermute | solution.py:34
  138.1 5.4 %collective-permute-start.16 = (f32[3,16,128]{2,1,0:T(8,128)S(1)}, f32[3,16,128]{2,1,0:T(8,128)S(1)}, u32[]{:S(2)}, u32[]{:S(2)}) collective-permute-start(f32[3,16,128]{2,1,0:T(8,128)S(1)} %get-tuple-element.56), channel_id=1, source_target_pairs={{0,8},{1,9},{2,10},{3,11},{4,12},{5,13},{6,14},{7,15},{8,0},{9,1},... | collective-permute-start | bytes 73736 | tf_op jit(solution)/shard_map/ppermute | solution.py:34
  141.4 5.0 %collective-permute-start.17 = (f32[3,16,128]{2,1,0:T(8,128)S(1)}, f32[3,16,128]{2,1,0:T(8,128)S(1)}, u32[]{:S(2)}, u32[]{:S(2)}) collective-permute-start(f32[3,16,128]{2,1,0:T(8,128)S(1)} %get-tuple-element.58), channel_id=1, source_target_pairs={{0,6},{1,7},{2,4},{3,5},{4,2},{5,3},{6,0},{7,1},{8,14},{9,15},{10,... | collective-permute-start | bytes 73736 | tf_op jit(solution)/shard_map/ppermute | solution.py:34
  146.4 6.9 %collective-permute-start.18 = (f32[3,2,2,4,128]{4,3,2,1,0:T(4,128)S(1)}, f32[3,2,2,4,128]{4,3,2,1,0:T(4,128)S(1)}, u32[]{:S(2)}, u32[]{:S(2)}) collective-permute-start(f32[3,2,2,4,128]{4,3,2,1,0:T(4,128)S(1)} %shard_map.51.own), channel_id=1, source_target_pairs={{0,15},{1,2},{2,1},{3,4},{4,3},{5,6},{6,5},{7,8},{8,7},{9,10},{10,... | collective-permute-start | bytes 73736 | tf_op jit(solution)/shard_map/ppermute | solution.py:34
  146.5 6.9 %collective-permute-start.19 = (f32[3,2,2,4,128]{4,3,2,1,0:T(4,128)S(1)}, f32[3,2,2,4,128]{4,3,2,1,0:T(4,128)S(1)}, u32[]{:S(2)}, u32[]{:S(2)}) collective-permute-start(f32[3,2,2,4,128]{4,3,2,1,0:T(4,128)S(1)} %shard_map.51.own), channel_id=1, source_target_pairs={{0,1},{1,0},{2,3},{3,2},{4,5},{5,4},{6,7},{7,6},{8,9},{9,8},{10,11... | collective-permute-start | bytes 73736 | tf_op jit(solution)/shard_map/ppermute | solution.py:34

commit v2 on v1

--- a/solution.py
+++ b/solution.py
@@ -79,7 +79,9 @@
 
 def next_chip(x, y, h, z, c):
     band = (h * SIZES[3] + z) * SIZES[4] + c + 2 * c - 1
-    return x, y, band // (SIZES[3] * SIZES[4]) % SIZES[2], band // SIZES[4] % SIZES[3], band % SIZES[4]
+    if band < 0 or band >= SIZES[2] * SIZES[3] * SIZES[4]:
+        return x, y, h, z, c
+    return x, y, band // (SIZES[3] * SIZES[4]), band // SIZES[4] % SIZES[3], band % SIZES[4]
 
 
 def gray(x):
@@ -564,22 +566,22 @@
         (by_core(flip_y, flip_b), by_core(flip_a, flip_y), by_core(flip_b, flip_a)),
         (flip_a, flip_b, flip_y),
     )
-    first = lax.optimization_barrier([hop(block, order[0]) for block, order in zip(blocks, orders)])
+    first = [hop(block, order[0]) for block, order in zip(blocks, orders)]
+    tables = [hop(table, order[2]) for order in orders]
+    first, tables = lax.optimization_barrier((first, tables))
     held = [[block, piece] for block, piece in zip(blocks, first)]
     send = [jnp.concatenate(have, axis=0) for have in held]
-    second = [hop(part, order[1]) for part, order in zip(send, orders)]
-    tables = [hop(table, order[2]) for order in orders]
-    second, tables = lax.optimization_barrier((second, tables))
+    second = lax.optimization_barrier([hop(part, order[1]) for part, order in zip(send, orders)])
     held = [have + [piece] for have, piece in zip(held, second)]
     sent = [hop(part, order[2]) for part, order in zip(offer(tables, held), orders)]
     return pick(table, [have + [piece] for have, piece in zip(held, sent)])
 
 
 def matched(src0, tgt0):
+    tgt1 = hop(tgt0, ring)
+    tgt2 = hop(tgt0, back)
     src1 = hop(src0, flip_h)
-    tgt1 = hop(tgt0, ring)
     src2 = hop(src0, flip_c)
-    tgt2 = hop(tgt0, back)
     tgt1, src1, src2, tgt2 = lax.optimization_barrier((tgt1, src1, src2, tgt2))
     tgt3 = hop(tgt1, ring)
     src3 = hop(src1, flip_c)

time: 156 us -> 156 us (level)
  the two profiles are of different devices: /device:TPU:0 before, /device:TPU:97 now
where the time goes in v2:
time: 156 us; the launch traced here: 154 us
  starting transfers between devices  100 us (64%)
  waiting for transfers between devices  32.5 us (21%)
  Pallas kernels  18.3 us (12%)
  local copies, waits for them, and re-layouts  3.16 us (2%)
    ppermute x20, starting transfers between devices, hop(): return lax.ppermute(value, AXES, route)  100 us
    ppermute x20, waiting for transfers between devices, hop(): return lax.ppermute(value, AXES, route)  32.5 us
    pallas_call x1, Pallas kernels, match_early(): pl.pallas_call(functools.partial(early_kernel, nsrc=nsrc, ntgt=ntgt, cell...  9.06 us
    pallas_call x1, Pallas kernels, match_late(): pl.pallas_call(functools.partial(late_kernel, nsrc=nsrc, ntgt=ntgt, cells...  4.97 us
  transfers between devices with their start and end apart: 20, of which 13 were waited for; matrix products, arithmetic and copies ran while one was open for 1% of the time, Pallas kernels for 6%

profile of v2, /device:TPU:97, one launch (start us, length us, event | category | flops | bytes accessed | tf_op | source)
XLA Modules:
  0.0 154.4 jit_solution(4271390329606190659)
XLA Ops:
  0.0 1.0 slice.8.refs_2_.refs_0_
  1.0 2.6 %collective-permute-start = (bf16[3,352,128]{2,1,0:T(8,128)(2,1)S(1)}, bf16[3,352,128]{2,1,0:T(8,128)(2,1)S(1)}, u32[]{:S(2)}, u32[]{:S(2)}) collective-permute-start(bf16[3,352,128]{2,1,0:T(8,128)(2,1)S(1)} %slice.8.refs_2_.refs_0_), channel_id=1, source_target_pairs={{0,16},{1,97},{2,18},{3,99},{4,20},{5,101},{6,22},{7,103},{8,24},{... | collective-permute-start | bytes 811016 | tf_op jit(solution)/shard_map/ppermute | solution.py:34
  3.5 0.9 slice.9.refs_5_.refs_4_
  4.5 0.8 copy.13.table
  5.3 1.4 collective-permute-start.2
  6.7 1.3 collective-permute-start.3
  8.0 1.6 %collective-permute-done.2.refs_0_ = s32[3,2]{1,0:T(4,128)S(1)} collective-permute-done((s32[3,2]{1,0:T(4,128)S(1)}, s32[3,2]{1,0:T(4,128)S(1)}, u32[]{:S(2)}, u32[]{:S(2)}) %collective-permute-start.2) | collective-permute-done | bytes 56 | tf_op jit(solution)/shard_map/ppermute | solution.py:34
  9.7 1.2 collective-permute-start.4
  11.6 6.1 %collective-permute-done.5.refs_7_.refs_6_ = bf16[6,160,128]{2,1,0:T(8,128)(2,1)S(1)} collective-permute-done((bf16[6,160,128]{2,1,0:T(8,128)(2,1)S(1)}, bf16[6,160,128]{2,1,0:T(8,128)(2,1)S(1)}, u32[]{:S(2)}, u32[]{:S(2)}) %collective-permute-start.5) | collective-permute-done | bytes 245792 | tf_op jit(solution)/shard_map/ppermute | solution.py:34
  18.3 1.1 shard_map.46
  19.6 1.2 collective-permute-start.7
  20.8 3.9 %collective-permute-done.7.refs_7_ = bf16[6,160,128]{2,1,0:T(8,128)(2,1)S(1)} collective-permute-done((bf16[6,160,128]{2,1,0:T(8,128)(2,1)S(1)}, bf16[6,160,128]{2,1,0:T(8,128)(2,1)S(1)}, u32[]{:S(2)}, u32[]{:S(2)}) %collective-permute-start.7) | collective-permute-done | bytes 245792 | tf_op jit(solution)/shard_map/ppermute | solution.py:34
  24.7 3.4 %collective-permute-done.6.refs_3_ = bf16[6,352,128]{2,1,0:T(8,128)(2,1)S(1)} collective-permute-done((bf16[6,352,128]{2,1,0:T(8,128)(2,1)S(1)}, bf16[6,352,128]{2,1,0:T(8,128)(2,1)S(1)}, u32[]{:S(2)}, u32[]{:S(2)}) %collective-permute-start.6) | collective-permute-done | bytes 540704 | tf_op jit(solution)/shard_map/ppermute | solution.py:34
  28.0 1.1 shard_map.47
  29.1 5.5 %collective-permute-start.10 = (bf16[3,512,128]{2,1,0:T(8,128)(2,1)S(1)}, bf16[3,512,128]{2,1,0:T(8,128)(2,1)S(1)}, u32[]{:S(2)}, u32[]{:S(2)}) collective-permute-start(bf16[3,512,128]{2,1,0:T(8,128)(2,1)S(1)} %get-tuple-element.40.refs_0_), channel_id=1, source_target_pairs={{0,1},{1,0},{2,3},{3,2},{4,5},{5,4},{6,7},{7,6},{8,9},{9,8},{10,11... | collective-permute-start | bytes 1179656 | tf_op jit(solution)/shard_map/ppermute | solution.py:34
  34.7 1.5 collective-permute-start.8
  36.1 2.6 %collective-permute-start.9 = (bf16[3,512,128]{2,1,0:T(8,128)(2,1)S(1)}, bf16[3,512,128]{2,1,0:T(8,128)(2,1)S(1)}, u32[]{:S(2)}, u32[]{:S(2)}) collective-permute-start(bf16[3,512,128]{2,1,0:T(8,128)(2,1)S(1)} %get-tuple-element.40.refs_0_), channel_id=1, source_target_pairs={{0,8},{1,9},{2,10},{3,11},{4,12},{5,13},{6,14},{7,15},{8,0},{9,1},... | collective-permute-start | bytes 1179656 | tf_op jit(solution)/shard_map/ppermute | solution.py:34
  38.7 6.1 %collective-permute-done.11.refs_6_ = bf16[3,512,128]{2,1,0:T(8,128)(2,1)S(1)} collective-permute-done((bf16[3,512,128]{2,1,0:T(8,128)(2,1)S(1)}, bf16[3,512,128]{2,1,0:T(8,128)(2,1)S(1)}, u32[]{:S(2)}, u32[]{:S(2)}) %collective-permute-start.11) | collective-permute-done | bytes 393248 | tf_op jit(solution)/shard_map/ppermute | solution.py:34
  44.8 1.6 %collective-permute-done.8.refs_5_ = bf16[3,512,128]{2,1,0:T(8,128)(2,1)S(1)} collective-permute-done((bf16[3,512,128]{2,1,0:T(8,128)(2,1)S(1)}, bf16[3,512,128]{2,1,0:T(8,128)(2,1)S(1)}, u32[]{:S(2)}, u32[]{:S(2)}) %collective-permute-start.8) | collective-permute-done | bytes 393248 | tf_op jit(solution)/shard_map/ppermute | solution.py:34
  46.5 2.7 %collective-permute-start.12 = (bf16[3,512,128]{2,1,0:T(8,128)(2,1)S(1)}, bf16[3,512,128]{2,1,0:T(8,128)(2,1)S(1)}, u32[]{:S(2)}, u32[]{:S(2)}) collective-permute-start(bf16[3,512,128]{2,1,0:T(8,128)(2,1)S(1)} %collective-permute-done.9.refs_1_), channel_id=1, source_target_pairs={{0,1},{1,0},{2,3},{3,2},{4,5},{5,4},{6,7},{7,6},{8,9},{9,8},{10,11... | collective-permute-start | bytes 1179656 | tf_op jit(solution)/shard_map/ppermute | solution.py:34
  49.3 1.2 collective-permute-done.12.refs_3_
  50.5 9.1 %shard_map.48 = (f32[3,2048,128]{2,1,0:T(8,128)S(1)}, f32[3,2048,128]{2,1,0:T(8,128)S(1)}, f32[3,3,8,512]{3,2,1,0:T(8,128)S(1)}, f32[3,3,8,512]{3,2,1,0:T(8,128)S(1)}, f32[3,3,8,512]{3,2,1,0:T(8,128)S(1)}) custom-call(bf16[3,512,128]{2,1,0:T(8,128)(2,1)S(1)} %get-tuple-element.40.refs_0_, bf16[3,512,128]{2,1,0:T(8,128)(2,1)S(1)} %collective-permute-done.9.refs_1_, ...), custom_call_target="tpu_custom_call" | custom-call | flops 4824000000 | bytes 3600000 | tf_op jit(solution)/shard_map/pallas_call | solution.py:420
  59.6 5.0 %shard_map.49 = (f32[2,3,16,128]{3,2,1,0:T(8,128)S(1)}, f32[2,3,16,128]{3,2,1,0:T(8,128)S(1)}, f32[2,3,16,128]{3,2,1,0:T(8,128)S(1)}, f32[2,3,16,128]{3,2,1,0:T(8,128)S(1)}) custom-call(bf16[3,512,128]{2,1,0:T(8,128)(2,1)S(1)} %get-tuple-element.40.refs_0_, bf16[3,512,128]{2,1,0:T(8,128)(2,1)S(1)} %collective-permute-done.9.refs_1_, ...), custom_call_target="tpu_custom_call" | custom-call | flops 1608000000 | bytes 1200000 | tf_op jit(solution)/shard_map/pallas_call | solution.py:436
  64.6 69.5 %collective-permute-start.14 = (f32[2,3,16,128]{3,2,1,0:T(8,128)S(1)}, f32[2,3,16,128]{3,2,1,0:T(8,128)S(1)}, u32[]{:S(2)}, u32[]{:S(2)}) collective-permute-start(f32[2,3,16,128]{3,2,1,0:T(8,128)S(1)} %get-tuple-element.52), channel_id=1, source_target_pairs={{0,1},{1,0},{2,3},{3,2},{4,5},{5,4},{6,7},{7,6},{8,9},{9,8},{10,11... | collective-permute-start | bytes 147464 | tf_op jit(solution)/shard_map/ppermute | solution.py:34
  134.2 0.8 collective-permute-done.14.fwd_in
  134.9 2.1 %collective-permute-done.15.rev_in = f32[2,3,16,128]{3,2,1,0:T(8,128)S(1)} collective-permute-done((f32[2,3,16,128]{3,2,1,0:T(8,128)S(1)}, f32[2,3,16,128]{3,2,1,0:T(8,128)S(1)}, u32[]{:S(2)}, u32[]{:S(2)}) %collective-permute-start.15) | collective-permute-done | bytes 49184 | tf_op jit(solution)/shard_map/ppermute | solution.py:34
  137.0 2.7 %collective-permute-start.16 = (f32[3,16,128]{2,1,0:T(8,128)S(1)}, f32[3,16,128]{2,1,0:T(8,128)S(1)}, u32[]{:S(2)}, u32[]{:S(2)}) collective-permute-start(f32[3,16,128]{2,1,0:T(8,128)S(1)} %get-tuple-element.56), channel_id=1, source_target_pairs={{0,8},{1,9},{2,10},{3,11},{4,12},{5,13},{6,14},{7,15},{8,0},{9,1},... | collective-permute-start | bytes 73736 | tf_op jit(solution)/shard_map/ppermute | solution.py:34
  139.7 1.2 collective-permute-start.17
  141.3 2.3 %collective-permute-done.17.rev_in = f32[3,16,128]{2,1,0:T(8,128)S(1)} collective-permute-done((f32[3,16,128]{2,1,0:T(8,128)S(1)}, f32[3,16,128]{2,1,0:T(8,128)S(1)}, u32[]{:S(2)}, u32[]{:S(2)}) %collective-permute-start.17) | collective-permute-done | bytes 24608 | tf_op jit(solution)/shard_map/ppermute | solution.py:34
  143.6 5.7 %collective-permute-start.18 = (f32[3,2,2,4,128]{4,3,2,1,0:T(4,128)S(1)}, f32[3,2,2,4,128]{4,3,2,1,0:T(4,128)S(1)}, u32[]{:S(2)}, u32[]{:S(2)}) collective-permute-start(f32[3,2,2,4,128]{4,3,2,1,0:T(4,128)S(1)} %shard_map.51.own), channel_id=1, source_target_pairs={{0,0},{1,2},{2,1},{3,4},{4,3},{5,6},{6,5},{7,8},{8,7},{9,10},{10,9... | collective-permute-start | bytes 73736 | tf_op jit(solution)/shard_map/ppermute | solution.py:34
  150.0 2.4 %collective-permute-done.18.chip = f32[3,2,2,4,128]{4,3,2,1,0:T(4,128)S(1)} collective-permute-done((f32[3,2,2,4,128]{4,3,2,1,0:T(4,128)S(1)}, f32[3,2,2,4,128]{4,3,2,1,0:T(4,128)S(1)}, u32[]{:S(2)}, u32[]{:S(2)}) %collective-permute-start.18) | collective-permute-done | bytes 24608 | tf_op jit(solution)/shard_map/ppermute | solution.py:34
  152.4 2.0 %shard_map.52 = f32[3,2,2,4,128]{4,3,2,1,0:T(4,128)} custom-call(f32[144]{0:T(256)S(1)} %reshape.9.weight, f32[8]{0:T(128)S(1)} %reshape.10.bias, f32[3,2,2,4,128]{4,3,2,1,0:T(4,128)S(1)} %collective-permute-done.18.chip, f32[3,2,2,4,128]{4,3,2,1,0:T(4,128)S(1)} %shard_map.51.own, f32[3,2,2,4,128]{4,3,2,1,0:T(4,128)S(1)} %collective-permute-done.19.core), custom_call_target="tpu_custom_call" | custom-call | tf_op jit(solution)/shard_map/pallas_call | solution.py:554
  (28 shorter events, 2.8 us)
Async XLA Ops:
  1.0 8.7 %collective-permute-start = (bf16[3,352,128]{2,1,0:T(8,128)(2,1)S(1)}, bf16[3,352,128]{2,1,0:T(8,128)(2,1)S(1)}, u32[]{:S(2)}, u32[]{:S(2)}) collective-permute-start(bf16[3,352,128]{2,1,0:T(8,128)(2,1)S(1)} %slice.8.refs_2_.refs_0_), channel_id=1, source_target_pairs={{0,16},{1,97},{2,18},{3,99},{4,20},{5,101},{6,22},{7,103},{8,24},{... | collective-permute-start | bytes 811016 | tf_op jit(solution)/shard_map/ppermute | solution.py:34
  4.4 5.2 %collective-permute-start.1 = (bf16[3,160,128]{2,1,0:T(8,128)(2,1)S(1)}, bf16[3,160,128]{2,1,0:T(8,128)(2,1)S(1)}, u32[]{:S(2)}, u32[]{:S(2)}) collective-permute-start(bf16[3,160,128]{2,1,0:T(8,128)(2,1)S(1)} %slice.9.refs_5_.refs_4_), channel_id=1, source_target_pairs={{0,32},{1,33},{2,34},{3,35},{4,36},{5,37},{6,38},{7,39},{8,40},{9,... | collective-permute-start | bytes 368648 | tf_op jit(solution)/shard_map/ppermute | solution.py:34
  5.3 4.4 %collective-permute-start.2 = (s32[3,2]{1,0:T(4,128)S(1)}, s32[3,2]{1,0:T(4,128)S(1)}, u32[]{:S(2)}, u32[]{:S(2)}) collective-permute-start(s32[3,2]{1,0:T(4,128)S(1)} %copy.13.table), channel_id=1, source_target_pairs={{0,96},{1,33},{2,98},{3,35},{4,100},{5,37},{6,102},{7,39},{8,104},... | collective-permute-start | bytes 80 | tf_op jit(solution)/shard_map/ppermute | solution.py:34
  6.7 2.9 %collective-permute-start.3 = (s32[3,2]{1,0:T(4,128)S(1)}, s32[3,2]{1,0:T(4,128)S(1)}, u32[]{:S(2)}, u32[]{:S(2)}) collective-permute-start(s32[3,2]{1,0:T(4,128)S(1)} %copy.13.table), channel_id=1, source_target_pairs={{0,16},{1,17},{2,18},{3,19},{4,20},{5,21},{6,22},{7,23},{8,24},{9,... | collective-permute-start | bytes 80 | tf_op jit(solution)/shard_map/ppermute | solution.py:34
  9.7 8.6 %collective-permute-start.4 = (bf16[6,352,128]{2,1,0:T(8,128)(2,1)S(1)}, bf16[6,352,128]{2,1,0:T(8,128)(2,1)S(1)}, u32[]{:S(2)}, u32[]{:S(2)}) collective-permute-start(bf16[6,352,128]{2,1,0:T(8,128)(2,1)S(1)} %pad_maximum_fusion), channel_id=1, source_target_pairs={{0,32},{1,17},{2,34},{3,19},{4,36},{5,21},{6,38},{7,23},{8,40},{9,... | collective-permute-start | bytes 1622024 | tf_op jit(solution)/shard_map/ppermute | solution.py:34
  10.9 6.8 %collective-permute-start.5 = (bf16[6,160,128]{2,1,0:T(8,128)(2,1)S(1)}, bf16[6,160,128]{2,1,0:T(8,128)(2,1)S(1)}, u32[]{:S(2)}, u32[]{:S(2)}) collective-permute-start(bf16[6,160,128]{2,1,0:T(8,128)(2,1)S(1)} %pad_maximum_fusion.1), channel_id=1, source_target_pairs={{0,96},{1,97},{2,98},{3,99},{4,100},{5,101},{6,102},{7,103},{8,104... | collective-permute-start | bytes 737288 | tf_op jit(solution)/shard_map/ppermute | solution.py:34
  19.5 8.6 %collective-permute-start.6 = (bf16[6,352,128]{2,1,0:T(8,128)(2,1)S(1)}, bf16[6,352,128]{2,1,0:T(8,128)(2,1)S(1)}, u32[]{:S(2)}, u32[]{:S(2)}) collective-permute-start(bf16[6,352,128]{2,1,0:T(8,128)(2,1)S(1)} %get-tuple-element.38), channel_id=1, source_target_pairs={{0,96},{1,33},{2,98},{3,35},{4,100},{5,37},{6,102},{7,39},{8,104},... | collective-permute-start | bytes 1622024 | tf_op jit(solution)/shard_map/ppermute | solution.py:34
  19.6 5.1 %collective-permute-start.7 = (bf16[6,160,128]{2,1,0:T(8,128)(2,1)S(1)}, bf16[6,160,128]{2,1,0:T(8,128)(2,1)S(1)}, u32[]{:S(2)}, u32[]{:S(2)}) collective-permute-start(bf16[6,160,128]{2,1,0:T(8,128)(2,1)S(1)} %get-tuple-element.39), channel_id=1, source_target_pairs={{0,16},{1,17},{2,18},{3,19},{4,20},{5,21},{6,22},{7,23},{8,24},{9,... | collective-permute-start | bytes 737288 | tf_op jit(solution)/shard_map/ppermute | solution.py:34
  29.1 9.6 %collective-permute-start.10 = (bf16[3,512,128]{2,1,0:T(8,128)(2,1)S(1)}, bf16[3,512,128]{2,1,0:T(8,128)(2,1)S(1)}, u32[]{:S(2)}, u32[]{:S(2)}) collective-permute-start(bf16[3,512,128]{2,1,0:T(8,128)(2,1)S(1)} %get-tuple-element.40.refs_0_), channel_id=1, source_target_pairs={{0,1},{1,0},{2,3},{3,2},{4,5},{5,4},{6,7},{7,6},{8,9},{9,8},{10,11... | collective-permute-start | bytes 1179656 | tf_op jit(solution)/shard_map/ppermute | solution.py:34
  34.6 10.2 %collective-permute-start.11 = (bf16[3,512,128]{2,1,0:T(8,128)(2,1)S(1)}, bf16[3,512,128]{2,1,0:T(8,128)(2,1)S(1)}, u32[]{:S(2)}, u32[]{:S(2)}) collective-permute-start(bf16[3,512,128]{2,1,0:T(8,128)(2,1)S(1)} %get-tuple-element.41.refs_4_), channel_id=1, source_target_pairs={{0,6},{1,3},{2,0},{3,5},{4,2},{5,7},{6,4},{7,1},{8,14},{9,11},{10,... | collective-permute-start | bytes 1179656 | tf_op jit(solution)/shard_map/ppermute | solution.py:34
  34.7 11.8 %collective-permute-start.8 = (bf16[3,512,128]{2,1,0:T(8,128)(2,1)S(1)}, bf16[3,512,128]{2,1,0:T(8,128)(2,1)S(1)}, u32[]{:S(2)}, u32[]{:S(2)}) collective-permute-start(bf16[3,512,128]{2,1,0:T(8,128)(2,1)S(1)} %get-tuple-element.41.refs_4_), channel_id=1, source_target_pairs={{0,2},{1,7},{2,4},{3,1},{4,6},{5,3},{6,0},{7,5},{8,10},{9,15},{10,... | collective-permute-start | bytes 1179656 | tf_op jit(solution)/shard_map/ppermute | solution.py:34
  36.1 10.3 %collective-permute-start.9 = (bf16[3,512,128]{2,1,0:T(8,128)(2,1)S(1)}, bf16[3,512,128]{2,1,0:T(8,128)(2,1)S(1)}, u32[]{:S(2)}, u32[]{:S(2)}) collective-permute-start(bf16[3,512,128]{2,1,0:T(8,128)(2,1)S(1)} %get-tuple-element.40.refs_0_), channel_id=1, source_target_pairs={{0,8},{1,9},{2,10},{3,11},{4,12},{5,13},{6,14},{7,15},{8,0},{9,1},... | collective-permute-start | bytes 1179656 | tf_op jit(solution)/shard_map/ppermute | solution.py:34
  46.5 4.0 %collective-permute-start.12 = (bf16[3,512,128]{2,1,0:T(8,128)(2,1)S(1)}, bf16[3,512,128]{2,1,0:T(8,128)(2,1)S(1)}, u32[]{:S(2)}, u32[]{:S(2)}) collective-permute-start(bf16[3,512,128]{2,1,0:T(8,128)(2,1)S(1)} %collective-permute-done.9.refs_1_), channel_id=1, source_target_pairs={{0,1},{1,0},{2,3},{3,2},{4,5},{5,4},{6,7},{7,6},{8,9},{9,8},{10,11... | collective-permute-start | bytes 1179656 | tf_op jit(solution)/shard_map/ppermute | solution.py:34
  49.2 10.4 %collective-permute-start.13 = (bf16[3,512,128]{2,1,0:T(8,128)(2,1)S(1)}, bf16[3,512,128]{2,1,0:T(8,128)(2,1)S(1)}, u32[]{:S(2)}, u32[]{:S(2)}) collective-permute-start(bf16[3,512,128]{2,1,0:T(8,128)(2,1)S(1)} %collective-permute-done.8.refs_5_), channel_id=1, source_target_pairs={{0,2},{1,7},{2,4},{3,1},{4,6},{5,3},{6,0},{7,5},{8,10},{9,15},{10,... | collective-permute-start | bytes 1179656 | tf_op jit(solution)/shard_map/ppermute | solution.py:34
  59.6 89.9 %copy-start = (f32[4,2,2,3,3]{0,2,4,3,1:T(2,128)S(1)}, f32[4,2,2,3,3]{0,2,4,3,1:T(2,128)}, u32[]{:S(2)}) copy-start(f32[4,2,2,3,3]{0,2,4,3,1:T(2,128)} %param.6) | copy-start | bytes 1732
  59.6 90.2 %copy-start.1 = (f32[4,2]{0,1:T(2,128)S(1)}, f32[4,2]{0,1:T(2,128)}, u32[]{:S(2)}) copy-start(f32[4,2]{0,1:T(2,128)} %param.7) | copy-start | bytes 100
  64.6 70.3 %collective-permute-start.14 = (f32[2,3,16,128]{3,2,1,0:T(8,128)S(1)}, f32[2,3,16,128]{3,2,1,0:T(8,128)S(1)}, u32[]{:S(2)}, u32[]{:S(2)}) collective-permute-start(f32[2,3,16,128]{3,2,1,0:T(8,128)S(1)} %get-tuple-element.52), channel_id=1, source_target_pairs={{0,1},{1,0},{2,3},{3,2},{4,5},{5,4},{6,7},{7,6},{8,9},{9,8},{10,11... | collective-permute-start | bytes 147464 | tf_op jit(solution)/shard_map/ppermute | solution.py:34
  134.0 2.9 %collective-permute-start.15 = (f32[2,3,16,128]{3,2,1,0:T(8,128)S(1)}, f32[2,3,16,128]{3,2,1,0:T(8,128)S(1)}, u32[]{:S(2)}, u32[]{:S(2)}) collective-permute-start(f32[2,3,16,128]{3,2,1,0:T(8,128)S(1)} %get-tuple-element.54), channel_id=1, source_target_pairs={{0,2},{1,3},{2,0},{3,1},{4,6},{5,7},{6,4},{7,5},{8,10},{9,11},{10,... | collective-permute-start | bytes 147464 | tf_op jit(solution)/shard_map/ppermute | solution.py:34
  137.0 4.3 %collective-permute-start.16 = (f32[3,16,128]{2,1,0:T(8,128)S(1)}, f32[3,16,128]{2,1,0:T(8,128)S(1)}, u32[]{:S(2)}, u32[]{:S(2)}) collective-permute-start(f32[3,16,128]{2,1,0:T(8,128)S(1)} %get-tuple-element.56), channel_id=1, source_target_pairs={{0,8},{1,9},{2,10},{3,11},{4,12},{5,13},{6,14},{7,15},{8,0},{9,1},... | collective-permute-start | bytes 73736 | tf_op jit(solution)/shard_map/ppermute | solution.py:34
  139.7 3.9 %collective-permute-start.17 = (f32[3,16,128]{2,1,0:T(8,128)S(1)}, f32[3,16,128]{2,1,0:T(8,128)S(1)}, u32[]{:S(2)}, u32[]{:S(2)}) collective-permute-start(f32[3,16,128]{2,1,0:T(8,128)S(1)} %get-tuple-element.58), channel_id=1, source_target_pairs={{0,6},{1,7},{2,4},{3,5},{4,2},{5,3},{6,0},{7,1},{8,14},{9,15},{10,... | collective-permute-start | bytes 73736 | tf_op jit(solution)/shard_map/ppermute | solution.py:34
  143.6 8.8 %collective-permute-start.18 = (f32[3,2,2,4,128]{4,3,2,1,0:T(4,128)S(1)}, f32[3,2,2,4,128]{4,3,2,1,0:T(4,128)S(1)}, u32[]{:S(2)}, u32[]{:S(2)}) collective-permute-start(f32[3,2,2,4,128]{4,3,2,1,0:T(4,128)S(1)} %shard_map.51.own), channel_id=1, source_target_pairs={{0,0},{1,2},{2,1},{3,4},{4,3},{5,6},{6,5},{7,8},{8,7},{9,10},{10,9... | collective-permute-start | bytes 73736 | tf_op jit(solution)/shard_map/ppermute | solution.py:34
  149.4 3.0 %collective-permute-start.19 = (f32[3,2,2,4,128]{4,3,2,1,0:T(4,128)S(1)}, f32[3,2,2,4,128]{4,3,2,1,0:T(4,128)S(1)}, u32[]{:S(2)}, u32[]{:S(2)}) collective-permute-start(f32[3,2,2,4,128]{4,3,2,1,0:T(4,128)S(1)} %shard_map.51.own), channel_id=1, source_target_pairs={{0,1},{1,0},{2,3},{3,2},{4,5},{5,4},{6,7},{7,6},{8,9},{9,8},{10,11... | collective-permute-start | bytes 73736 | tf_op jit(solution)/shard_map/ppermute | solution.py:34

commit v3 on v2

--- a/solution.py
+++ b/solution.py
@@ -234,10 +234,16 @@
             put(slice(c * width, (c + 1) * width), i == 0 and cols_first, (tt[c], xx[c], src_rows[i] * tt[c] - uu[c]))
 
 
-def early_kernel(*refs, nsrc, ntgt, cells, width):
-    src, tgt = refs[:nsrc], refs[nsrc : nsrc + ntgt]
-    acc, accy, g0, gq, gy, rhs = refs[nsrc + ntgt :]
+def early_kernel(*refs, which, ntgt, cells, width, ready):
+    nsrc = len(which)
+    src, refs = refs[:nsrc], refs[nsrc:]
+    if ready:
+        rhs, acc, accy, g0, gq, gy = refs
+    else:
+        tgt, refs = refs[:ntgt], refs[ntgt:]
+        acc, accy, g0, gq, gy, rhs = refs
     src_rows, tgt_rows, _ = places(cells, width)
+    src_rows = [src_rows[i] for i in which]
     scale = score_gain / math.sqrt(src[0].shape[-1]) * math.log2(math.e)
 
     def one(p, jb, first):
@@ -249,15 +255,14 @@
             for ref, value in zip((g0, gq, gy), values):
                 ref[p, jb, :, lanes] = value if new else ref[p, jb, :, lanes] + value
 
-        b = rhs[jb * cells : (jb + 1) * cells, :]
+        b = rhs[p, jb * cells : (jb + 1) * cells, :]
         block([ref[p] for ref in src], b, tgt_rows[jb], src_rows, sums, (put, True), cells, width)
 
     def pair(p, carry):
-        targets(tgt, p, scale, rhs, 0, cells)
-        one(p, 0, True)
-
-        for jb in range(1, ntgt):
-            one(p, jb, False)
+        if not ready:
+            targets(tgt, p, scale, rhs.at[p], 0, cells)
+        for jb in range(ntgt):
+            one(p, jb, jb == 0)
         return carry
 
     lax.fori_loop(0, src[0].shape[0], pair, 0)
@@ -265,14 +270,13 @@
 
 def late_kernel(*refs, nsrc, ntgt, cells, width):
     src, tgt = refs[:nsrc], refs[nsrc : nsrc + ntgt]
-    acc_in, accy_in, g0_in, gq_in, gy_in, fwd_keep, fwd_send, rev_keep, rev_send, rev, rhs, acc, accy, g0, gq, gy, shift_r, shift_c = refs[
-        nsrc + ntgt :
-    ]
+    before = (refs[nsrc + ntgt : nsrc + ntgt + 5], refs[nsrc + ntgt + 5 : nsrc + ntgt + 10])
+    fwd_keep, fwd_send, rev_keep, rev_send, rev, rhs, acc, accy, g0, gq, gy, shift_r, shift_c = refs[nsrc + ntgt + 10 :]
     fwd = [(fwd_keep, 0), (fwd_keep, 1), (fwd_send, 0), (fwd_send, 1)]
     band_rows = cells // width
     src_rows, tgt_rows, tgt_slot = places(cells, width)
     scale = score_gain / math.sqrt(src[0].shape[-1]) * math.log2(math.e)
-    early = g0_in.shape[1]
+    early = before[0][2].shape[1]
     lane = lax.broadcasted_iota(jnp.int32, (16, width), 1)
     row16 = lax.broadcasted_iota(jnp.int32, (16, width), 0)
     ramp = (2 * lane - (width - 1)).astype(jnp.float32)
@@ -335,8 +339,11 @@
         for jb in range(early, ntgt):
 
             def sums(rows, total, rowed):
-                acc[rows, :] = (acc_in[p, rows, :] if jb == early else acc[rows, :]) + total
-                accy[rows, :] = (accy_in[p, rows, :] if jb == early else accy[rows, :]) + rowed
+                i, r0 = divmod(rows.start, cells)
+                r0 += i // 2 * cells
+                old = before[i % 2]
+                acc[rows, :] = (old[0][p, r0 : r0 + 8, :] if jb == early else acc[rows, :]) + total
+                accy[rows, :] = (old[1][p, r0 : r0 + 8, :] if jb == early else accy[rows, :]) + rowed
 
             b = rhs[jb * cells : (jb + 1) * cells, :]
             block(sources, b, tgt_rows[jb], src_rows, sums, (put(jb), True), cells, width)
@@ -344,7 +351,7 @@
         def cols_of(j, cs):
             if j >= early:
                 return g0[j, :, cs], gq[j, :, cs], gy[j, :, cs]
-            return g0_in[p, j, :, cs], gq_in[p, j, :, cs], gy_in[p, j, :, cs]
+            return [before[0][n][p, j, :, cs] + before[1][n][p, j, :, cs] for n in (2, 3, 4)]
 
         ok = emit(p, cols_of, False)
 
@@ -411,21 +418,25 @@
     )
 
 
-def match_early(src, tgt):
+def match_early(src, which, tgt=None, scaled=None):
     pairs, cells, chans = src[0].shape
     width = 128
-    nsrc, ntgt = len(src), len(tgt)
+    nsrc = len(src)
+    ntgt = len(tgt) if tgt else scaled.shape[1] // cells
     rows = jax.ShapeDtypeStruct((pairs, nsrc * cells, width), jnp.float32)
     cols = jax.ShapeDtypeStruct((pairs, ntgt, 8, cells), jnp.float32)
+    shapes = [rows, rows, cols, cols, cols]
+    if tgt:
+        shapes.append(jax.ShapeDtypeStruct((pairs, ntgt * cells, 2 * chans), jnp.bfloat16))
+    operands = (*src, *tgt) if tgt else (*src, scaled)
     return pl.pallas_call(
-        functools.partial(early_kernel, nsrc=nsrc, ntgt=ntgt, cells=cells, width=width),
-        out_shape=[rows, rows, cols, cols, cols],
-        in_specs=[VMEM] * (nsrc + ntgt),
-        out_specs=[VMEM] * 5,
-        scratch_shapes=[pltpu.VMEM((ntgt * cells, 2 * chans), jnp.bfloat16)],
-        compiler_params=pltpu.CompilerParams(vmem_limit_bytes=16 << 20),
+        functools.partial(early_kernel, which=which, ntgt=ntgt, cells=cells, width=width, ready=not tgt),
+        out_shape=shapes,
+        in_specs=[VMEM] * len(operands),
+        out_specs=[VMEM] * len(shapes),
+        compiler_params=pltpu.CompilerParams(vmem_limit_bytes=14 << 20),
         cost_estimate=cost(pairs, nsrc * ntgt),
-    )(*src, *tgt)
+    )(*operands)
 
 
 def match_late(src, tgt, early):
@@ -436,7 +447,7 @@
     return pl.pallas_call(
         functools.partial(late_kernel, nsrc=nsrc, ntgt=ntgt, cells=cells, width=width),
         out_shape=[stats] * 4,
-        in_specs=[VMEM] * (nsrc + ntgt + 5),
+        in_specs=[VMEM] * (nsrc + ntgt + 10),
         out_specs=[VMEM] * 4,
         scratch_shapes=[
             pltpu.VMEM((4,) + stats.shape[1:], jnp.float32),
@@ -566,12 +577,12 @@
         (by_core(flip_y, flip_b), by_core(flip_a, flip_y), by_core(flip_b, flip_a)),
         (flip_a, flip_b, flip_y),
     )
-    first = [hop(block, order[0]) for block, order in zip(blocks, orders)]
-    tables = [hop(table, order[2]) for order in orders]
-    first, tables = lax.optimization_barrier((first, tables))
+    first = lax.optimization_barrier([hop(block, order[0]) for block, order in zip(blocks, orders)])
     held = [[block, piece] for block, piece in zip(blocks, first)]
     send = [jnp.concatenate(have, axis=0) for have in held]
-    second = lax.optimization_barrier([hop(part, order[1]) for part, order in zip(send, orders)])
+    second = [hop(part, order[1]) for part, order in zip(send, orders)]
+    tables = [hop(table, order[2]) for order in orders]
+    second, tables = lax.optimization_barrier((second, tables))
     held = [have + [piece] for have, piece in zip(held, second)]
     sent = [hop(part, order[2]) for part, order in zip(offer(tables, held), orders)]
     return pick(table, [have + [piece] for have, piece in zip(held, sent)])
@@ -582,12 +593,12 @@
     tgt2 = hop(tgt0, back)
     src1 = hop(src0, flip_h)
     src2 = hop(src0, flip_c)
-    tgt1, src1, src2, tgt2 = lax.optimization_barrier((tgt1, src1, src2, tgt2))
+    tgt1, tgt2, src2 = lax.optimization_barrier((tgt1, tgt2, src2))
     tgt3 = hop(tgt1, ring)
+    *own, scaled = match_early((src0, src2), (0, 2), tgt=(tgt0, tgt1, tgt2))
     src3 = hop(src1, flip_c)
-    src = (src0, src1, src2, src3)
-    early = match_early(src, (tgt0, tgt1, tgt2))
-    return match_late(src, (tgt0, tgt1, tgt2, tgt3), early)
+    other = match_early((src1, src3), (1, 3), scaled=scaled)
+    return match_late((src0, src1, src2, src3), (tgt0, tgt1, tgt2, tgt3), (*own, *other))
 
 
 def shards(features, frame_pairs, conv_weight, conv_bias):

time: 156 us -> 154 us (0.987)
  starting transfers between devices: 100 us -> 95.3 us
  waiting for transfers between devices: 32.5 us -> 34.8 us
    ppermute x20, starting transfers between devices: 100 us -> 95.3 us  [hop(): return lax.ppermute(value, AXES, route)]
    ppermute x20, waiting for transfers between devices: 32.5 us -> 34.8 us  [hop(): return lax.ppermute(value, AXES, route)]
    pallas_call x1 -> x2, Pallas kernels: 9.06 us -> 9.68 us  [match_early(): pl.pallas_call(functools.partial(early_kernel, which=which, ntgt=ntgt, ce...]
  transfers between devices with their start and end apart: 20 -> 20, of which waited for: 13 -> 10; matrix products, arithmetic and copies ran while one was open for 1% -> 1% of each run, Pallas kernels for 6% -> 6%
where the time goes in v3:
time: 154 us; the launch traced here: 152 us
  starting transfers between devices  95.3 us (62%)
  waiting for transfers between devices  34.8 us (23%)
  Pallas kernels  18.9 us (12%)
  local copies, waits for them, and re-layouts  2.5 us (2%)
    ppermute x20, starting transfers between devices, hop(): return lax.ppermute(value, AXES, route)  95.3 us
    ppermute x20, waiting for transfers between devices, hop(): return lax.ppermute(value, AXES, route)  34.8 us
    pallas_call x2, Pallas kernels, match_early(): pl.pallas_call(functools.partial(early_kernel, which=which, ntgt=ntgt, ce...  9.68 us
    pallas_call x1, Pallas kernels, match_late(): pl.pallas_call(functools.partial(late_kernel, nsrc=nsrc, ntgt=ntgt, cells...  4.96 us
  transfers between devices with their start and end apart: 20, of which 10 were waited for; matrix products, arithmetic and copies ran while one was open for 1% of the time, Pallas kernels for 6%

profile of v3, /device:TPU:97, one launch (start us, length us, event | category | flops | bytes accessed | tf_op | source)
XLA Modules:
  0.0 151.8 jit_solution(3126362246552005513)
XLA Ops:
  0.0 1.0 slice.8.refs_2_.refs_0_
  1.0 2.6 %collective-permute-start = (bf16[3,352,128]{2,1,0:T(8,128)(2,1)S(1)}, bf16[3,352,128]{2,1,0:T(8,128)(2,1)S(1)}, u32[]{:S(2)}, u32[]{:S(2)}) collective-permute-start(bf16[3,352,128]{2,1,0:T(8,128)(2,1)S(1)} %slice.8.refs_2_.refs_0_), channel_id=1, source_target_pairs={{0,16},{1,97},{2,18},{3,99},{4,20},{5,101},{6,22},{7,103},{8,24},{... | collective-permute-start | bytes 811016 | tf_op jit(solution)/shard_map/ppermute | solution.py:34
  3.5 0.9 slice.9.refs_5_.refs_4_
  4.5 5.1 %collective-permute-done.1.refs_6_.refs_5_ = bf16[3,160,128]{2,1,0:T(8,128)(2,1)S(1)} collective-permute-done((bf16[3,160,128]{2,1,0:T(8,128)(2,1)S(1)}, bf16[3,160,128]{2,1,0:T(8,128)(2,1)S(1)}, u32[]{:S(2)}, u32[]{:S(2)}) %collective-permute-start.1) | collective-permute-done | bytes 122912 | tf_op jit(solution)/shard_map/ppermute | solution.py:34
  9.7 0.4 collective-permute-start.2
  10.1 1.5 collective-permute-start.3
  11.7 0.2 collective-permute-start.5
  12.0 2.5 %collective-permute-done.4.refs_0_ = s32[3,2]{1,0:T(4,128)S(1)} collective-permute-done((s32[3,2]{1,0:T(4,128)S(1)}, s32[3,2]{1,0:T(4,128)S(1)}, u32[]{:S(2)}, u32[]{:S(2)}) %collective-permute-start.4) | collective-permute-done | bytes 56 | tf_op jit(solution)/shard_map/ppermute | solution.py:34
  14.4 3.9 %collective-permute-done.5.refs_1_ = s32[3,2]{1,0:T(4,128)S(1)} collective-permute-done((s32[3,2]{1,0:T(4,128)S(1)}, s32[3,2]{1,0:T(4,128)S(1)}, u32[]{:S(2)}, u32[]{:S(2)}) %collective-permute-start.5) | collective-permute-done | bytes 56 | tf_op jit(solution)/shard_map/ppermute | solution.py:34
  18.3 1.1 shard_map.46
  19.6 1.2 collective-permute-start.7
  20.8 3.9 %collective-permute-done.7.refs_7_ = bf16[6,160,128]{2,1,0:T(8,128)(2,1)S(1)} collective-permute-done((bf16[6,160,128]{2,1,0:T(8,128)(2,1)S(1)}, bf16[6,160,128]{2,1,0:T(8,128)(2,1)S(1)}, u32[]{:S(2)}, u32[]{:S(2)}) %collective-permute-start.7) | collective-permute-done | bytes 245792 | tf_op jit(solution)/shard_map/ppermute | solution.py:34
  24.7 3.4 %collective-permute-done.6.refs_3_ = bf16[6,352,128]{2,1,0:T(8,128)(2,1)S(1)} collective-permute-done((bf16[6,352,128]{2,1,0:T(8,128)(2,1)S(1)}, bf16[6,352,128]{2,1,0:T(8,128)(2,1)S(1)}, u32[]{:S(2)}, u32[]{:S(2)}) %collective-permute-start.6) | collective-permute-done | bytes 540704 | tf_op jit(solution)/shard_map/ppermute | solution.py:34
  28.0 1.1 shard_map.47
  29.1 3.1 %collective-permute-start.8 = (bf16[3,512,128]{2,1,0:T(8,128)(2,1)S(1)}, bf16[3,512,128]{2,1,0:T(8,128)(2,1)S(1)}, u32[]{:S(2)}, u32[]{:S(2)}) collective-permute-start(bf16[3,512,128]{2,1,0:T(8,128)(2,1)S(1)} %get-tuple-element.45.refs_0_), channel_id=1, source_target_pairs={{0,8},{1,9},{2,10},{3,11},{4,12},{5,13},{6,14},{7,15},{8,0},{9,1},... | collective-permute-start | bytes 1179656 | tf_op jit(solution)/shard_map/ppermute | solution.py:34
  32.2 4.1 %collective-permute-start.11 = (bf16[3,512,128]{2,1,0:T(8,128)(2,1)S(1)}, bf16[3,512,128]{2,1,0:T(8,128)(2,1)S(1)}, u32[]{:S(2)}, u32[]{:S(2)}) collective-permute-start(bf16[3,512,128]{2,1,0:T(8,128)(2,1)S(1)} %get-tuple-element.45.refs_0_), channel_id=1, source_target_pairs={{0,1},{1,0},{2,3},{3,2},{4,5},{5,4},{6,7},{7,6},{8,9},{9,8},{10,11... | collective-permute-start | bytes 1179656 | tf_op jit(solution)/shard_map/ppermute | solution.py:34
  36.4 1.6 %collective-permute-done.8.refs_0_.refs_1_ = bf16[3,512,128]{2,1,0:T(8,128)(2,1)S(1)} collective-permute-done((bf16[3,512,128]{2,1,0:T(8,128)(2,1)S(1)}, bf16[3,512,128]{2,1,0:T(8,128)(2,1)S(1)}, u32[]{:S(2)}, u32[]{:S(2)}) %collective-permute-start.8) | collective-permute-done | bytes 393248 | tf_op jit(solution)/shard_map/ppermute | solution.py:34
  37.9 4.4 %collective-permute-start.12 = (bf16[3,512,128]{2,1,0:T(8,128)(2,1)S(1)}, bf16[3,512,128]{2,1,0:T(8,128)(2,1)S(1)}, u32[]{:S(2)}, u32[]{:S(2)}) collective-permute-start(bf16[3,512,128]{2,1,0:T(8,128)(2,1)S(1)} %collective-permute-done.8.refs_0_.refs_1_), channel_id=1, source_target_pairs={{0,1},{1,0},{2,3},{3,2},{4,5},{5,4},{6,7},{7,6},{8,9},{9,8},{10,11... | collective-permute-start | bytes 1179656 | tf_op jit(solution)/shard_map/ppermute | solution.py:34
  42.3 6.4 %collective-permute-done.9.refs_3_.refs_5_ = bf16[3,512,128]{2,1,0:T(8,128)(2,1)S(1)} collective-permute-done((bf16[3,512,128]{2,1,0:T(8,128)(2,1)S(1)}, bf16[3,512,128]{2,1,0:T(8,128)(2,1)S(1)}, u32[]{:S(2)}, u32[]{:S(2)}) %collective-permute-start.9) | collective-permute-done | bytes 393248 | tf_op jit(solution)/shard_map/ppermute | solution.py:34
  48.7 4.9 %shard_map.48 = (f32[3,1024,128]{2,1,0:T(8,128)S(1)}, f32[3,1024,128]{2,1,0:T(8,128)S(1)}, f32[3,3,8,512]{3,2,1,0:T(8,128)S(1)}, f32[3,3,8,512]{3,2,1,0:T(8,128)...) custom-call(bf16[3,512,128]{2,1,0:T(8,128)(2,1)S(1)} %get-tuple-element.45.refs_0_, ...), custom_call_target="tpu_custom_call" | custom-call | flops 2412000000 | bytes 1800000 | tf_op jit(solution)/shard_map/pallas_call | solution.py:432
  53.6 4.8 %shard_map.49 = (f32[3,1024,128]{2,1,0:T(8,128)S(1)}, f32[3,1024,128]{2,1,0:T(8,128)S(1)}, f32[3,3,8,512]{3,2,1,0:T(8,128)S(1)}, f32[3,3,8,512]{3,2,1,0:T(8,128)S(1)}, f32[3,3,8,512]{3,2,1,0:T(8,128)S(1)}) custom-call(bf16[3,512,128]{2,1,0:T(8,128)(2,1)S(1)} %collective-permute-done.8.refs_0_.refs_1_, ...), custom_call_target="tpu_custom_call" | custom-call | flops 2412000000 | bytes 1800000 | tf_op jit(solution)/shard_map/pallas_call | solution.py:432
  58.4 5.0 %shard_map.50 = (f32[2,3,16,128]{3,2,1,0:T(8,128)S(1)}, f32[2,3,16,128]{3,2,1,0:T(8,128)S(1)}, f32[2,3,16,128]{3,2,1,0:T(8,128)S(1)}, f32[2,3,16,128]{3,2,1,0:T(8,128)S(1)}) custom-call(bf16[3,512,128]{2,1,0:T(8,128)(2,1)S(1)} %get-tuple-element.45.refs_0_, bf16[3,512,128]{2,1,0:T(8,128)(2,1)S(1)} %collective-permute-done.8.refs_0_.refs_1_, ...), custom_call_target="tpu_custom_call" | custom-call | flops 1608000000 | bytes 1200000 | tf_op jit(solution)/shard_map/pallas_call | solution.py:447
  63.4 69.6 %collective-permute-start.14 = (f32[2,3,16,128]{3,2,1,0:T(8,128)S(1)}, f32[2,3,16,128]{3,2,1,0:T(8,128)S(1)}, u32[]{:S(2)}, u32[]{:S(2)}) collective-permute-start(f32[2,3,16,128]{3,2,1,0:T(8,128)S(1)} %get-tuple-element.62), channel_id=1, source_target_pairs={{0,1},{1,0},{2,3},{3,2},{4,5},{5,4},{6,7},{7,6},{8,9},{9,8},{10,11... | collective-permute-start | bytes 147464 | tf_op jit(solution)/shard_map/ppermute | solution.py:34
  132.9 1.7 %collective-permute-start.15 = (f32[2,3,16,128]{3,2,1,0:T(8,128)S(1)}, f32[2,3,16,128]{3,2,1,0:T(8,128)S(1)}, u32[]{:S(2)}, u32[]{:S(2)}) collective-permute-start(f32[2,3,16,128]{3,2,1,0:T(8,128)S(1)} %get-tuple-element.64), channel_id=1, source_target_pairs={{0,2},{1,3},{2,0},{3,1},{4,6},{5,7},{6,4},{7,5},{8,10},{9,11},{10,... | collective-permute-start | bytes 147464 | tf_op jit(solution)/shard_map/ppermute | solution.py:34
  134.7 2.0 %collective-permute-done.15.rev_in = f32[2,3,16,128]{3,2,1,0:T(8,128)S(1)} collective-permute-done((f32[2,3,16,128]{3,2,1,0:T(8,128)S(1)}, f32[2,3,16,128]{3,2,1,0:T(8,128)S(1)}, u32[]{:S(2)}, u32[]{:S(2)}) %collective-permute-start.15) | collective-permute-done | bytes 49184 | tf_op jit(solution)/shard_map/ppermute | solution.py:34
  136.7 0.1 collective-permute-start.16
  136.9 4.1 %collective-permute-done.16.fwd_in = f32[3,16,128]{2,1,0:T(8,128)S(1)} collective-permute-done((f32[3,16,128]{2,1,0:T(8,128)S(1)}, f32[3,16,128]{2,1,0:T(8,128)S(1)}, u32[]{:S(2)}, u32[]{:S(2)}) %collective-permute-start.16) | collective-permute-done | bytes 24608 | tf_op jit(solution)/shard_map/ppermute | solution.py:34
  141.0 6.0 %collective-permute-start.18 = (f32[3,2,2,4,128]{4,3,2,1,0:T(4,128)S(1)}, f32[3,2,2,4,128]{4,3,2,1,0:T(4,128)S(1)}, u32[]{:S(2)}, u32[]{:S(2)}) collective-permute-start(f32[3,2,2,4,128]{4,3,2,1,0:T(4,128)S(1)} %shard_map.52.own), channel_id=1, source_target_pairs={{0,0},{1,2},{2,1},{3,4},{4,3},{5,6},{6,5},{7,8},{8,7},{9,10},{10,9... | collective-permute-start | bytes 73736 | tf_op jit(solution)/shard_map/ppermute | solution.py:34
  147.1 0.2 copy.9
  147.3 0.1 reshape.9.weight
  147.6 2.1 %collective-permute-done.18.chip = f32[3,2,2,4,128]{4,3,2,1,0:T(4,128)S(1)} collective-permute-done((f32[3,2,2,4,128]{4,3,2,1,0:T(4,128)S(1)}, f32[3,2,2,4,128]{4,3,2,1,0:T(4,128)S(1)}, u32[]{:S(2)}, u32[]{:S(2)}) %collective-permute-start.18) | collective-permute-done | bytes 24608 | tf_op jit(solution)/shard_map/ppermute | solution.py:34
  149.8 2.0 %shard_map.53 = f32[3,2,2,4,128]{4,3,2,1,0:T(4,128)} custom-call(f32[144]{0:T(256)S(1)} %reshape.9.weight, f32[8]{0:T(128)S(1)} %reshape.10.bias, f32[3,2,2,4,128]{4,3,2,1,0:T(4,128)S(1)} %collective-permute-done.18.chip, f32[3,2,2,4,128]{4,3,2,1,0:T(4,128)S(1)} %shard_map.52.own, f32[3,2,2,4,128]{4,3,2,1,0:T(4,128)S(1)} %collective-permute-done.19.core), custom_call_target="tpu_custom_call" | custom-call | tf_op jit(solution)/shard_map/pallas_call | solution.py:565
  (31 shorter events, 0.8 us)
Async XLA Ops:
  0.0 11.6 %copy-start.1 = (s32[3,2]{0,1:T(2,128)S(1)}, s32[3,2]{0,1:T(2,128)}, u32[]{:S(2)}) copy-start(s32[3,2]{0,1:T(2,128)} %param.5) | copy-start | bytes 76
  1.0 8.7 %collective-permute-start = (bf16[3,352,128]{2,1,0:T(8,128)(2,1)S(1)}, bf16[3,352,128]{2,1,0:T(8,128)(2,1)S(1)}, u32[]{:S(2)}, u32[]{:S(2)}) collective-permute-start(bf16[3,352,128]{2,1,0:T(8,128)(2,1)S(1)} %slice.8.refs_2_.refs_0_), channel_id=1, source_target_pairs={{0,16},{1,97},{2,18},{3,99},{4,20},{5,101},{6,22},{7,103},{8,24},{... | collective-permute-start | bytes 811016 | tf_op jit(solution)/shard_map/ppermute | solution.py:34
  4.5 5.2 %collective-permute-start.1 = (bf16[3,160,128]{2,1,0:T(8,128)(2,1)S(1)}, bf16[3,160,128]{2,1,0:T(8,128)(2,1)S(1)}, u32[]{:S(2)}, u32[]{:S(2)}) collective-permute-start(bf16[3,160,128]{2,1,0:T(8,128)(2,1)S(1)} %slice.9.refs_5_.refs_4_), channel_id=1, source_target_pairs={{0,32},{1,33},{2,34},{3,35},{4,36},{5,37},{6,38},{7,39},{8,40},{9,... | collective-permute-start | bytes 368648 | tf_op jit(solution)/shard_map/ppermute | solution.py:34
  9.7 8.6 %collective-permute-start.2 = (bf16[6,352,128]{2,1,0:T(8,128)(2,1)S(1)}, bf16[6,352,128]{2,1,0:T(8,128)(2,1)S(1)}, u32[]{:S(2)}, u32[]{:S(2)}) collective-permute-start(bf16[6,352,128]{2,1,0:T(8,128)(2,1)S(1)} %pad_maximum_fusion), channel_id=1, source_target_pairs={{0,32},{1,17},{2,34},{3,19},{4,36},{5,21},{6,38},{7,23},{8,40},{9,... | collective-permute-start | bytes 1622024 | tf_op jit(solution)/shard_map/ppermute | solution.py:34
  10.1 8.2 %collective-permute-start.3 = (bf16[6,160,128]{2,1,0:T(8,128)(2,1)S(1)}, bf16[6,160,128]{2,1,0:T(8,128)(2,1)S(1)}, u32[]{:S(2)}, u32[]{:S(2)}) collective-permute-start(bf16[6,160,128]{2,1,0:T(8,128)(2,1)S(1)} %pad_maximum_fusion.1), channel_id=1, source_target_pairs={{0,96},{1,97},{2,98},{3,99},{4,100},{5,101},{6,102},{7,103},{8,104... | collective-permute-start | bytes 737288 | tf_op jit(solution)/shard_map/ppermute | solution.py:34
  11.7 2.7 %collective-permute-start.4 = (s32[3,2]{1,0:T(4,128)S(1)}, s32[3,2]{1,0:T(4,128)S(1)}, u32[]{:S(2)}, u32[]{:S(2)}) collective-permute-start(s32[3,2]{1,0:T(4,128)S(1)} %copy.13.table), channel_id=1, source_target_pairs={{0,96},{1,33},{2,98},{3,35},{4,100},{5,37},{6,102},{7,39},{8,104},... | collective-permute-start | bytes 80 | tf_op jit(solution)/shard_map/ppermute | solution.py:34
  11.7 6.6 %collective-permute-start.5 = (s32[3,2]{1,0:T(4,128)S(1)}, s32[3,2]{1,0:T(4,128)S(1)}, u32[]{:S(2)}, u32[]{:S(2)}) collective-permute-start(s32[3,2]{1,0:T(4,128)S(1)} %copy.13.table), channel_id=1, source_target_pairs={{0,16},{1,17},{2,18},{3,19},{4,20},{5,21},{6,22},{7,23},{8,24},{9,... | collective-permute-start | bytes 80 | tf_op jit(solution)/shard_map/ppermute | solution.py:34
  19.5 8.6 %collective-permute-start.6 = (bf16[6,352,128]{2,1,0:T(8,128)(2,1)S(1)}, bf16[6,352,128]{2,1,0:T(8,128)(2,1)S(1)}, u32[]{:S(2)}, u32[]{:S(2)}) collective-permute-start(bf16[6,352,128]{2,1,0:T(8,128)(2,1)S(1)} %get-tuple-element.43), channel_id=1, source_target_pairs={{0,96},{1,33},{2,98},{3,35},{4,100},{5,37},{6,102},{7,39},{8,104},... | collective-permute-start | bytes 1622024 | tf_op jit(solution)/shard_map/ppermute | solution.py:34
  19.6 5.1 %collective-permute-start.7 = (bf16[6,160,128]{2,1,0:T(8,128)(2,1)S(1)}, bf16[6,160,128]{2,1,0:T(8,128)(2,1)S(1)}, u32[]{:S(2)}, u32[]{:S(2)}) collective-permute-start(bf16[6,160,128]{2,1,0:T(8,128)(2,1)S(1)} %get-tuple-element.44), channel_id=1, source_target_pairs={{0,16},{1,17},{2,18},{3,19},{4,20},{5,21},{6,22},{7,23},{8,24},{9,... | collective-permute-start | bytes 737288 | tf_op jit(solution)/shard_map/ppermute | solution.py:34
  29.1 8.8 %collective-permute-start.8 = (bf16[3,512,128]{2,1,0:T(8,128)(2,1)S(1)}, bf16[3,512,128]{2,1,0:T(8,128)(2,1)S(1)}, u32[]{:S(2)}, u32[]{:S(2)}) collective-permute-start(bf16[3,512,128]{2,1,0:T(8,128)(2,1)S(1)} %get-tuple-element.45.refs_0_), channel_id=1, source_target_pairs={{0,8},{1,9},{2,10},{3,11},{4,12},{5,13},{6,14},{7,15},{8,0},{9,1},... | collective-permute-start | bytes 1179656 | tf_op jit(solution)/shard_map/ppermute | solution.py:34
  32.2 10.1 %collective-permute-start.10 = (bf16[3,512,128]{2,1,0:T(8,128)(2,1)S(1)}, bf16[3,512,128]{2,1,0:T(8,128)(2,1)S(1)}, u32[]{:S(2)}, u32[]{:S(2)}) collective-permute-start(bf16[3,512,128]{2,1,0:T(8,128)(2,1)S(1)} %get-tuple-element.46.refs_2_.refs_4_), channel_id=1, source_target_pairs={{0,6},{1,3},{2,0},{3,5},{4,2},{5,7},{6,4},{7,1},{8,14},{9,11},{10,... | collective-permute-start | bytes 1179656 | tf_op jit(solution)/shard_map/ppermute | solution.py:34
  32.2 10.1 %collective-permute-start.11 = (bf16[3,512,128]{2,1,0:T(8,128)(2,1)S(1)}, bf16[3,512,128]{2,1,0:T(8,128)(2,1)S(1)}, u32[]{:S(2)}, u32[]{:S(2)}) collective-permute-start(bf16[3,512,128]{2,1,0:T(8,128)(2,1)S(1)} %get-tuple-element.45.refs_0_), channel_id=1, source_target_pairs={{0,1},{1,0},{2,3},{3,2},{4,5},{5,4},{6,7},{7,6},{8,9},{9,8},{10,11... | collective-permute-start | bytes 1179656 | tf_op jit(solution)/shard_map/ppermute | solution.py:34
  36.4 12.3 %collective-permute-start.9 = (bf16[3,512,128]{2,1,0:T(8,128)(2,1)S(1)}, bf16[3,512,128]{2,1,0:T(8,128)(2,1)S(1)}, u32[]{:S(2)}, u32[]{:S(2)}) collective-permute-start(bf16[3,512,128]{2,1,0:T(8,128)(2,1)S(1)} %get-tuple-element.46.refs_2_.refs_4_), channel_id=1, source_target_pairs={{0,2},{1,7},{2,4},{3,1},{4,6},{5,3},{6,0},{7,5},{8,10},{9,15},{10,... | collective-permute-start | bytes 1179656 | tf_op jit(solution)/shard_map/ppermute | solution.py:34
  37.9 15.6 %collective-permute-start.12 = (bf16[3,512,128]{2,1,0:T(8,128)(2,1)S(1)}, bf16[3,512,128]{2,1,0:T(8,128)(2,1)S(1)}, u32[]{:S(2)}, u32[]{:S(2)}) collective-permute-start(bf16[3,512,128]{2,1,0:T(8,128)(2,1)S(1)} %collective-permute-done.8.refs_0_.refs_1_), channel_id=1, source_target_pairs={{0,1},{1,0},{2,3},{3,2},{4,5},{5,4},{6,7},{7,6},{8,9},{9,8},{10,11... | collective-permute-start | bytes 1179656 | tf_op jit(solution)/shard_map/ppermute | solution.py:34
  48.7 9.7 %collective-permute-start.13 = (bf16[3,512,128]{2,1,0:T(8,128)(2,1)S(1)}, bf16[3,512,128]{2,1,0:T(8,128)(2,1)S(1)}, u32[]{:S(2)}, u32[]{:S(2)}) collective-permute-start(bf16[3,512,128]{2,1,0:T(8,128)(2,1)S(1)} %collective-permute-done.9.refs_3_.refs_5_), channel_id=1, source_target_pairs={{0,2},{1,7},{2,4},{3,1},{4,6},{5,3},{6,0},{7,5},{8,10},{9,15},{10,... | collective-permute-start | bytes 1179656 | tf_op jit(solution)/shard_map/ppermute | solution.py:34
  58.4 88.7 %copy-start = (f32[4,2,2,3,3]{0,2,4,3,1:T(2,128)S(1)}, f32[4,2,2,3,3]{0,2,4,3,1:T(2,128)}, u32[]{:S(2)}) copy-start(f32[4,2,2,3,3]{0,2,4,3,1:T(2,128)} %param.6) | copy-start | bytes 1732
  58.4 89.1 %copy-start.2 = (f32[4,2]{0,1:T(2,128)S(1)}, f32[4,2]{0,1:T(2,128)}, u32[]{:S(2)}) copy-start(f32[4,2]{0,1:T(2,128)} %param.7) | copy-start | bytes 100
  63.4 71.3 %collective-permute-start.14 = (f32[2,3,16,128]{3,2,1,0:T(8,128)S(1)}, f32[2,3,16,128]{3,2,1,0:T(8,128)S(1)}, u32[]{:S(2)}, u32[]{:S(2)}) collective-permute-start(f32[2,3,16,128]{3,2,1,0:T(8,128)S(1)} %get-tuple-element.62), channel_id=1, source_target_pairs={{0,1},{1,0},{2,3},{3,2},{4,5},{5,4},{6,7},{7,6},{8,9},{9,8},{10,11... | collective-permute-start | bytes 147464 | tf_op jit(solution)/shard_map/ppermute | solution.py:34
  132.9 3.7 %collective-permute-start.15 = (f32[2,3,16,128]{3,2,1,0:T(8,128)S(1)}, f32[2,3,16,128]{3,2,1,0:T(8,128)S(1)}, u32[]{:S(2)}, u32[]{:S(2)}) collective-permute-start(f32[2,3,16,128]{3,2,1,0:T(8,128)S(1)} %get-tuple-element.64), channel_id=1, source_target_pairs={{0,2},{1,3},{2,0},{3,1},{4,6},{5,7},{6,4},{7,5},{8,10},{9,11},{10,... | collective-permute-start | bytes 147464 | tf_op jit(solution)/shard_map/ppermute | solution.py:34
  136.7 4.3 %collective-permute-start.16 = (f32[3,16,128]{2,1,0:T(8,128)S(1)}, f32[3,16,128]{2,1,0:T(8,128)S(1)}, u32[]{:S(2)}, u32[]{:S(2)}) collective-permute-start(f32[3,16,128]{2,1,0:T(8,128)S(1)} %get-tuple-element.66), channel_id=1, source_target_pairs={{0,8},{1,9},{2,10},{3,11},{4,12},{5,13},{6,14},{7,15},{8,0},{9,1},... | collective-permute-start | bytes 73736 | tf_op jit(solution)/shard_map/ppermute | solution.py:34
  136.8 4.1 %collective-permute-start.17 = (f32[3,16,128]{2,1,0:T(8,128)S(1)}, f32[3,16,128]{2,1,0:T(8,128)S(1)}, u32[]{:S(2)}, u32[]{:S(2)}) collective-permute-start(f32[3,16,128]{2,1,0:T(8,128)S(1)} %get-tuple-element.68), channel_id=1, source_target_pairs={{0,6},{1,7},{2,4},{3,5},{4,2},{5,3},{6,0},{7,1},{8,14},{9,15},{10,... | collective-permute-start | bytes 73736 | tf_op jit(solution)/shard_map/ppermute | solution.py:34
  141.0 8.8 %collective-permute-start.18 = (f32[3,2,2,4,128]{4,3,2,1,0:T(4,128)S(1)}, f32[3,2,2,4,128]{4,3,2,1,0:T(4,128)S(1)}, u32[]{:S(2)}, u32[]{:S(2)}) collective-permute-start(f32[3,2,2,4,128]{4,3,2,1,0:T(4,128)S(1)} %shard_map.52.own), channel_id=1, source_target_pairs={{0,0},{1,2},{2,1},{3,4},{4,3},{5,6},{6,5},{7,8},{8,7},{9,10},{10,9... | collective-permute-start | bytes 73736 | tf_op jit(solution)/shard_map/ppermute | solution.py:34
  147.0 2.7 %collective-permute-start.19 = (f32[3,2,2,4,128]{4,3,2,1,0:T(4,128)S(1)}, f32[3,2,2,4,128]{4,3,2,1,0:T(4,128)S(1)}, u32[]{:S(2)}, u32[]{:S(2)}) collective-permute-start(f32[3,2,2,4,128]{4,3,2,1,0:T(4,128)S(1)} %shard_map.52.own), channel_id=1, source_target_pairs={{0,1},{1,0},{2,3},{3,2},{4,5},{5,4},{6,7},{7,6},{8,9},{9,8},{10,11... | collective-permute-start | bytes 73736 | tf_op jit(solution)/shard_map/ppermute | solution.py:34

commit v4 on v3

--- a/solution.py
+++ b/solution.py
@@ -234,49 +234,53 @@
             put(slice(c * width, (c + 1) * width), i == 0 and cols_first, (tt[c], xx[c], src_rows[i] * tt[c] - uu[c]))
 
 
-def early_kernel(*refs, which, ntgt, cells, width, ready):
-    nsrc = len(which)
+def early_kernel(*refs, which, bands, cells, width, given):
+    nsrc, ntgt = len(which), len(bands)
+    handed = bool(given)
     src, refs = refs[:nsrc], refs[nsrc:]
-    if ready:
-        rhs, acc, accy, g0, gq, gy = refs
+    if given:
+        scaled, (acc, accy, g0, gq, gy) = refs[: len(given)], refs[len(given) :]
     else:
-        tgt, refs = refs[:ntgt], refs[ntgt:]
-        acc, accy, g0, gq, gy, rhs = refs
+        tgt, (acc, accy, g0, gq, gy, rhs) = refs[:ntgt], refs[ntgt:]
+        scaled, given = (rhs,), (ntgt,)
+    seats = [(ref, n * cells) for ref, count in zip(scaled, given) for n in range(count)]
     src_rows, tgt_rows, _ = places(cells, width)
     src_rows = [src_rows[i] for i in which]
     scale = score_gain / math.sqrt(src[0].shape[-1]) * math.log2(math.e)
 
-    def one(p, jb, first):
+    def one(p, n, first):
         def sums(rows, total, rowed):
             acc[p, rows, :] = total if first else acc[p, rows, :] + total
             accy[p, rows, :] = rowed if first else accy[p, rows, :] + rowed
 
         def put(lanes, new, values):
             for ref, value in zip((g0, gq, gy), values):
-                ref[p, jb, :, lanes] = value if new else ref[p, jb, :, lanes] + value
-
-        b = rhs[p, jb * cells : (jb + 1) * cells, :]
-        block([ref[p] for ref in src], b, tgt_rows[jb], src_rows, sums, (put, True), cells, width)
+                ref[p, n, :, lanes] = value if new else ref[p, n, :, lanes] + value
+
+        ref, start = seats[n]
+        b = ref[p, start : start + cells, :]
+        block([ref[p] for ref in src], b, tgt_rows[bands[n]], src_rows, sums, (put, True), cells, width)
 
     def pair(p, carry):
-        if not ready:
-            targets(tgt, p, scale, rhs.at[p], 0, cells)
-        for jb in range(ntgt):
-            one(p, jb, jb == 0)
+        if not handed:
+            targets(tgt, p, scale, scaled[0].at[p], 0, cells)
+        for n in range(ntgt):
+            one(p, n, n == 0)
         return carry
 
     lax.fori_loop(0, src[0].shape[0], pair, 0)
 
 
-def late_kernel(*refs, nsrc, ntgt, cells, width):
+def late_kernel(*refs, nsrc, ntgt, cells, width, calls):
     src, tgt = refs[:nsrc], refs[nsrc : nsrc + ntgt]
-    before = (refs[nsrc + ntgt : nsrc + ntgt + 5], refs[nsrc + ntgt + 5 : nsrc + ntgt + 10])
-    fwd_keep, fwd_send, rev_keep, rev_send, rev, rhs, acc, accy, g0, gq, gy, shift_r, shift_c = refs[nsrc + ntgt + 10 :]
+    base = nsrc + ntgt
+    before = [(*call, refs[base + 5 * n : base + 5 * n + 5]) for n, call in enumerate(calls)]
+    fwd_keep, fwd_send, rev_keep, rev_send, rev, rhs, acc, accy, g0, gq, gy, shift_r, shift_c = refs[base + 5 * len(calls) :]
     fwd = [(fwd_keep, 0), (fwd_keep, 1), (fwd_send, 0), (fwd_send, 1)]
     band_rows = cells // width
     src_rows, tgt_rows, tgt_slot = places(cells, width)
     scale = score_gain / math.sqrt(src[0].shape[-1]) * math.log2(math.e)
-    early = before[0][2].shape[1]
+    early = ntgt - 1
     lane = lax.broadcasted_iota(jnp.int32, (16, width), 1)
     row16 = lax.broadcasted_iota(jnp.int32, (16, width), 0)
     ramp = (2 * lane - (width - 1)).astype(jnp.float32)
@@ -340,10 +344,13 @@
 
             def sums(rows, total, rowed):
                 i, r0 = divmod(rows.start, cells)
-                r0 += i // 2 * cells
-                old = before[i % 2]
-                acc[rows, :] = (old[0][p, r0 : r0 + 8, :] if jb == early else acc[rows, :]) + total
-                accy[rows, :] = (old[1][p, r0 : r0 + 8, :] if jb == early else accy[rows, :]) + rowed
+                for which, _, old in before:
+                    if i in which:
+                        at = which.index(i) * cells + r0
+                        total = total + old[0][p, at : at + 8, :]
+                        rowed = rowed + old[1][p, at : at + 8, :]
+                acc[rows, :] = total
+                accy[rows, :] = rowed
 
             b = rhs[jb * cells : (jb + 1) * cells, :]
             block(sources, b, tgt_rows[jb], src_rows, sums, (put(jb), True), cells, width)
@@ -351,7 +358,8 @@
         def cols_of(j, cs):
             if j >= early:
                 return g0[j, :, cs], gq[j, :, cs], gy[j, :, cs]
-            return [before[0][n][p, j, :, cs] + before[1][n][p, j, :, cs] for n in (2, 3, 4)]
+            olds = [(old, bands.index(j)) for _, bands, old in before if j in bands]
+            return [functools.reduce(jnp.add, [old[n][p, at, :, cs] for old, at in olds]) for n in (2, 3, 4)]
 
         ok = emit(p, cols_of, False)
 
@@ -418,19 +426,19 @@
     )
 
 
-def match_early(src, which, tgt=None, scaled=None):
+def match_early(src, which, bands, tgt=None, scaled=()):
     pairs, cells, chans = src[0].shape
     width = 128
-    nsrc = len(src)
-    ntgt = len(tgt) if tgt else scaled.shape[1] // cells
+    nsrc, ntgt = len(src), len(bands)
     rows = jax.ShapeDtypeStruct((pairs, nsrc * cells, width), jnp.float32)
     cols = jax.ShapeDtypeStruct((pairs, ntgt, 8, cells), jnp.float32)
     shapes = [rows, rows, cols, cols, cols]
     if tgt:
         shapes.append(jax.ShapeDtypeStruct((pairs, ntgt * cells, 2 * chans), jnp.bfloat16))
-    operands = (*src, *tgt) if tgt else (*src, scaled)
+    operands = (*src, *tgt) if tgt else (*src, *scaled)
+    given = tuple(part.shape[1] // cells for part in scaled)
     return pl.pallas_call(
-        functools.partial(early_kernel, which=which, ntgt=ntgt, cells=cells, width=width, ready=not tgt),
+        functools.partial(early_kernel, which=which, bands=bands, cells=cells, width=width, given=given),
         out_shape=shapes,
         in_specs=[VMEM] * len(operands),
         out_specs=[VMEM] * len(shapes),
@@ -439,15 +447,15 @@
     )(*operands)
 
 
-def match_late(src, tgt, early):
+def match_late(src, tgt, early, calls):
     pairs, cells, chans = src[0].shape
     width = 128
     nsrc, ntgt = len(src), len(tgt)
     stats = jax.ShapeDtypeStruct((2, pairs, 4 * cells // width, width), jnp.float32)
     return pl.pallas_call(
-        functools.partial(late_kernel, nsrc=nsrc, ntgt=ntgt, cells=cells, width=width),
+        functools.partial(late_kernel, nsrc=nsrc, ntgt=ntgt, cells=cells, width=width, calls=calls),
         out_shape=[stats] * 4,
-        in_specs=[VMEM] * (nsrc + ntgt + 10),
+        in_specs=[VMEM] * (nsrc + ntgt + len(early)),
         out_specs=[VMEM] * 4,
         scratch_shapes=[
             pltpu.VMEM((4,) + stats.shape[1:], jnp.float32),
@@ -514,27 +522,27 @@
     )(fwd, fwd_in, rev, rev_in)
 
 
-def refine_kernel(weight, bias, chip, own, core, out, *cur, layers):
+def refine_kernel(weight, bias, chip, own, core, out, mask, *cur, layers):
     pairs, ways, comps, band_rows, width = own.shape
-    high = 16
+    high = 3 * band_rows
     total = pairs * ways * high
     band = (lax.axis_index("bh") * SIZES[3] + lax.axis_index("bz")) * SIZES[4] + lax.axis_index("bc")
     last = SIZES[2] * SIZES[3] * SIZES[4] - 1
     odd = lax.axis_index("bc") == 1
-    for i in range(comps):
-        for p in range(pairs):
-            for d in range(ways):
-                base = (p * ways + d) * high
+    full = lambda value: jnp.full((band_rows, width), value, jnp.float32)
+    for p in range(pairs):
+        for d in range(ways):
+            base = (p * ways + d) * high
+            mask[base : base + band_rows] = full(jnp.where(band == 0, 0.0, 1.0))
+            mask[base + band_rows : base + 2 * band_rows] = full(1.0)
+            mask[base + 2 * band_rows : base + high] = full(jnp.where(band == last, 0.0, 1.0))
+            for i in range(comps):
                 near, far = core[p, d, i], chip[p, d, i]
                 cur[i][base : base + band_rows] = jnp.where(odd, near, far)
                 cur[i][base + band_rows : base + 2 * band_rows] = own[p, d, i]
-                cur[i][base + 2 * band_rows : base + 3 * band_rows] = jnp.where(odd, far, near)
-                cur[i][base + 3 * band_rows : base + high] = jnp.zeros((high - 3 * band_rows, width), jnp.float32)
-    row = lax.broadcasted_iota(jnp.int32, (total, width), 0) & (high - 1)
+                cur[i][base + 2 * band_rows : base + high] = jnp.where(odd, far, near)
+    inside = mask[...]
     lane = lax.broadcasted_iota(jnp.int32, (total, width), 1)
-    low = jnp.where(band == 0, band_rows, 0)
-    top = jnp.where(band == last, 2 * band_rows, 3 * band_rows)
-    inside = ((row >= low) & (row < top)).astype(jnp.float32)
     keep_left = (lane > 0).astype(jnp.float32)
     keep_right = (lane < width - 1).astype(jnp.float32)
     for layer in range(layers):
@@ -561,13 +569,13 @@
 
 
 def refine(weight, bias, chip, own, core):
-    pairs, ways, comps, _, width = own.shape
+    pairs, ways, comps, band_rows, width = own.shape
     return pl.pallas_call(
         functools.partial(refine_kernel, layers=weight.shape[0]),
         out_shape=jax.ShapeDtypeStruct(own.shape, jnp.float32),
         in_specs=[SMEM, SMEM, VMEM, VMEM, VMEM],
         out_specs=VMEM,
-        scratch_shapes=[pltpu.VMEM((pairs * ways * 16, width), jnp.float32)] * comps,
+        scratch_shapes=[pltpu.VMEM((pairs * ways * 3 * band_rows, width), jnp.float32)] * (comps + 1),
         compiler_params=pltpu.CompilerParams(vmem_limit_bytes=4 << 20),
     )(weight.reshape(-1), bias.reshape(-1), chip, own, core)
 
@@ -593,12 +601,13 @@
     tgt2 = hop(tgt0, back)
     src1 = hop(src0, flip_h)
     src2 = hop(src0, flip_c)
-    tgt1, tgt2, src2 = lax.optimization_barrier((tgt1, tgt2, src2))
+    *own, scaled0 = match_early((src0, src2), (0, 2), (0,), tgt=(tgt0,))
     tgt3 = hop(tgt1, ring)
-    *own, scaled = match_early((src0, src2), (0, 2), tgt=(tgt0, tgt1, tgt2))
+    *near, scaled1 = match_early((src0, src2), (0, 2), (1, 2), tgt=(tgt1, tgt2))
     src3 = hop(src1, flip_c)
-    other = match_early((src1, src3), (1, 3), scaled=scaled)
-    return match_late((src0, src1, src2, src3), (tgt0, tgt1, tgt2, tgt3), (*own, *other))
+    other = match_early((src1, src3), (1, 3), (0, 1, 2), scaled=(scaled0, scaled1))
+    calls = (((0, 2), (0,)), ((0, 2), (1, 2)), ((1, 3), (0, 1, 2)))
+    return match_late((src0, src1, src2, src3), (tgt0, tgt1, tgt2, tgt3), (*own, *near, *other), calls)
 
 
 def shards(features, frame_pairs, conv_weight, conv_bias):

time: 154 us -> 154 us (level)
  waiting for transfers between devices: 34.8 us -> 30.3 us
  starting transfers between devices: 95.3 us -> 98.5 us
    ppermute x20, waiting for transfers between devices: 34.8 us -> 30.3 us  [hop(): return lax.ppermute(value, AXES, route)]
    ppermute x20, starting transfers between devices: 95.3 us -> 98.5 us  [hop(): return lax.ppermute(value, AXES, route)]
    pallas_call x2 -> x3, Pallas kernels: 9.68 us -> 10.1 us  [match_early(): pl.pallas_call(functools.partial(early_kernel, which=which, bands=bands,...]
  transfers between devices with their start and end apart: 20 -> 20, of which waited for: 10 -> 10; matrix products, arithmetic and copies ran while one was open for 1% -> 1% of each run, Pallas kernels for 6% -> 7%
where the time goes in v4:
time: 154 us; the launch traced here: 151 us
  starting transfers between devices  98.5 us (64%)
  waiting for transfers between devices  30.3 us (20%)
  Pallas kernels  19.5 us (13%)
  local copies, waits for them, and re-layouts  2.5 us (2%)
    ppermute x20, starting transfers between devices, hop(): return lax.ppermute(value, AXES, route)  98.5 us
    ppermute x20, waiting for transfers between devices, hop(): return lax.ppermute(value, AXES, route)  30.3 us
    pallas_call x3, Pallas kernels, match_early(): pl.pallas_call(functools.partial(early_kernel, which=which, bands=bands,...  10.1 us
    pallas_call x1, Pallas kernels, match_late(): pl.pallas_call(functools.partial(late_kernel, nsrc=nsrc, ntgt=ntgt, cells...  5.21 us
  transfers between devices with their start and end apart: 20, of which 10 were waited for; matrix products, arithmetic and copies ran while one was open for 1% of the time, Pallas kernels for 7%

profile of v4, /device:TPU:97, one launch (start us, length us, event | category | flops | bytes accessed | tf_op | source)
XLA Modules:
  0.0 151.0 jit_solution(1695223939267457959)
XLA Ops:
  0.0 1.0 slice.8.refs_2_.refs_0_
  1.0 2.6 %collective-permute-start = (bf16[3,352,128]{2,1,0:T(8,128)(2,1)S(1)}, bf16[3,352,128]{2,1,0:T(8,128)(2,1)S(1)}, u32[]{:S(2)}, u32[]{:S(2)}) collective-permute-start(bf16[3,352,128]{2,1,0:T(8,128)(2,1)S(1)} %slice.8.refs_2_.refs_0_), channel_id=1, source_target_pairs={{0,16},{1,97},{2,18},{3,99},{4,20},{5,101},{6,22},{7,103},{8,24},{... | collective-permute-start | bytes 811016 | tf_op jit(solution)/shard_map/ppermute | solution.py:34
  3.5 0.9 slice.9.refs_5_.refs_4_
  4.5 5.1 %collective-permute-done.1.refs_6_.refs_5_ = bf16[3,160,128]{2,1,0:T(8,128)(2,1)S(1)} collective-permute-done((bf16[3,160,128]{2,1,0:T(8,128)(2,1)S(1)}, bf16[3,160,128]{2,1,0:T(8,128)(2,1)S(1)}, u32[]{:S(2)}, u32[]{:S(2)}) %collective-permute-start.1) | collective-permute-done | bytes 122912 | tf_op jit(solution)/shard_map/ppermute | solution.py:34
  9.7 0.4 collective-permute-start.2
  10.1 1.5 collective-permute-start.3
  11.7 0.2 collective-permute-start.5
  12.0 2.5 %collective-permute-done.4.refs_0_ = s32[3,2]{1,0:T(4,128)S(1)} collective-permute-done((s32[3,2]{1,0:T(4,128)S(1)}, s32[3,2]{1,0:T(4,128)S(1)}, u32[]{:S(2)}, u32[]{:S(2)}) %collective-permute-start.4) | collective-permute-done | bytes 56 | tf_op jit(solution)/shard_map/ppermute | solution.py:34
  14.4 3.9 %collective-permute-done.5.refs_1_ = s32[3,2]{1,0:T(4,128)S(1)} collective-permute-done((s32[3,2]{1,0:T(4,128)S(1)}, s32[3,2]{1,0:T(4,128)S(1)}, u32[]{:S(2)}, u32[]{:S(2)}) %collective-permute-start.5) | collective-permute-done | bytes 56 | tf_op jit(solution)/shard_map/ppermute | solution.py:34
  18.3 1.1 shard_map.46
  19.6 1.2 collective-permute-start.7
  20.8 3.9 %collective-permute-done.7.refs_7_ = bf16[6,160,128]{2,1,0:T(8,128)(2,1)S(1)} collective-permute-done((bf16[6,160,128]{2,1,0:T(8,128)(2,1)S(1)}, bf16[6,160,128]{2,1,0:T(8,128)(2,1)S(1)}, u32[]{:S(2)}, u32[]{:S(2)}) %collective-permute-start.7) | collective-permute-done | bytes 245792 | tf_op jit(solution)/shard_map/ppermute | solution.py:34
  24.7 3.4 %collective-permute-done.6.refs_3_ = bf16[6,352,128]{2,1,0:T(8,128)(2,1)S(1)} collective-permute-done((bf16[6,352,128]{2,1,0:T(8,128)(2,1)S(1)}, bf16[6,352,128]{2,1,0:T(8,128)(2,1)S(1)}, u32[]{:S(2)}, u32[]{:S(2)}) %collective-permute-start.6) | collective-permute-done | bytes 540704 | tf_op jit(solution)/shard_map/ppermute | solution.py:34
  28.0 1.1 shard_map.47
  29.1 3.1 %collective-permute-start.8 = (bf16[3,512,128]{2,1,0:T(8,128)(2,1)S(1)}, bf16[3,512,128]{2,1,0:T(8,128)(2,1)S(1)}, u32[]{:S(2)}, u32[]{:S(2)}) collective-permute-start(bf16[3,512,128]{2,1,0:T(8,128)(2,1)S(1)} %get-tuple-element.48.refs_0_), channel_id=1, source_target_pairs={{0,8},{1,9},{2,10},{3,11},{4,12},{5,13},{6,14},{7,15},{8,0},{9,1},... | collective-permute-start | bytes 1179656 | tf_op jit(solution)/shard_map/ppermute | solution.py:34
  32.3 3.6 %collective-permute-start.9 = (bf16[3,512,128]{2,1,0:T(8,128)(2,1)S(1)}, bf16[3,512,128]{2,1,0:T(8,128)(2,1)S(1)}, u32[]{:S(2)}, u32[]{:S(2)}) collective-permute-start(bf16[3,512,128]{2,1,0:T(8,128)(2,1)S(1)} %get-tuple-element.48.refs_0_), channel_id=1, source_target_pairs={{0,1},{1,0},{2,3},{3,2},{4,5},{5,4},{6,7},{7,6},{8,9},{9,8},{10,11... | collective-permute-start | bytes 1179656 | tf_op jit(solution)/shard_map/ppermute | solution.py:34
  36.0 0.8 collective-permute-start.12
  36.8 1.1 collective-permute-done.8.refs_0_.refs_1_
  37.9 4.4 %collective-permute-start.10 = (bf16[3,512,128]{2,1,0:T(8,128)(2,1)S(1)}, bf16[3,512,128]{2,1,0:T(8,128)(2,1)S(1)}, u32[]{:S(2)}, u32[]{:S(2)}) collective-permute-start(bf16[3,512,128]{2,1,0:T(8,128)(2,1)S(1)} %collective-permute-done.8.refs_0_.refs_1_), channel_id=1, source_target_pairs={{0,1},{1,0},{2,3},{3,2},{4,5},{5,4},{6,7},{7,6},{8,9},{9,8},{10,11... | collective-permute-start | bytes 1179656 | tf_op jit(solution)/shard_map/ppermute | solution.py:34
  42.4 1.9 %shard_map.48 = (f32[3,1024,128]{2,1,0:T(8,128)S(1)}, f32[3,1024,128]{2,1,0:T(8,128)S(1)}, f32[3,1,8,512]{3,2,1,0:T(8,128)S(1)}, f32[3,1,8,512]{3,2,1,0:T(8,128)...) custom-call(bf16[3,512,128]{2,1,0:T(8,128)(2,1)S(1)} %get-tuple-element.48.refs_0_, ...), custom_call_target="tpu_custom_call" | custom-call | flops 804000000 | bytes 600000 | tf_op jit(solution)/shard_map/pallas_call | solution.py:440
  44.3 2.9 %collective-permute-done.12.refs_3_.refs_6_ = bf16[3,512,128]{2,1,0:T(8,128)(2,1)S(1)} collective-permute-done((bf16[3,512,128]{2,1,0:T(8,128)(2,1)S(1)}, bf16[3,512,128]{2,1,0:T(8,128)(2,1)S(1)}, u32[]{:S(2)}, u32[]{:S(2)}) %collective-permute-start.12) | collective-permute-done | bytes 393248 | tf_op jit(solution)/shard_map/ppermute | solution.py:34
  47.2 3.4 %shard_map.49 = (f32[3,1024,128]{2,1,0:T(8,128)S(1)}, f32[3,1024,128]{2,1,0:T(8,128)S(1)}, f32[3,2,8,512]{3,2,1,0:T(8,128)S(1)}, f32[3,2,8,512]{3,2,1,0:T(8,128)...) custom-call(bf16[3,512,128]{2,1,0:T(8,128)(2,1)S(1)} %get-tuple-element.48.refs_0_, ...), custom_call_target="tpu_custom_call" | custom-call | flops 1608000000 | bytes 1200000 | tf_op jit(solution)/shard_map/pallas_call | solution.py:440
  50.6 4.8 %shard_map.50 = (f32[3,1024,128]{2,1,0:T(8,128)S(1)}, f32[3,1024,128]{2,1,0:T(8,128)S(1)}, f32[3,3,8,512]{3,2,1,0:T(8,128)S(1)}, f32[3,3,8,512]{3,2,1,0:T(8,128)S(1)}, f32[3,3,8,512]{3,2,1,0:T(8,128)S(1)}) custom-call(bf16[3,512,128]{2,1,0:T(8,128)(2,1)S(1)} %collective-permute-done.8.refs_0_.refs_1_, ...), custom_call_target="tpu_custom_call" | custom-call | flops 2412000000 | bytes 1800000 | tf_op jit(solution)/shard_map/pallas_call | solution.py:440
  55.5 5.2 %shard_map.51 = (f32[2,3,16,128]{3,2,1,0:T(8,128)S(1)}, f32[2,3,16,128]{3,2,1,0:T(8,128)S(1)}, f32[2,3,16,128]{3,2,1,0:T(8,128)S(1)}, f32[2,3,16,128]{3,2,1,0:T(8,128)S(1)}) custom-call(bf16[3,512,128]{2,1,0:T(8,128)(2,1)S(1)} %get-tuple-element.48.refs_0_, bf16[3,512,128]{2,1,0:T(8,128)(2,1)S(1)} %collective-permute-done.8.refs_0_.refs_1_, ...), custom_call_target="tpu_custom_call" | custom-call | flops 1608000000 | bytes 1200000 | tf_op jit(solution)/shard_map/pallas_call | solution.py:455
  60.7 72.3 %collective-permute-start.14 = (f32[2,3,16,128]{3,2,1,0:T(8,128)S(1)}, f32[2,3,16,128]{3,2,1,0:T(8,128)S(1)}, u32[]{:S(2)}, u32[]{:S(2)}) collective-permute-start(f32[2,3,16,128]{3,2,1,0:T(8,128)S(1)} %get-tuple-element.68), channel_id=1, source_target_pairs={{0,1},{1,0},{2,3},{3,2},{4,5},{5,4},{6,7},{7,6},{8,9},{9,8},{10,11... | collective-permute-start | bytes 147464 | tf_op jit(solution)/shard_map/ppermute | solution.py:34
  133.1 1.0 collective-permute-start.15
  134.1 1.9 %collective-permute-done.15.rev_in = f32[2,3,16,128]{3,2,1,0:T(8,128)S(1)} collective-permute-done((f32[2,3,16,128]{3,2,1,0:T(8,128)S(1)}, f32[2,3,16,128]{3,2,1,0:T(8,128)S(1)}, u32[]{:S(2)}, u32[]{:S(2)}) %collective-permute-start.15) | collective-permute-done | bytes 49184 | tf_op jit(solution)/shard_map/ppermute | solution.py:34
  136.2 4.1 %collective-permute-done.16.fwd_in = f32[3,16,128]{2,1,0:T(8,128)S(1)} collective-permute-done((f32[3,16,128]{2,1,0:T(8,128)S(1)}, f32[3,16,128]{2,1,0:T(8,128)S(1)}, u32[]{:S(2)}, u32[]{:S(2)}) %collective-permute-start.16) | collective-permute-done | bytes 24608 | tf_op jit(solution)/shard_map/ppermute | solution.py:34
  140.3 6.6 %collective-permute-start.18 = (f32[3,2,2,4,128]{4,3,2,1,0:T(4,128)S(1)}, f32[3,2,2,4,128]{4,3,2,1,0:T(4,128)S(1)}, u32[]{:S(2)}, u32[]{:S(2)}) collective-permute-start(f32[3,2,2,4,128]{4,3,2,1,0:T(4,128)S(1)} %shard_map.53.own), channel_id=1, source_target_pairs={{0,0},{1,2},{2,1},{3,4},{4,3},{5,6},{6,5},{7,8},{8,7},{9,10},{10,9... | collective-permute-start | bytes 73736 | tf_op jit(solution)/shard_map/ppermute | solution.py:34
  147.0 0.2 copy.9
  147.5 1.6 %collective-permute-done.18.chip = f32[3,2,2,4,128]{4,3,2,1,0:T(4,128)S(1)} collective-permute-done((f32[3,2,2,4,128]{4,3,2,1,0:T(4,128)S(1)}, f32[3,2,2,4,128]{4,3,2,1,0:T(4,128)S(1)}, u32[]{:S(2)}, u32[]{:S(2)}) %collective-permute-start.18) | collective-permute-done | bytes 24608 | tf_op jit(solution)/shard_map/ppermute | solution.py:34
  149.1 1.9 %shard_map.54 = f32[3,2,2,4,128]{4,3,2,1,0:T(4,128)} custom-call(f32[144]{0:T(256)S(1)} %reshape.9.weight, f32[8]{0:T(128)S(1)} %reshape.10.bias, f32[3,2,2,4,128]{4,3,2,1,0:T(4,128)S(1)} %collective-permute-done.18.chip, f32[3,2,2,4,128]{4,3,2,1,0:T(4,128)S(1)} %shard_map.53.own, f32[3,2,2,4,128]{4,3,2,1,0:T(4,128)S(1)} %collective-permute-done.19.core), custom_call_target="tpu_custom_call" | custom-call | tf_op jit(solution)/shard_map/pallas_call | solution.py:573
  (32 shorter events, 1.3 us)
Async XLA Ops:
  0.0 11.6 %copy-start.1 = (s32[3,2]{0,1:T(2,128)S(1)}, s32[3,2]{0,1:T(2,128)}, u32[]{:S(2)}) copy-start(s32[3,2]{0,1:T(2,128)} %param.5) | copy-start | bytes 76
  1.0 8.7 %collective-permute-start = (bf16[3,352,128]{2,1,0:T(8,128)(2,1)S(1)}, bf16[3,352,128]{2,1,0:T(8,128)(2,1)S(1)}, u32[]{:S(2)}, u32[]{:S(2)}) collective-permute-start(bf16[3,352,128]{2,1,0:T(8,128)(2,1)S(1)} %slice.8.refs_2_.refs_0_), channel_id=1, source_target_pairs={{0,16},{1,97},{2,18},{3,99},{4,20},{5,101},{6,22},{7,103},{8,24},{... | collective-permute-start | bytes 811016 | tf_op jit(solution)/shard_map/ppermute | solution.py:34
  4.5 5.2 %collective-permute-start.1 = (bf16[3,160,128]{2,1,0:T(8,128)(2,1)S(1)}, bf16[3,160,128]{2,1,0:T(8,128)(2,1)S(1)}, u32[]{:S(2)}, u32[]{:S(2)}) collective-permute-start(bf16[3,160,128]{2,1,0:T(8,128)(2,1)S(1)} %slice.9.refs_5_.refs_4_), channel_id=1, source_target_pairs={{0,32},{1,33},{2,34},{3,35},{4,36},{5,37},{6,38},{7,39},{8,40},{9,... | collective-permute-start | bytes 368648 | tf_op jit(solution)/shard_map/ppermute | solution.py:34
  9.7 8.6 %collective-permute-start.2 = (bf16[6,352,128]{2,1,0:T(8,128)(2,1)S(1)}, bf16[6,352,128]{2,1,0:T(8,128)(2,1)S(1)}, u32[]{:S(2)}, u32[]{:S(2)}) collective-permute-start(bf16[6,352,128]{2,1,0:T(8,128)(2,1)S(1)} %pad_maximum_fusion), channel_id=1, source_target_pairs={{0,32},{1,17},{2,34},{3,19},{4,36},{5,21},{6,38},{7,23},{8,40},{9,... | collective-permute-start | bytes 1622024 | tf_op jit(solution)/shard_map/ppermute | solution.py:34
  10.1 8.2 %collective-permute-start.3 = (bf16[6,160,128]{2,1,0:T(8,128)(2,1)S(1)}, bf16[6,160,128]{2,1,0:T(8,128)(2,1)S(1)}, u32[]{:S(2)}, u32[]{:S(2)}) collective-permute-start(bf16[6,160,128]{2,1,0:T(8,128)(2,1)S(1)} %pad_maximum_fusion.1), channel_id=1, source_target_pairs={{0,96},{1,97},{2,98},{3,99},{4,100},{5,101},{6,102},{7,103},{8,104... | collective-permute-start | bytes 737288 | tf_op jit(solution)/shard_map/ppermute | solution.py:34
  11.7 2.7 %collective-permute-start.4 = (s32[3,2]{1,0:T(4,128)S(1)}, s32[3,2]{1,0:T(4,128)S(1)}, u32[]{:S(2)}, u32[]{:S(2)}) collective-permute-start(s32[3,2]{1,0:T(4,128)S(1)} %copy.13.table), channel_id=1, source_target_pairs={{0,96},{1,33},{2,98},{3,35},{4,100},{5,37},{6,102},{7,39},{8,104},... | collective-permute-start | bytes 80 | tf_op jit(solution)/shard_map/ppermute | solution.py:34
  11.7 6.6 %collective-permute-start.5 = (s32[3,2]{1,0:T(4,128)S(1)}, s32[3,2]{1,0:T(4,128)S(1)}, u32[]{:S(2)}, u32[]{:S(2)}) collective-permute-start(s32[3,2]{1,0:T(4,128)S(1)} %copy.13.table), channel_id=1, source_target_pairs={{0,16},{1,17},{2,18},{3,19},{4,20},{5,21},{6,22},{7,23},{8,24},{9,... | collective-permute-start | bytes 80 | tf_op jit(solution)/shard_map/ppermute | solution.py:34
  19.5 8.6 %collective-permute-start.6 = (bf16[6,352,128]{2,1,0:T(8,128)(2,1)S(1)}, bf16[6,352,128]{2,1,0:T(8,128)(2,1)S(1)}, u32[]{:S(2)}, u32[]{:S(2)}) collective-permute-start(bf16[6,352,128]{2,1,0:T(8,128)(2,1)S(1)} %get-tuple-element.46), channel_id=1, source_target_pairs={{0,96},{1,33},{2,98},{3,35},{4,100},{5,37},{6,102},{7,39},{8,104},... | collective-permute-start | bytes 1622024 | tf_op jit(solution)/shard_map/ppermute | solution.py:34
  19.6 5.1 %collective-permute-start.7 = (bf16[6,160,128]{2,1,0:T(8,128)(2,1)S(1)}, bf16[6,160,128]{2,1,0:T(8,128)(2,1)S(1)}, u32[]{:S(2)}, u32[]{:S(2)}) collective-permute-start(bf16[6,160,128]{2,1,0:T(8,128)(2,1)S(1)} %get-tuple-element.47), channel_id=1, source_target_pairs={{0,16},{1,17},{2,18},{3,19},{4,20},{5,21},{6,22},{7,23},{8,24},{9,... | collective-permute-start | bytes 737288 | tf_op jit(solution)/shard_map/ppermute | solution.py:34
  29.1 8.8 %collective-permute-start.8 = (bf16[3,512,128]{2,1,0:T(8,128)(2,1)S(1)}, bf16[3,512,128]{2,1,0:T(8,128)(2,1)S(1)}, u32[]{:S(2)}, u32[]{:S(2)}) collective-permute-start(bf16[3,512,128]{2,1,0:T(8,128)(2,1)S(1)} %get-tuple-element.48.refs_0_), channel_id=1, source_target_pairs={{0,8},{1,9},{2,10},{3,11},{4,12},{5,13},{6,14},{7,15},{8,0},{9,1},... | collective-permute-start | bytes 1179656 | tf_op jit(solution)/shard_map/ppermute | solution.py:34
  32.2 10.1 %collective-permute-start.11 = (bf16[3,512,128]{2,1,0:T(8,128)(2,1)S(1)}, bf16[3,512,128]{2,1,0:T(8,128)(2,1)S(1)}, u32[]{:S(2)}, u32[]{:S(2)}) collective-permute-start(bf16[3,512,128]{2,1,0:T(8,128)(2,1)S(1)} %get-tuple-element.49.refs_2_.refs_4_), channel_id=1, source_target_pairs={{0,2},{1,7},{2,4},{3,1},{4,6},{5,3},{6,0},{7,5},{8,10},{9,15},{10,... | collective-permute-start | bytes 1179656 | tf_op jit(solution)/shard_map/ppermute | solution.py:34
  32.3 10.1 %collective-permute-start.9 = (bf16[3,512,128]{2,1,0:T(8,128)(2,1)S(1)}, bf16[3,512,128]{2,1,0:T(8,128)(2,1)S(1)}, u32[]{:S(2)}, u32[]{:S(2)}) collective-permute-start(bf16[3,512,128]{2,1,0:T(8,128)(2,1)S(1)} %get-tuple-element.48.refs_0_), channel_id=1, source_target_pairs={{0,1},{1,0},{2,3},{3,2},{4,5},{5,4},{6,7},{7,6},{8,9},{9,8},{10,11... | collective-permute-start | bytes 1179656 | tf_op jit(solution)/shard_map/ppermute | solution.py:34
  36.0 11.2 %collective-permute-start.12 = (bf16[3,512,128]{2,1,0:T(8,128)(2,1)S(1)}, bf16[3,512,128]{2,1,0:T(8,128)(2,1)S(1)}, u32[]{:S(2)}, u32[]{:S(2)}) collective-permute-start(bf16[3,512,128]{2,1,0:T(8,128)(2,1)S(1)} %get-tuple-element.49.refs_2_.refs_4_), channel_id=1, source_target_pairs={{0,6},{1,3},{2,0},{3,5},{4,2},{5,7},{6,4},{7,1},{8,14},{9,11},{10,... | collective-permute-start | bytes 1179656 | tf_op jit(solution)/shard_map/ppermute | solution.py:34
  37.9 12.7 %collective-permute-start.10 = (bf16[3,512,128]{2,1,0:T(8,128)(2,1)S(1)}, bf16[3,512,128]{2,1,0:T(8,128)(2,1)S(1)}, u32[]{:S(2)}, u32[]{:S(2)}) collective-permute-start(bf16[3,512,128]{2,1,0:T(8,128)(2,1)S(1)} %collective-permute-done.8.refs_0_.refs_1_), channel_id=1, source_target_pairs={{0,1},{1,0},{2,3},{3,2},{4,5},{5,4},{6,7},{7,6},{8,9},{9,8},{10,11... | collective-permute-start | bytes 1179656 | tf_op jit(solution)/shard_map/ppermute | solution.py:34
  42.3 13.2 %collective-permute-start.13 = (bf16[3,512,128]{2,1,0:T(8,128)(2,1)S(1)}, bf16[3,512,128]{2,1,0:T(8,128)(2,1)S(1)}, u32[]{:S(2)}, u32[]{:S(2)}) collective-permute-start(bf16[3,512,128]{2,1,0:T(8,128)(2,1)S(1)} %collective-permute-done.11.refs_2_.refs_5_), channel_id=1, source_target_pairs={{0,2},{1,7},{2,4},{3,1},{4,6},{5,3},{6,0},{7,5},{8,10},{9,15},{10,... | collective-permute-start | bytes 1179656 | tf_op jit(solution)/shard_map/ppermute | solution.py:34
  55.5 91.6 %copy-start = (f32[4,2,2,3,3]{0,2,4,3,1:T(2,128)S(1)}, f32[4,2,2,3,3]{0,2,4,3,1:T(2,128)}, u32[]{:S(2)}) copy-start(f32[4,2,2,3,3]{0,2,4,3,1:T(2,128)} %param.6) | copy-start | bytes 1732
  55.5 91.9 %copy-start.2 = (f32[4,2]{0,1:T(2,128)S(1)}, f32[4,2]{0,1:T(2,128)}, u32[]{:S(2)}) copy-start(f32[4,2]{0,1:T(2,128)} %param.7) | copy-start | bytes 100
  60.7 73.4 %collective-permute-start.14 = (f32[2,3,16,128]{3,2,1,0:T(8,128)S(1)}, f32[2,3,16,128]{3,2,1,0:T(8,128)S(1)}, u32[]{:S(2)}, u32[]{:S(2)}) collective-permute-start(f32[2,3,16,128]{3,2,1,0:T(8,128)S(1)} %get-tuple-element.68), channel_id=1, source_target_pairs={{0,1},{1,0},{2,3},{3,2},{4,5},{5,4},{6,7},{7,6},{8,9},{9,8},{10,11... | collective-permute-start | bytes 147464 | tf_op jit(solution)/shard_map/ppermute | solution.py:34
  133.1 2.9 %collective-permute-start.15 = (f32[2,3,16,128]{3,2,1,0:T(8,128)S(1)}, f32[2,3,16,128]{3,2,1,0:T(8,128)S(1)}, u32[]{:S(2)}, u32[]{:S(2)}) collective-permute-start(f32[2,3,16,128]{3,2,1,0:T(8,128)S(1)} %get-tuple-element.70), channel_id=1, source_target_pairs={{0,2},{1,3},{2,0},{3,1},{4,6},{5,7},{6,4},{7,5},{8,10},{9,11},{10,... | collective-permute-start | bytes 147464 | tf_op jit(solution)/shard_map/ppermute | solution.py:34
  136.0 4.3 %collective-permute-start.16 = (f32[3,16,128]{2,1,0:T(8,128)S(1)}, f32[3,16,128]{2,1,0:T(8,128)S(1)}, u32[]{:S(2)}, u32[]{:S(2)}) collective-permute-start(f32[3,16,128]{2,1,0:T(8,128)S(1)} %get-tuple-element.72), channel_id=1, source_target_pairs={{0,8},{1,9},{2,10},{3,11},{4,12},{5,13},{6,14},{7,15},{8,0},{9,1},... | collective-permute-start | bytes 73736 | tf_op jit(solution)/shard_map/ppermute | solution.py:34
  136.2 4.1 %collective-permute-start.17 = (f32[3,16,128]{2,1,0:T(8,128)S(1)}, f32[3,16,128]{2,1,0:T(8,128)S(1)}, u32[]{:S(2)}, u32[]{:S(2)}) collective-permute-start(f32[3,16,128]{2,1,0:T(8,128)S(1)} %get-tuple-element.74), channel_id=1, source_target_pairs={{0,6},{1,7},{2,4},{3,5},{4,2},{5,3},{6,0},{7,1},{8,14},{9,15},{10,... | collective-permute-start | bytes 73736 | tf_op jit(solution)/shard_map/ppermute | solution.py:34
  140.3 8.8 %collective-permute-start.18 = (f32[3,2,2,4,128]{4,3,2,1,0:T(4,128)S(1)}, f32[3,2,2,4,128]{4,3,2,1,0:T(4,128)S(1)}, u32[]{:S(2)}, u32[]{:S(2)}) collective-permute-start(f32[3,2,2,4,128]{4,3,2,1,0:T(4,128)S(1)} %shard_map.53.own), channel_id=1, source_target_pairs={{0,0},{1,2},{2,1},{3,4},{4,3},{5,6},{6,5},{7,8},{8,7},{9,10},{10,9... | collective-permute-start | bytes 73736 | tf_op jit(solution)/shard_map/ppermute | solution.py:34
  146.9 2.2 %collective-permute-start.19 = (f32[3,2,2,4,128]{4,3,2,1,0:T(4,128)S(1)}, f32[3,2,2,4,128]{4,3,2,1,0:T(4,128)S(1)}, u32[]{:S(2)}, u32[]{:S(2)}) collective-permute-start(f32[3,2,2,4,128]{4,3,2,1,0:T(4,128)S(1)} %shard_map.53.own), channel_id=1, source_target_pairs={{0,1},{1,0},{2,3},{3,2},{4,5},{5,4},{6,7},{7,6},{8,9},{9,8},{10,11... | collective-permute-start | bytes 73736 | tf_op jit(solution)/shard_map/ppermute | solution.py:34

commit v5 on v4

--- a/solution.py
+++ b/solution.py
@@ -580,6 +580,23 @@
     )(weight.reshape(-1), bias.reshape(-1), chip, own, core)
 
 
+def split_kernel(whole, first, second):
+    cut = first.shape[1]
+    first[...] = whole[:, :cut]
+    second[...] = whole[:, cut:]
+
+
+def split(whole, cut):
+    frames, cells, chans = whole.shape
+    return pl.pallas_call(
+        split_kernel,
+        out_shape=[jax.ShapeDtypeStruct((frames, size, chans), whole.dtype) for size in (cut, cells - cut)],
+        in_specs=[VMEM],
+        out_specs=[VMEM, VMEM],
+        compiler_params=pltpu.CompilerParams(vmem_limit_bytes=4 << 20),
+    )(whole)
+
+
 def gather_frames(blocks, table):
     orders = (
         (by_core(flip_y, flip_b), by_core(flip_a, flip_y), by_core(flip_b, flip_a)),
@@ -614,8 +631,7 @@
     frames, band_rows, width, chans = features.shape
     cells = band_rows * width
     flat_features = features.reshape(frames, cells, chans)
-    cut = cells * 11 // 16
-    src0, tgt0 = gather_frames([flat_features[:, :cut], flat_features[:, cut:]], frame_pairs)
+    src0, tgt0 = gather_frames(split(flat_features, cells * 19 // 32), frame_pairs)
     fwd_keep, fwd_send, rev_keep, rev_send = matched(src0, tgt0)
     fwd0, fwd1, rev0, rev1 = half(fwd_keep, hop(fwd_send, flip_c), rev_keep, hop(rev_send, flip_za), band_rows)
     flows = merge(fwd0, hop(fwd1, flip_h), rev0, hop(rev1, flip_zb), band_rows, width)

time: 154 us -> 155 us (level)
  waiting for transfers between devices: 30.3 us -> 32.3 us
    ppermute x20, waiting for transfers between devices: 30.3 us -> 32.3 us  [hop(): return lax.ppermute(value, AXES, route)]
    slice x2 -> x0, local copies, waits for them, and re-layouts: 1.89 us -> none  [the longest x1 0.98 us: shards(): flat_features[:, :cut]]
  transfers between devices with their start and end apart: 20 -> 20, of which waited for: 10 -> 11; matrix products, arithmetic and copies ran while one was open for 1% -> 0% of each run, Pallas kernels for 7% -> 7%
where the time goes in v5:
time: 155 us; the launch traced here: 152 us
  starting transfers between devices  97.9 us (63%)
  waiting for transfers between devices  32.3 us (21%)
  Pallas kernels  19.5 us (13%)
  local copies, waits for them, and re-layouts  1.62 us (1%)
    ppermute x20, starting transfers between devices, hop(): return lax.ppermute(value, AXES, route)  97.9 us
    ppermute x20, waiting for transfers between devices, hop(): return lax.ppermute(value, AXES, route)  32.3 us
    pallas_call x3, Pallas kernels, match_early(): pl.pallas_call(functools.partial(early_kernel, which=which, bands=bands,...  10.1 us
    pallas_call x1, Pallas kernels, match_late(): pl.pallas_call(functools.partial(late_kernel, nsrc=nsrc, ntgt=ntgt, cells...  5.21 us
  transfers between devices with their start and end apart: 20, of which 11 were waited for; matrix products, arithmetic and copies ran while one was open for 0% of the time, Pallas kernels for 7%

profile of v5, /device:TPU:97, one launch (start us, length us, event | category | flops | bytes accessed | tf_op | source)
XLA Modules:
  0.0 151.6 jit_solution(7135190576711791651)
XLA Ops:
  0.0 1.0 copy-done
  1.0 2.6 %collective-permute-start = (bf16[3,304,128]{2,1,0:T(8,128)(2,1)S(1)}, bf16[3,304,128]{2,1,0:T(8,128)(2,1)S(1)}, u32[]{:S(2)}, u32[]{:S(2)}) collective-permute-start(bf16[3,304,128]{2,1,0:T(8,128)(2,1)S(1)} %get-tuple-element.42.refs_2_.refs_0_), channel_id=1, source_target_pairs={{0,16},{1,97},{2,18},{3,99},{4,20},{5,101},{6,22},{7,103},{8,24},{... | collective-permute-start | bytes 700424 | tf_op jit(solution)/shard_map/ppermute | solution.py:34
  3.6 5.9 %collective-permute-done.1.refs_6_.refs_5_ = bf16[3,208,128]{2,1,0:T(8,128)(2,1)S(1)} collective-permute-done((bf16[3,208,128]{2,1,0:T(8,128)(2,1)S(1)}, bf16[3,208,128]{2,1,0:T(8,128)(2,1)S(1)}, u32[]{:S(2)}, u32[]{:S(2)}) %collective-permute-start.1) | collective-permute-done | bytes 159776 | tf_op jit(solution)/shard_map/ppermute | solution.py:34
  9.5 0.4 collective-permute-start.2
  10.0 1.3 collective-permute-start.3
  11.4 0.2 collective-permute-start.5
  11.6 2.5 %collective-permute-done.4.refs_0_ = s32[3,2]{1,0:T(4,128)S(1)} collective-permute-done((s32[3,2]{1,0:T(4,128)S(1)}, s32[3,2]{1,0:T(4,128)S(1)}, u32[]{:S(2)}, u32[]{:S(2)}) %collective-permute-start.4) | collective-permute-done | bytes 56 | tf_op jit(solution)/shard_map/ppermute | solution.py:34
  14.1 3.3 %collective-permute-done.5.refs_1_ = s32[3,2]{1,0:T(4,128)S(1)} collective-permute-done((s32[3,2]{1,0:T(4,128)S(1)}, s32[3,2]{1,0:T(4,128)S(1)}, u32[]{:S(2)}, u32[]{:S(2)}) %collective-permute-start.5) | collective-permute-done | bytes 56 | tf_op jit(solution)/shard_map/ppermute | solution.py:34
  17.4 2.4 %collective-permute-done.3.refs_7_.refs_6_ = bf16[6,208,128]{2,1,0:T(8,128)(2,1)S(1)} collective-permute-done((bf16[6,208,128]{2,1,0:T(8,128)(2,1)S(1)}, bf16[6,208,128]{2,1,0:T(8,128)(2,1)S(1)}, u32[]{:S(2)}, u32[]{:S(2)}) %collective-permute-start.3) | collective-permute-done | bytes 319520 | tf_op jit(solution)/shard_map/ppermute | solution.py:34
  19.8 1.1 shard_map.47
  21.1 1.0 collective-permute-start.7
  22.1 5.3 %collective-permute-done.7.refs_7_ = bf16[6,208,128]{2,1,0:T(8,128)(2,1)S(1)} collective-permute-done((bf16[6,208,128]{2,1,0:T(8,128)(2,1)S(1)}, bf16[6,208,128]{2,1,0:T(8,128)(2,1)S(1)}, u32[]{:S(2)}, u32[]{:S(2)}) %collective-permute-start.7) | collective-permute-done | bytes 319520 | tf_op jit(solution)/shard_map/ppermute | solution.py:34
  27.4 1.3 collective-permute-done.6.refs_3_
  28.8 1.1 shard_map.48
  29.8 3.0 %collective-permute-start.8 = (bf16[3,512,128]{2,1,0:T(8,128)(2,1)S(1)}, bf16[3,512,128]{2,1,0:T(8,128)(2,1)S(1)}, u32[]{:S(2)}, u32[]{:S(2)}) collective-permute-start(bf16[3,512,128]{2,1,0:T(8,128)(2,1)S(1)} %get-tuple-element.52.refs_0_), channel_id=1, source_target_pairs={{0,8},{1,9},{2,10},{3,11},{4,12},{5,13},{6,14},{7,15},{8,0},{9,1},... | collective-permute-start | bytes 1179656 | tf_op jit(solution)/shard_map/ppermute | solution.py:34
  32.9 3.7 %collective-permute-start.9 = (bf16[3,512,128]{2,1,0:T(8,128)(2,1)S(1)}, bf16[3,512,128]{2,1,0:T(8,128)(2,1)S(1)}, u32[]{:S(2)}, u32[]{:S(2)}) collective-permute-start(bf16[3,512,128]{2,1,0:T(8,128)(2,1)S(1)} %get-tuple-element.52.refs_0_), channel_id=1, source_target_pairs={{0,1},{1,0},{2,3},{3,2},{4,5},{5,4},{6,7},{7,6},{8,9},{9,8},{10,11... | collective-permute-start | bytes 1179656 | tf_op jit(solution)/shard_map/ppermute | solution.py:34
  36.6 0.8 collective-permute-start.12
  37.5 1.1 collective-permute-done.8.refs_0_.refs_1_
  38.6 4.4 %collective-permute-start.10 = (bf16[3,512,128]{2,1,0:T(8,128)(2,1)S(1)}, bf16[3,512,128]{2,1,0:T(8,128)(2,1)S(1)}, u32[]{:S(2)}, u32[]{:S(2)}) collective-permute-start(bf16[3,512,128]{2,1,0:T(8,128)(2,1)S(1)} %collective-permute-done.8.refs_0_.refs_1_), channel_id=1, source_target_pairs={{0,1},{1,0},{2,3},{3,2},{4,5},{5,4},{6,7},{7,6},{8,9},{9,8},{10,11... | collective-permute-start | bytes 1179656 | tf_op jit(solution)/shard_map/ppermute | solution.py:34
  43.1 1.9 %shard_map.49 = (f32[3,1024,128]{2,1,0:T(8,128)S(1)}, f32[3,1024,128]{2,1,0:T(8,128)S(1)}, f32[3,1,8,512]{3,2,1,0:T(8,128)S(1)}, f32[3,1,8,512]{3,2,1,0:T(8,128)...) custom-call(bf16[3,512,128]{2,1,0:T(8,128)(2,1)S(1)} %get-tuple-element.52.refs_0_, ...), custom_call_target="tpu_custom_call" | custom-call | flops 804000000 | bytes 600000 | tf_op jit(solution)/shard_map/pallas_call | solution.py:440
  45.0 2.9 %collective-permute-done.12.refs_3_.refs_6_ = bf16[3,512,128]{2,1,0:T(8,128)(2,1)S(1)} collective-permute-done((bf16[3,512,128]{2,1,0:T(8,128)(2,1)S(1)}, bf16[3,512,128]{2,1,0:T(8,128)(2,1)S(1)}, u32[]{:S(2)}, u32[]{:S(2)}) %collective-permute-start.12) | collective-permute-done | bytes 393248 | tf_op jit(solution)/shard_map/ppermute | solution.py:34
  47.9 3.4 %shard_map.50 = (f32[3,1024,128]{2,1,0:T(8,128)S(1)}, f32[3,1024,128]{2,1,0:T(8,128)S(1)}, f32[3,2,8,512]{3,2,1,0:T(8,128)S(1)}, f32[3,2,8,512]{3,2,1,0:T(8,128)...) custom-call(bf16[3,512,128]{2,1,0:T(8,128)(2,1)S(1)} %get-tuple-element.52.refs_0_, ...), custom_call_target="tpu_custom_call" | custom-call | flops 1608000000 | bytes 1200000 | tf_op jit(solution)/shard_map/pallas_call | solution.py:440
  51.3 4.8 %shard_map.51 = (f32[3,1024,128]{2,1,0:T(8,128)S(1)}, f32[3,1024,128]{2,1,0:T(8,128)S(1)}, f32[3,3,8,512]{3,2,1,0:T(8,128)S(1)}, f32[3,3,8,512]{3,2,1,0:T(8,128)S(1)}, f32[3,3,8,512]{3,2,1,0:T(8,128)S(1)}) custom-call(bf16[3,512,128]{2,1,0:T(8,128)(2,1)S(1)} %collective-permute-done.8.refs_0_.refs_1_, ...), custom_call_target="tpu_custom_call" | custom-call | flops 2412000000 | bytes 1800000 | tf_op jit(solution)/shard_map/pallas_call | solution.py:440
  56.1 5.2 %shard_map.52 = (f32[2,3,16,128]{3,2,1,0:T(8,128)S(1)}, f32[2,3,16,128]{3,2,1,0:T(8,128)S(1)}, f32[2,3,16,128]{3,2,1,0:T(8,128)S(1)}, f32[2,3,16,128]{3,2,1,0:T(8,128)S(1)}) custom-call(bf16[3,512,128]{2,1,0:T(8,128)(2,1)S(1)} %get-tuple-element.52.refs_0_, bf16[3,512,128]{2,1,0:T(8,128)(2,1)S(1)} %collective-permute-done.8.refs_0_.refs_1_, ...), custom_call_target="tpu_custom_call" | custom-call | flops 1608000000 | bytes 1200000 | tf_op jit(solution)/shard_map/pallas_call | solution.py:455
  61.4 72.4 %collective-permute-start.14 = (f32[2,3,16,128]{3,2,1,0:T(8,128)S(1)}, f32[2,3,16,128]{3,2,1,0:T(8,128)S(1)}, u32[]{:S(2)}, u32[]{:S(2)}) collective-permute-start(f32[2,3,16,128]{3,2,1,0:T(8,128)S(1)} %get-tuple-element.72), channel_id=1, source_target_pairs={{0,1},{1,0},{2,3},{3,2},{4,5},{5,4},{6,7},{7,6},{8,9},{9,8},{10,11... | collective-permute-start | bytes 147464 | tf_op jit(solution)/shard_map/ppermute | solution.py:34
  133.7 1.0 collective-permute-start.15
  134.7 1.9 %collective-permute-done.15.rev_in = f32[2,3,16,128]{3,2,1,0:T(8,128)S(1)} collective-permute-done((f32[2,3,16,128]{3,2,1,0:T(8,128)S(1)}, f32[2,3,16,128]{3,2,1,0:T(8,128)S(1)}, u32[]{:S(2)}, u32[]{:S(2)}) %collective-permute-start.15) | collective-permute-done | bytes 49184 | tf_op jit(solution)/shard_map/ppermute | solution.py:34
  136.9 4.1 %collective-permute-done.16.fwd_in = f32[3,16,128]{2,1,0:T(8,128)S(1)} collective-permute-done((f32[3,16,128]{2,1,0:T(8,128)S(1)}, f32[3,16,128]{2,1,0:T(8,128)S(1)}, u32[]{:S(2)}, u32[]{:S(2)}) %collective-permute-start.16) | collective-permute-done | bytes 24608 | tf_op jit(solution)/shard_map/ppermute | solution.py:34
  141.0 6.6 %collective-permute-start.18 = (f32[3,2,2,4,128]{4,3,2,1,0:T(4,128)S(1)}, f32[3,2,2,4,128]{4,3,2,1,0:T(4,128)S(1)}, u32[]{:S(2)}, u32[]{:S(2)}) collective-permute-start(f32[3,2,2,4,128]{4,3,2,1,0:T(4,128)S(1)} %shard_map.54.own), channel_id=1, source_target_pairs={{0,0},{1,2},{2,1},{3,4},{4,3},{5,6},{6,5},{7,8},{8,7},{9,10},{10,9... | collective-permute-start | bytes 73736 | tf_op jit(solution)/shard_map/ppermute | solution.py:34
  147.7 0.2 copy.9
  148.2 1.6 %collective-permute-done.18.chip = f32[3,2,2,4,128]{4,3,2,1,0:T(4,128)S(1)} collective-permute-done((f32[3,2,2,4,128]{4,3,2,1,0:T(4,128)S(1)}, f32[3,2,2,4,128]{4,3,2,1,0:T(4,128)S(1)}, u32[]{:S(2)}, u32[]{:S(2)}) %collective-permute-start.18) | collective-permute-done | bytes 24608 | tf_op jit(solution)/shard_map/ppermute | solution.py:34
  149.8 1.9 %shard_map.55 = f32[3,2,2,4,128]{4,3,2,1,0:T(4,128)} custom-call(f32[144]{0:T(256)S(1)} %reshape.9.weight, f32[8]{0:T(128)S(1)} %reshape.10.bias, f32[3,2,2,4,128]{4,3,2,1,0:T(4,128)S(1)} %collective-permute-done.18.chip, f32[3,2,2,4,128]{4,3,2,1,0:T(4,128)S(1)} %shard_map.54.own, f32[3,2,2,4,128]{4,3,2,1,0:T(4,128)S(1)} %collective-permute-done.19.core), custom_call_target="tpu_custom_call" | custom-call | tf_op jit(solution)/shard_map/pallas_call | solution.py:573
  (33 shorter events, 1.2 us)
Async XLA Ops:
  0.0 11.3 %copy-start.2 = (s32[3,2]{0,1:T(2,128)S(1)}, s32[3,2]{0,1:T(2,128)}, u32[]{:S(2)}) copy-start(s32[3,2]{0,1:T(2,128)} %param.5) | copy-start | bytes 76
  0.0 1.0 copy-start
  1.0 8.5 %collective-permute-start = (bf16[3,304,128]{2,1,0:T(8,128)(2,1)S(1)}, bf16[3,304,128]{2,1,0:T(8,128)(2,1)S(1)}, u32[]{:S(2)}, u32[]{:S(2)}) collective-permute-start(bf16[3,304,128]{2,1,0:T(8,128)(2,1)S(1)} %get-tuple-element.42.refs_2_.refs_0_), channel_id=1, source_target_pairs={{0,16},{1,97},{2,18},{3,99},{4,20},{5,101},{6,22},{7,103},{8,24},{... | collective-permute-start | bytes 700424 | tf_op jit(solution)/shard_map/ppermute | solution.py:34
  3.6 5.9 %collective-permute-start.1 = (bf16[3,208,128]{2,1,0:T(8,128)(2,1)S(1)}, bf16[3,208,128]{2,1,0:T(8,128)(2,1)S(1)}, u32[]{:S(2)}, u32[]{:S(2)}) collective-permute-start(bf16[3,208,128]{2,1,0:T(8,128)(2,1)S(1)} %get-tuple-element.43.refs_5_.refs_4_), channel_id=1, source_target_pairs={{0,32},{1,33},{2,34},{3,35},{4,36},{5,37},{6,38},{7,39},{8,40},{9,... | collective-permute-start | bytes 479240 | tf_op jit(solution)/shard_map/ppermute | solution.py:34
  9.5 10.3 %collective-permute-start.2 = (bf16[6,304,128]{2,1,0:T(8,128)(2,1)S(1)}, bf16[6,304,128]{2,1,0:T(8,128)(2,1)S(1)}, u32[]{:S(2)}, u32[]{:S(2)}) collective-permute-start(bf16[6,304,128]{2,1,0:T(8,128)(2,1)S(1)} %pad_maximum_fusion), channel_id=1, source_target_pairs={{0,32},{1,17},{2,34},{3,19},{4,36},{5,21},{6,38},{7,23},{8,40},{9,... | collective-permute-start | bytes 1400840 | tf_op jit(solution)/shard_map/ppermute | solution.py:34
  10.0 9.8 %collective-permute-start.3 = (bf16[6,208,128]{2,1,0:T(8,128)(2,1)S(1)}, bf16[6,208,128]{2,1,0:T(8,128)(2,1)S(1)}, u32[]{:S(2)}, u32[]{:S(2)}) collective-permute-start(bf16[6,208,128]{2,1,0:T(8,128)(2,1)S(1)} %pad_maximum_fusion.1), channel_id=1, source_target_pairs={{0,96},{1,97},{2,98},{3,99},{4,100},{5,101},{6,102},{7,103},{8,104... | collective-permute-start | bytes 958472 | tf_op jit(solution)/shard_map/ppermute | solution.py:34
  11.4 2.7 %collective-permute-start.4 = (s32[3,2]{1,0:T(4,128)S(1)}, s32[3,2]{1,0:T(4,128)S(1)}, u32[]{:S(2)}, u32[]{:S(2)}) collective-permute-start(s32[3,2]{1,0:T(4,128)S(1)} %copy.13.table), channel_id=1, source_target_pairs={{0,96},{1,33},{2,98},{3,35},{4,100},{5,37},{6,102},{7,39},{8,104},... | collective-permute-start | bytes 80 | tf_op jit(solution)/shard_map/ppermute | solution.py:34
  11.4 6.0 %collective-permute-start.5 = (s32[3,2]{1,0:T(4,128)S(1)}, s32[3,2]{1,0:T(4,128)S(1)}, u32[]{:S(2)}, u32[]{:S(2)}) collective-permute-start(s32[3,2]{1,0:T(4,128)S(1)} %copy.13.table), channel_id=1, source_target_pairs={{0,16},{1,17},{2,18},{3,19},{4,20},{5,21},{6,22},{7,23},{8,24},{9,... | collective-permute-start | bytes 80 | tf_op jit(solution)/shard_map/ppermute | solution.py:34
  21.0 7.8 %collective-permute-start.6 = (bf16[6,304,128]{2,1,0:T(8,128)(2,1)S(1)}, bf16[6,304,128]{2,1,0:T(8,128)(2,1)S(1)}, u32[]{:S(2)}, u32[]{:S(2)}) collective-permute-start(bf16[6,304,128]{2,1,0:T(8,128)(2,1)S(1)} %get-tuple-element.50), channel_id=1, source_target_pairs={{0,96},{1,33},{2,98},{3,35},{4,100},{5,37},{6,102},{7,39},{8,104},... | collective-permute-start | bytes 1400840 | tf_op jit(solution)/shard_map/ppermute | solution.py:34
  21.1 6.3 %collective-permute-start.7 = (bf16[6,208,128]{2,1,0:T(8,128)(2,1)S(1)}, bf16[6,208,128]{2,1,0:T(8,128)(2,1)S(1)}, u32[]{:S(2)}, u32[]{:S(2)}) collective-permute-start(bf16[6,208,128]{2,1,0:T(8,128)(2,1)S(1)} %get-tuple-element.51), channel_id=1, source_target_pairs={{0,16},{1,17},{2,18},{3,19},{4,20},{5,21},{6,22},{7,23},{8,24},{9,... | collective-permute-start | bytes 958472 | tf_op jit(solution)/shard_map/ppermute | solution.py:34
  29.8 8.7 %collective-permute-start.8 = (bf16[3,512,128]{2,1,0:T(8,128)(2,1)S(1)}, bf16[3,512,128]{2,1,0:T(8,128)(2,1)S(1)}, u32[]{:S(2)}, u32[]{:S(2)}) collective-permute-start(bf16[3,512,128]{2,1,0:T(8,128)(2,1)S(1)} %get-tuple-element.52.refs_0_), channel_id=1, source_target_pairs={{0,8},{1,9},{2,10},{3,11},{4,12},{5,13},{6,14},{7,15},{8,0},{9,1},... | collective-permute-start | bytes 1179656 | tf_op jit(solution)/shard_map/ppermute | solution.py:34
  32.8 10.1 %collective-permute-start.11 = (bf16[3,512,128]{2,1,0:T(8,128)(2,1)S(1)}, bf16[3,512,128]{2,1,0:T(8,128)(2,1)S(1)}, u32[]{:S(2)}, u32[]{:S(2)}) collective-permute-start(bf16[3,512,128]{2,1,0:T(8,128)(2,1)S(1)} %get-tuple-element.53.refs_2_.refs_4_), channel_id=1, source_target_pairs={{0,2},{1,7},{2,4},{3,1},{4,6},{5,3},{6,0},{7,5},{8,10},{9,15},{10,... | collective-permute-start | bytes 1179656 | tf_op jit(solution)/shard_map/ppermute | solution.py:34
  32.9 10.1 %collective-permute-start.9 = (bf16[3,512,128]{2,1,0:T(8,128)(2,1)S(1)}, bf16[3,512,128]{2,1,0:T(8,128)(2,1)S(1)}, u32[]{:S(2)}, u32[]{:S(2)}) collective-permute-start(bf16[3,512,128]{2,1,0:T(8,128)(2,1)S(1)} %get-tuple-element.52.refs_0_), channel_id=1, source_target_pairs={{0,1},{1,0},{2,3},{3,2},{4,5},{5,4},{6,7},{7,6},{8,9},{9,8},{10,11... | collective-permute-start | bytes 1179656 | tf_op jit(solution)/shard_map/ppermute | solution.py:34
  36.6 11.2 %collective-permute-start.12 = (bf16[3,512,128]{2,1,0:T(8,128)(2,1)S(1)}, bf16[3,512,128]{2,1,0:T(8,128)(2,1)S(1)}, u32[]{:S(2)}, u32[]{:S(2)}) collective-permute-start(bf16[3,512,128]{2,1,0:T(8,128)(2,1)S(1)} %get-tuple-element.53.refs_2_.refs_4_), channel_id=1, source_target_pairs={{0,6},{1,3},{2,0},{3,5},{4,2},{5,7},{6,4},{7,1},{8,14},{9,11},{10,... | collective-permute-start | bytes 1179656 | tf_op jit(solution)/shard_map/ppermute | solution.py:34
  38.6 12.7 %collective-permute-start.10 = (bf16[3,512,128]{2,1,0:T(8,128)(2,1)S(1)}, bf16[3,512,128]{2,1,0:T(8,128)(2,1)S(1)}, u32[]{:S(2)}, u32[]{:S(2)}) collective-permute-start(bf16[3,512,128]{2,1,0:T(8,128)(2,1)S(1)} %collective-permute-done.8.refs_0_.refs_1_), channel_id=1, source_target_pairs={{0,1},{1,0},{2,3},{3,2},{4,5},{5,4},{6,7},{7,6},{8,9},{9,8},{10,11... | collective-permute-start | bytes 1179656 | tf_op jit(solution)/shard_map/ppermute | solution.py:34
  42.9 13.2 %collective-permute-start.13 = (bf16[3,512,128]{2,1,0:T(8,128)(2,1)S(1)}, bf16[3,512,128]{2,1,0:T(8,128)(2,1)S(1)}, u32[]{:S(2)}, u32[]{:S(2)}) collective-permute-start(bf16[3,512,128]{2,1,0:T(8,128)(2,1)S(1)} %collective-permute-done.11.refs_2_.refs_5_), channel_id=1, source_target_pairs={{0,2},{1,7},{2,4},{3,1},{4,6},{5,3},{6,0},{7,5},{8,10},{9,15},{10,... | collective-permute-start | bytes 1179656 | tf_op jit(solution)/shard_map/ppermute | solution.py:34
  56.1 91.6 %copy-start.1 = (f32[4,2,2,3,3]{0,2,4,3,1:T(2,128)S(1)}, f32[4,2,2,3,3]{0,2,4,3,1:T(2,128)}, u32[]{:S(2)}) copy-start(f32[4,2,2,3,3]{0,2,4,3,1:T(2,128)} %param.6) | copy-start | bytes 1732
  56.1 91.9 %copy-start.3 = (f32[4,2]{0,1:T(2,128)S(1)}, f32[4,2]{0,1:T(2,128)}, u32[]{:S(2)}) copy-start(f32[4,2]{0,1:T(2,128)} %param.7) | copy-start | bytes 100
  61.4 73.4 %collective-permute-start.14 = (f32[2,3,16,128]{3,2,1,0:T(8,128)S(1)}, f32[2,3,16,128]{3,2,1,0:T(8,128)S(1)}, u32[]{:S(2)}, u32[]{:S(2)}) collective-permute-start(f32[2,3,16,128]{3,2,1,0:T(8,128)S(1)} %get-tuple-element.72), channel_id=1, source_target_pairs={{0,1},{1,0},{2,3},{3,2},{4,5},{5,4},{6,7},{7,6},{8,9},{9,8},{10,11... | collective-permute-start | bytes 147464 | tf_op jit(solution)/shard_map/ppermute | solution.py:34
  133.7 2.9 %collective-permute-start.15 = (f32[2,3,16,128]{3,2,1,0:T(8,128)S(1)}, f32[2,3,16,128]{3,2,1,0:T(8,128)S(1)}, u32[]{:S(2)}, u32[]{:S(2)}) collective-permute-start(f32[2,3,16,128]{3,2,1,0:T(8,128)S(1)} %get-tuple-element.74), channel_id=1, source_target_pairs={{0,2},{1,3},{2,0},{3,1},{4,6},{5,7},{6,4},{7,5},{8,10},{9,11},{10,... | collective-permute-start | bytes 147464 | tf_op jit(solution)/shard_map/ppermute | solution.py:34
  136.7 4.3 %collective-permute-start.16 = (f32[3,16,128]{2,1,0:T(8,128)S(1)}, f32[3,16,128]{2,1,0:T(8,128)S(1)}, u32[]{:S(2)}, u32[]{:S(2)}) collective-permute-start(f32[3,16,128]{2,1,0:T(8,128)S(1)} %get-tuple-element.76), channel_id=1, source_target_pairs={{0,8},{1,9},{2,10},{3,11},{4,12},{5,13},{6,14},{7,15},{8,0},{9,1},... | collective-permute-start | bytes 73736 | tf_op jit(solution)/shard_map/ppermute | solution.py:34
  136.8 4.1 %collective-permute-start.17 = (f32[3,16,128]{2,1,0:T(8,128)S(1)}, f32[3,16,128]{2,1,0:T(8,128)S(1)}, u32[]{:S(2)}, u32[]{:S(2)}) collective-permute-start(f32[3,16,128]{2,1,0:T(8,128)S(1)} %get-tuple-element.78), channel_id=1, source_target_pairs={{0,6},{1,7},{2,4},{3,5},{4,2},{5,3},{6,0},{7,1},{8,14},{9,15},{10,... | collective-permute-start | bytes 73736 | tf_op jit(solution)/shard_map/ppermute | solution.py:34
  141.0 8.8 %collective-permute-start.18 = (f32[3,2,2,4,128]{4,3,2,1,0:T(4,128)S(1)}, f32[3,2,2,4,128]{4,3,2,1,0:T(4,128)S(1)}, u32[]{:S(2)}, u32[]{:S(2)}) collective-permute-start(f32[3,2,2,4,128]{4,3,2,1,0:T(4,128)S(1)} %shard_map.54.own), channel_id=1, source_target_pairs={{0,0},{1,2},{2,1},{3,4},{4,3},{5,6},{6,5},{7,8},{8,7},{9,10},{10,9... | collective-permute-start | bytes 73736 | tf_op jit(solution)/shard_map/ppermute | solution.py:34
  147.6 2.2 %collective-permute-start.19 = (f32[3,2,2,4,128]{4,3,2,1,0:T(4,128)S(1)}, f32[3,2,2,4,128]{4,3,2,1,0:T(4,128)S(1)}, u32[]{:S(2)}, u32[]{:S(2)}) collective-permute-start(f32[3,2,2,4,128]{4,3,2,1,0:T(4,128)S(1)} %shard_map.54.own), channel_id=1, source_target_pairs={{0,1},{1,0},{2,3},{3,2},{4,5},{5,4},{6,7},{7,6},{8,9},{9,8},{10,11... | collective-permute-start | bytes 73736 | tf_op jit(solution)/shard_map/ppermute | solution.py:34

commit v6 on v5

--- a/solution.py
+++ b/solution.py
@@ -100,17 +100,16 @@
 
 
 def copy_held(pieces, bits, which, frames, take, also=True):
-    place = bits[0] + 2 * bits[1]
-    for piece, low, span in zip(pieces, (0, 1, 2), (1, 1, 2)):
-
-        @pl.when((place >= low) & (place < low + span) & also)
+    for side, piece in enumerate(pieces):
+
+        @pl.when((bits[1] == side) & also)
         def _():
-            take(piece[(place - low) * frames + which])
+            take(piece[bits[0] * frames + which])
 
 
 def offer_kernel(*refs, parts):
-    tables, pieces, outs = refs[:parts], refs[parts : 4 * parts], refs[4 * parts :]
-    frames = pieces[0].shape[0]
+    tables, pieces, outs = refs[:parts], refs[parts : 3 * parts], refs[3 * parts :]
+    frames = pieces[0].shape[0] // 2
     for v in range(parts):
         for slot in range(tables[v].shape[0]):
             for side in range(2):
@@ -119,7 +118,7 @@
                 def take(value):
                     outs[v][2 * slot + side] = value
 
-                copy_held(pieces[3 * v : 3 * v + 3], seats[v], which, frames, take)
+                copy_held(pieces[2 * v : 2 * v + 2], seats[v], which, frames, take)
 
 
 def offer(tables, held):
@@ -135,23 +134,23 @@
 
 
 def pick_kernel(table, *refs, parts):
-    pieces, outs = refs[: 4 * parts], refs[4 * parts :]
-    frames = pieces[0].shape[0]
+    pieces, outs = refs[: 3 * parts], refs[3 * parts :]
+    frames = pieces[0].shape[0] // 2
     for slot in range(table.shape[0]):
         for side in range(2):
             seats, which = seat(table[slot, side], frames)
             start = 0
             for v in range(parts):
-                count = pieces[4 * v].shape[1]
+                count = pieces[3 * v].shape[1]
 
                 def take(value):
                     outs[side][slot, start : start + count] = value
 
-                copy_held(pieces[4 * v : 4 * v + 3], seats[v], which, frames, take, seats[v][2] == 0)
+                copy_held(pieces[3 * v : 3 * v + 2], seats[v], which, frames, take, seats[v][2] == 0)
 
                 @pl.when(seats[v][2] == 1)
                 def _():
-                    take(pieces[4 * v + 3][2 * slot + side])
+                    take(pieces[3 * v + 2][2 * slot + side])
 
                 start += count
 
@@ -603,12 +602,11 @@
         (flip_a, flip_b, flip_y),
     )
     first = lax.optimization_barrier([hop(block, order[0]) for block, order in zip(blocks, orders)])
-    held = [[block, piece] for block, piece in zip(blocks, first)]
-    send = [jnp.concatenate(have, axis=0) for have in held]
+    send = [jnp.concatenate(both, axis=0) for both in zip(blocks, first)]
     second = [hop(part, order[1]) for part, order in zip(send, orders)]
     tables = [hop(table, order[2]) for order in orders]
     second, tables = lax.optimization_barrier((second, tables))
-    held = [have + [piece] for have, piece in zip(held, second)]
+    held = [[part, piece] for part, piece in zip(send, second)]
     sent = [hop(part, order[2]) for part, order in zip(offer(tables, held), orders)]
     return pick(table, [have + [piece] for have, piece in zip(held, sent)])
 
@@ -631,12 +629,12 @@
     frames, band_rows, width, chans = features.shape
     cells = band_rows * width
     flat_features = features.reshape(frames, cells, chans)
-    src0, tgt0 = gather_frames(split(flat_features, cells * 19 // 32), frame_pairs)
+    src0, tgt0 = gather_frames(split(flat_features, cells * 11 // 16), frame_pairs)
     fwd_keep, fwd_send, rev_keep, rev_send = matched(src0, tgt0)
     fwd0, fwd1, rev0, rev1 = half(fwd_keep, hop(fwd_send, flip_c), rev_keep, hop(rev_send, flip_za), band_rows)
     flows = merge(fwd0, hop(fwd1, flip_h), rev0, hop(rev1, flip_zb), band_rows, width)
+    core = hop(flows, flip_c)
     chip = hop(flows, next_chip)
-    core = hop(flows, flip_c)
     return refine(conv_weight, conv_bias, chip, flows, core)
 
 

time: 155 us -> 153 us (0.987)
  waiting for transfers between devices: 32.3 us -> 29.5 us
    ppermute x20, waiting for transfers between devices: 32.3 us -> 29.5 us  [hop(): return lax.ppermute(value, AXES, route)]
where the time goes in v6:
time: 153 us; the launch traced here: 150 us
  starting transfers between devices  99.2 us (65%)
  waiting for transfers between devices  29.5 us (19%)
  Pallas kernels  19.3 us (13%)
  local copies, waits for them, and re-layouts  1.7 us (1%)
    ppermute x20, starting transfers between devices, hop(): return lax.ppermute(value, AXES, route)  99.2 us
    ppermute x20, waiting for transfers between devices, hop(): return lax.ppermute(value, AXES, route)  29.5 us
    pallas_call x3, Pallas kernels, match_early(): pl.pallas_call(functools.partial(early_kernel, which=which, bands=bands,...  10.2 us
    pallas_call x1, Pallas kernels, match_late(): pl.pallas_call(functools.partial(late_kernel, nsrc=nsrc, ntgt=ntgt, cells...  5.21 us
  transfers between devices with their start and end apart: 20, of which 11 were waited for; matrix products, arithmetic and copies ran while one was open for 0% of the time, Pallas kernels for 7%

profile of v6, /device:TPU:97, one launch (start us, length us, event | category | flops | bytes accessed | tf_op | source)
XLA Modules:
  0.0 149.8 jit_solution(2722572808325019361)
XLA Ops:
  0.0 1.0 copy-done
  1.0 2.6 %collective-permute-start = (bf16[3,352,128]{2,1,0:T(8,128)(2,1)S(1)}, bf16[3,352,128]{2,1,0:T(8,128)(2,1)S(1)}, u32[]{:S(2)}, u32[]{:S(2)}) collective-permute-start(bf16[3,352,128]{2,1,0:T(8,128)(2,1)S(1)} %get-tuple-element.42), channel_id=1, source_target_pairs={{0,16},{1,97},{2,18},{3,99},{4,20},{5,101},{6,22},{7,103},{8,24},{... | collective-permute-start | bytes 811016 | tf_op jit(solution)/shard_map/ppermute | solution.py:34
  3.6 5.1 %collective-permute-done.1 = bf16[3,160,128]{2,1,0:T(8,128)(2,1)S(1)} collective-permute-done((bf16[3,160,128]{2,1,0:T(8,128)(2,1)S(1)}, bf16[3,160,128]{2,1,0:T(8,128)(2,1)S(1)}, u32[]{:S(2)}, u32[]{:S(2)}) %collective-permute-start.1) | collective-permute-done | bytes 122912 | tf_op jit(solution)/shard_map/ppermute | solution.py:34
  8.8 0.5 collective-permute-start.2
  9.3 2.3 %collective-permute-start.3 = (bf16[6,160,128]{2,1,0:T(8,128)(2,1)S(1)}, bf16[6,160,128]{2,1,0:T(8,128)(2,1)S(1)}, u32[]{:S(2)}, u32[]{:S(2)}) collective-permute-start(bf16[6,160,128]{2,1,0:T(8,128)(2,1)S(1)} %constant_dynamic-update-slice_fusion.2.refs_4_.refs_3_), channel_id=1, source_target_pairs={{0,96},{1,97},{2,98},{3,99},{4,100},{5,101},{6,102},{7,103},{8,104... | collective-permute-start | bytes 737288 | tf_op jit(solution)/shard_map/ppermute | solution.py:34
  11.8 0.2 collective-permute-start.5
  12.0 2.5 %collective-permute-done.4.refs_0_ = s32[3,2]{1,0:T(4,128)S(1)} collective-permute-done((s32[3,2]{1,0:T(4,128)S(1)}, s32[3,2]{1,0:T(4,128)S(1)}, u32[]{:S(2)}, u32[]{:S(2)}) %collective-permute-start.4) | collective-permute-done | bytes 56 | tf_op jit(solution)/shard_map/ppermute | solution.py:34
  14.5 2.9 %collective-permute-done.5.refs_1_ = s32[3,2]{1,0:T(4,128)S(1)} collective-permute-done((s32[3,2]{1,0:T(4,128)S(1)}, s32[3,2]{1,0:T(4,128)S(1)}, u32[]{:S(2)}, u32[]{:S(2)}) %collective-permute-start.5) | collective-permute-done | bytes 56 | tf_op jit(solution)/shard_map/ppermute | solution.py:34
  17.5 1.0 shard_map.47
  18.7 1.0 collective-permute-start.7
  19.7 4.1 %collective-permute-done.7.refs_5_ = bf16[6,160,128]{2,1,0:T(8,128)(2,1)S(1)} collective-permute-done((bf16[6,160,128]{2,1,0:T(8,128)(2,1)S(1)}, bf16[6,160,128]{2,1,0:T(8,128)(2,1)S(1)}, u32[]{:S(2)}, u32[]{:S(2)}) %collective-permute-start.7) | collective-permute-done | bytes 245792 | tf_op jit(solution)/shard_map/ppermute | solution.py:34
  23.8 3.4 %collective-permute-done.6.refs_2_ = bf16[6,352,128]{2,1,0:T(8,128)(2,1)S(1)} collective-permute-done((bf16[6,352,128]{2,1,0:T(8,128)(2,1)S(1)}, bf16[6,352,128]{2,1,0:T(8,128)(2,1)S(1)}, u32[]{:S(2)}, u32[]{:S(2)}) %collective-permute-start.6) | collective-permute-done | bytes 540704 | tf_op jit(solution)/shard_map/ppermute | solution.py:34
  27.2 0.9 shard_map.48
  28.1 2.9 %collective-permute-start.8 = (bf16[3,512,128]{2,1,0:T(8,128)(2,1)S(1)}, bf16[3,512,128]{2,1,0:T(8,128)(2,1)S(1)}, u32[]{:S(2)}, u32[]{:S(2)}) collective-permute-start(bf16[3,512,128]{2,1,0:T(8,128)(2,1)S(1)} %get-tuple-element.52.refs_0_), channel_id=1, source_target_pairs={{0,8},{1,9},{2,10},{3,11},{4,12},{5,13},{6,14},{7,15},{8,0},{9,1},... | collective-permute-start | bytes 1179656 | tf_op jit(solution)/shard_map/ppermute | solution.py:34
  31.2 3.6 %collective-permute-start.9 = (bf16[3,512,128]{2,1,0:T(8,128)(2,1)S(1)}, bf16[3,512,128]{2,1,0:T(8,128)(2,1)S(1)}, u32[]{:S(2)}, u32[]{:S(2)}) collective-permute-start(bf16[3,512,128]{2,1,0:T(8,128)(2,1)S(1)} %get-tuple-element.52.refs_0_), channel_id=1, source_target_pairs={{0,1},{1,0},{2,3},{3,2},{4,5},{5,4},{6,7},{7,6},{8,9},{9,8},{10,11... | collective-permute-start | bytes 1179656 | tf_op jit(solution)/shard_map/ppermute | solution.py:34
  34.8 0.8 collective-permute-start.12
  35.6 1.2 collective-permute-done.8.refs_0_.refs_1_
  36.8 4.4 %collective-permute-start.10 = (bf16[3,512,128]{2,1,0:T(8,128)(2,1)S(1)}, bf16[3,512,128]{2,1,0:T(8,128)(2,1)S(1)}, u32[]{:S(2)}, u32[]{:S(2)}) collective-permute-start(bf16[3,512,128]{2,1,0:T(8,128)(2,1)S(1)} %collective-permute-done.8.refs_0_.refs_1_), channel_id=1, source_target_pairs={{0,1},{1,0},{2,3},{3,2},{4,5},{5,4},{6,7},{7,6},{8,9},{9,8},{10,11... | collective-permute-start | bytes 1179656 | tf_op jit(solution)/shard_map/ppermute | solution.py:34
  41.3 1.9 %shard_map.49 = (f32[3,1024,128]{2,1,0:T(8,128)S(1)}, f32[3,1024,128]{2,1,0:T(8,128)S(1)}, f32[3,1,8,512]{3,2,1,0:T(8,128)S(1)}, f32[3,1,8,512]{3,2,1,0:T(8,128)...) custom-call(bf16[3,512,128]{2,1,0:T(8,128)(2,1)S(1)} %get-tuple-element.52.refs_0_, ...), custom_call_target="tpu_custom_call" | custom-call | flops 804000000 | bytes 600000 | tf_op jit(solution)/shard_map/pallas_call | solution.py:439
  43.3 2.8 %collective-permute-done.12.refs_3_.refs_6_ = bf16[3,512,128]{2,1,0:T(8,128)(2,1)S(1)} collective-permute-done((bf16[3,512,128]{2,1,0:T(8,128)(2,1)S(1)}, bf16[3,512,128]{2,1,0:T(8,128)(2,1)S(1)}, u32[]{:S(2)}, u32[]{:S(2)}) %collective-permute-start.12) | collective-permute-done | bytes 393248 | tf_op jit(solution)/shard_map/ppermute | solution.py:34
  46.0 3.4 %shard_map.50 = (f32[3,1024,128]{2,1,0:T(8,128)S(1)}, f32[3,1024,128]{2,1,0:T(8,128)S(1)}, f32[3,2,8,512]{3,2,1,0:T(8,128)S(1)}, f32[3,2,8,512]{3,2,1,0:T(8,128)...) custom-call(bf16[3,512,128]{2,1,0:T(8,128)(2,1)S(1)} %get-tuple-element.52.refs_0_, ...), custom_call_target="tpu_custom_call" | custom-call | flops 1608000000 | bytes 1200000 | tf_op jit(solution)/shard_map/pallas_call | solution.py:439
  49.5 4.8 %shard_map.51 = (f32[3,1024,128]{2,1,0:T(8,128)S(1)}, f32[3,1024,128]{2,1,0:T(8,128)S(1)}, f32[3,3,8,512]{3,2,1,0:T(8,128)S(1)}, f32[3,3,8,512]{3,2,1,0:T(8,128)S(1)}, f32[3,3,8,512]{3,2,1,0:T(8,128)S(1)}) custom-call(bf16[3,512,128]{2,1,0:T(8,128)(2,1)S(1)} %collective-permute-done.8.refs_0_.refs_1_, ...), custom_call_target="tpu_custom_call" | custom-call | flops 2412000000 | bytes 1800000 | tf_op jit(solution)/shard_map/pallas_call | solution.py:439
  54.3 5.2 %shard_map.52 = (f32[2,3,16,128]{3,2,1,0:T(8,128)S(1)}, f32[2,3,16,128]{3,2,1,0:T(8,128)S(1)}, f32[2,3,16,128]{3,2,1,0:T(8,128)S(1)}, f32[2,3,16,128]{3,2,1,0:T(8,128)S(1)}) custom-call(bf16[3,512,128]{2,1,0:T(8,128)(2,1)S(1)} %get-tuple-element.52.refs_0_, bf16[3,512,128]{2,1,0:T(8,128)(2,1)S(1)} %collective-permute-done.8.refs_0_.refs_1_, ...), custom_call_target="tpu_custom_call" | custom-call | flops 1608000000 | bytes 1200000 | tf_op jit(solution)/shard_map/pallas_call | solution.py:454
  59.5 72.3 %collective-permute-start.14 = (f32[2,3,16,128]{3,2,1,0:T(8,128)S(1)}, f32[2,3,16,128]{3,2,1,0:T(8,128)S(1)}, u32[]{:S(2)}, u32[]{:S(2)}) collective-permute-start(f32[2,3,16,128]{3,2,1,0:T(8,128)S(1)} %get-tuple-element.72), channel_id=1, source_target_pairs={{0,1},{1,0},{2,3},{3,2},{4,5},{5,4},{6,7},{7,6},{8,9},{9,8},{10,11... | collective-permute-start | bytes 147464 | tf_op jit(solution)/shard_map/ppermute | solution.py:34
  131.9 1.0 collective-permute-start.15
  132.9 1.9 %collective-permute-done.15.rev_in = f32[2,3,16,128]{3,2,1,0:T(8,128)S(1)} collective-permute-done((f32[2,3,16,128]{3,2,1,0:T(8,128)S(1)}, f32[2,3,16,128]{3,2,1,0:T(8,128)S(1)}, u32[]{:S(2)}, u32[]{:S(2)}) %collective-permute-start.15) | collective-permute-done | bytes 49184 | tf_op jit(solution)/shard_map/ppermute | solution.py:34
  134.9 0.3 collective-permute-start.16
  135.1 4.0 %collective-permute-done.16.fwd_in = f32[3,16,128]{2,1,0:T(8,128)S(1)} collective-permute-done((f32[3,16,128]{2,1,0:T(8,128)S(1)}, f32[3,16,128]{2,1,0:T(8,128)S(1)}, u32[]{:S(2)}, u32[]{:S(2)}) %collective-permute-start.16) | collective-permute-done | bytes 24608 | tf_op jit(solution)/shard_map/ppermute | solution.py:34
  139.2 6.6 %collective-permute-start.18 = (f32[3,2,2,4,128]{4,3,2,1,0:T(4,128)S(1)}, f32[3,2,2,4,128]{4,3,2,1,0:T(4,128)S(1)}, u32[]{:S(2)}, u32[]{:S(2)}) collective-permute-start(f32[3,2,2,4,128]{4,3,2,1,0:T(4,128)S(1)} %shard_map.54.own), channel_id=1, source_target_pairs={{0,0},{1,2},{2,1},{3,4},{4,3},{5,6},{6,5},{7,8},{8,7},{9,10},{10,9... | collective-permute-start | bytes 73736 | tf_op jit(solution)/shard_map/ppermute | solution.py:34
  145.9 0.2 copy.9
  146.4 1.6 %collective-permute-done.18.chip = f32[3,2,2,4,128]{4,3,2,1,0:T(4,128)S(1)} collective-permute-done((f32[3,2,2,4,128]{4,3,2,1,0:T(4,128)S(1)}, f32[3,2,2,4,128]{4,3,2,1,0:T(4,128)S(1)}, u32[]{:S(2)}, u32[]{:S(2)}) %collective-permute-start.18) | collective-permute-done | bytes 24608 | tf_op jit(solution)/shard_map/ppermute | solution.py:34
  147.9 1.9 %shard_map.55 = f32[3,2,2,4,128]{4,3,2,1,0:T(4,128)} custom-call(f32[144]{0:T(256)S(1)} %reshape.9.weight, f32[8]{0:T(128)S(1)} %reshape.10.bias, f32[3,2,2,4,128]{4,3,2,1,0:T(4,128)S(1)} %collective-permute-done.18.chip, f32[3,2,2,4,128]{4,3,2,1,0:T(4,128)S(1)} %shard_map.54.own, f32[3,2,2,4,128]{4,3,2,1,0:T(4,128)S(1)} %collective-permute-done.19.core), custom_call_target="tpu_custom_call" | custom-call | tf_op jit(solution)/shard_map/pallas_call | solution.py:572
  (35 shorter events, 1.2 us)
Async XLA Ops:
  0.0 11.7 %copy-start.2 = (s32[3,2]{0,1:T(2,128)S(1)}, s32[3,2]{0,1:T(2,128)}, u32[]{:S(2)}) copy-start(s32[3,2]{0,1:T(2,128)} %param.5) | copy-start | bytes 76
  0.0 1.0 copy-start
  1.0 7.7 %collective-permute-start = (bf16[3,352,128]{2,1,0:T(8,128)(2,1)S(1)}, bf16[3,352,128]{2,1,0:T(8,128)(2,1)S(1)}, u32[]{:S(2)}, u32[]{:S(2)}) collective-permute-start(bf16[3,352,128]{2,1,0:T(8,128)(2,1)S(1)} %get-tuple-element.42), channel_id=1, source_target_pairs={{0,16},{1,97},{2,18},{3,99},{4,20},{5,101},{6,22},{7,103},{8,24},{... | collective-permute-start | bytes 811016 | tf_op jit(solution)/shard_map/ppermute | solution.py:34
  3.6 5.1 %collective-permute-start.1 = (bf16[3,160,128]{2,1,0:T(8,128)(2,1)S(1)}, bf16[3,160,128]{2,1,0:T(8,128)(2,1)S(1)}, u32[]{:S(2)}, u32[]{:S(2)}) collective-permute-start(bf16[3,160,128]{2,1,0:T(8,128)(2,1)S(1)} %get-tuple-element.43), channel_id=1, source_target_pairs={{0,32},{1,33},{2,34},{3,35},{4,36},{5,37},{6,38},{7,39},{8,40},{9,... | collective-permute-start | bytes 368648 | tf_op jit(solution)/shard_map/ppermute | solution.py:34
  8.8 8.8 %collective-permute-start.2 = (bf16[6,352,128]{2,1,0:T(8,128)(2,1)S(1)}, bf16[6,352,128]{2,1,0:T(8,128)(2,1)S(1)}, u32[]{:S(2)}, u32[]{:S(2)}) collective-permute-start(bf16[6,352,128]{2,1,0:T(8,128)(2,1)S(1)} %constant_dynamic-update-slice_fusion.refs_2_.refs_0_), channel_id=1, source_target_pairs={{0,32},{1,17},{2,34},{3,19},{4,36},{5,21},{6,38},{7,23},{8,40},{9,... | collective-permute-start | bytes 1622024 | tf_op jit(solution)/shard_map/ppermute | solution.py:34
  9.3 8.2 %collective-permute-start.3 = (bf16[6,160,128]{2,1,0:T(8,128)(2,1)S(1)}, bf16[6,160,128]{2,1,0:T(8,128)(2,1)S(1)}, u32[]{:S(2)}, u32[]{:S(2)}) collective-permute-start(bf16[6,160,128]{2,1,0:T(8,128)(2,1)S(1)} %constant_dynamic-update-slice_fusion.2.refs_4_.refs_3_), channel_id=1, source_target_pairs={{0,96},{1,97},{2,98},{3,99},{4,100},{5,101},{6,102},{7,103},{8,104... | collective-permute-start | bytes 737288 | tf_op jit(solution)/shard_map/ppermute | solution.py:34
  11.8 2.7 %collective-permute-start.4 = (s32[3,2]{1,0:T(4,128)S(1)}, s32[3,2]{1,0:T(4,128)S(1)}, u32[]{:S(2)}, u32[]{:S(2)}) collective-permute-start(s32[3,2]{1,0:T(4,128)S(1)} %copy.13.table), channel_id=1, source_target_pairs={{0,96},{1,33},{2,98},{3,35},{4,100},{5,37},{6,102},{7,39},{8,104},... | collective-permute-start | bytes 80 | tf_op jit(solution)/shard_map/ppermute | solution.py:34
  11.8 5.6 %collective-permute-start.5 = (s32[3,2]{1,0:T(4,128)S(1)}, s32[3,2]{1,0:T(4,128)S(1)}, u32[]{:S(2)}, u32[]{:S(2)}) collective-permute-start(s32[3,2]{1,0:T(4,128)S(1)} %copy.13.table), channel_id=1, source_target_pairs={{0,16},{1,17},{2,18},{3,19},{4,20},{5,21},{6,22},{7,23},{8,24},{9,... | collective-permute-start | bytes 80 | tf_op jit(solution)/shard_map/ppermute | solution.py:34
  18.6 8.6 %collective-permute-start.6 = (bf16[6,352,128]{2,1,0:T(8,128)(2,1)S(1)}, bf16[6,352,128]{2,1,0:T(8,128)(2,1)S(1)}, u32[]{:S(2)}, u32[]{:S(2)}) collective-permute-start(bf16[6,352,128]{2,1,0:T(8,128)(2,1)S(1)} %get-tuple-element.50), channel_id=1, source_target_pairs={{0,96},{1,33},{2,98},{3,35},{4,100},{5,37},{6,102},{7,39},{8,104},... | collective-permute-start | bytes 1622024 | tf_op jit(solution)/shard_map/ppermute | solution.py:34
  18.7 5.1 %collective-permute-start.7 = (bf16[6,160,128]{2,1,0:T(8,128)(2,1)S(1)}, bf16[6,160,128]{2,1,0:T(8,128)(2,1)S(1)}, u32[]{:S(2)}, u32[]{:S(2)}) collective-permute-start(bf16[6,160,128]{2,1,0:T(8,128)(2,1)S(1)} %get-tuple-element.51), channel_id=1, source_target_pairs={{0,16},{1,17},{2,18},{3,19},{4,20},{5,21},{6,22},{7,23},{8,24},{9,... | collective-permute-start | bytes 737288 | tf_op jit(solution)/shard_map/ppermute | solution.py:34
  28.1 8.7 %collective-permute-start.8 = (bf16[3,512,128]{2,1,0:T(8,128)(2,1)S(1)}, bf16[3,512,128]{2,1,0:T(8,128)(2,1)S(1)}, u32[]{:S(2)}, u32[]{:S(2)}) collective-permute-start(bf16[3,512,128]{2,1,0:T(8,128)(2,1)S(1)} %get-tuple-element.52.refs_0_), channel_id=1, source_target_pairs={{0,8},{1,9},{2,10},{3,11},{4,12},{5,13},{6,14},{7,15},{8,0},{9,1},... | collective-permute-start | bytes 1179656 | tf_op jit(solution)/shard_map/ppermute | solution.py:34
  31.0 10.2 %collective-permute-start.11 = (bf16[3,512,128]{2,1,0:T(8,128)(2,1)S(1)}, bf16[3,512,128]{2,1,0:T(8,128)(2,1)S(1)}, u32[]{:S(2)}, u32[]{:S(2)}) collective-permute-start(bf16[3,512,128]{2,1,0:T(8,128)(2,1)S(1)} %get-tuple-element.53.refs_2_.refs_4_), channel_id=1, source_target_pairs={{0,2},{1,7},{2,4},{3,1},{4,6},{5,3},{6,0},{7,5},{8,10},{9,15},{10,... | collective-permute-start | bytes 1179656 | tf_op jit(solution)/shard_map/ppermute | solution.py:34
  31.2 10.2 %collective-permute-start.9 = (bf16[3,512,128]{2,1,0:T(8,128)(2,1)S(1)}, bf16[3,512,128]{2,1,0:T(8,128)(2,1)S(1)}, u32[]{:S(2)}, u32[]{:S(2)}) collective-permute-start(bf16[3,512,128]{2,1,0:T(8,128)(2,1)S(1)} %get-tuple-element.52.refs_0_), channel_id=1, source_target_pairs={{0,1},{1,0},{2,3},{3,2},{4,5},{5,4},{6,7},{7,6},{8,9},{9,8},{10,11... | collective-permute-start | bytes 1179656 | tf_op jit(solution)/shard_map/ppermute | solution.py:34
  34.8 11.2 %collective-permute-start.12 = (bf16[3,512,128]{2,1,0:T(8,128)(2,1)S(1)}, bf16[3,512,128]{2,1,0:T(8,128)(2,1)S(1)}, u32[]{:S(2)}, u32[]{:S(2)}) collective-permute-start(bf16[3,512,128]{2,1,0:T(8,128)(2,1)S(1)} %get-tuple-element.53.refs_2_.refs_4_), channel_id=1, source_target_pairs={{0,6},{1,3},{2,0},{3,5},{4,2},{5,7},{6,4},{7,1},{8,14},{9,11},{10,... | collective-permute-start | bytes 1179656 | tf_op jit(solution)/shard_map/ppermute | solution.py:34
  36.8 12.7 %collective-permute-start.10 = (bf16[3,512,128]{2,1,0:T(8,128)(2,1)S(1)}, bf16[3,512,128]{2,1,0:T(8,128)(2,1)S(1)}, u32[]{:S(2)}, u32[]{:S(2)}) collective-permute-start(bf16[3,512,128]{2,1,0:T(8,128)(2,1)S(1)} %collective-permute-done.8.refs_0_.refs_1_), channel_id=1, source_target_pairs={{0,1},{1,0},{2,3},{3,2},{4,5},{5,4},{6,7},{7,6},{8,9},{9,8},{10,11... | collective-permute-start | bytes 1179656 | tf_op jit(solution)/shard_map/ppermute | solution.py:34
  41.2 13.1 %collective-permute-start.13 = (bf16[3,512,128]{2,1,0:T(8,128)(2,1)S(1)}, bf16[3,512,128]{2,1,0:T(8,128)(2,1)S(1)}, u32[]{:S(2)}, u32[]{:S(2)}) collective-permute-start(bf16[3,512,128]{2,1,0:T(8,128)(2,1)S(1)} %collective-permute-done.11.refs_2_.refs_5_), channel_id=1, source_target_pairs={{0,2},{1,7},{2,4},{3,1},{4,6},{5,3},{6,0},{7,5},{8,10},{9,15},{10,... | collective-permute-start | bytes 1179656 | tf_op jit(solution)/shard_map/ppermute | solution.py:34
  54.3 91.6 %copy-start.1 = (f32[4,2,2,3,3]{0,2,4,3,1:T(2,128)S(1)}, f32[4,2,2,3,3]{0,2,4,3,1:T(2,128)}, u32[]{:S(2)}) copy-start(f32[4,2,2,3,3]{0,2,4,3,1:T(2,128)} %param.6) | copy-start | bytes 1732
  54.3 91.9 %copy-start.3 = (f32[4,2]{0,1:T(2,128)S(1)}, f32[4,2]{0,1:T(2,128)}, u32[]{:S(2)}) copy-start(f32[4,2]{0,1:T(2,128)} %param.7) | copy-start | bytes 100
  59.5 73.4 %collective-permute-start.14 = (f32[2,3,16,128]{3,2,1,0:T(8,128)S(1)}, f32[2,3,16,128]{3,2,1,0:T(8,128)S(1)}, u32[]{:S(2)}, u32[]{:S(2)}) collective-permute-start(f32[2,3,16,128]{3,2,1,0:T(8,128)S(1)} %get-tuple-element.72), channel_id=1, source_target_pairs={{0,1},{1,0},{2,3},{3,2},{4,5},{5,4},{6,7},{7,6},{8,9},{9,8},{10,11... | collective-permute-start | bytes 147464 | tf_op jit(solution)/shard_map/ppermute | solution.py:34
  131.9 2.9 %collective-permute-start.15 = (f32[2,3,16,128]{3,2,1,0:T(8,128)S(1)}, f32[2,3,16,128]{3,2,1,0:T(8,128)S(1)}, u32[]{:S(2)}, u32[]{:S(2)}) collective-permute-start(f32[2,3,16,128]{3,2,1,0:T(8,128)S(1)} %get-tuple-element.74), channel_id=1, source_target_pairs={{0,2},{1,3},{2,0},{3,1},{4,6},{5,7},{6,4},{7,5},{8,10},{9,11},{10,... | collective-permute-start | bytes 147464 | tf_op jit(solution)/shard_map/ppermute | solution.py:34
  134.9 4.3 %collective-permute-start.16 = (f32[3,16,128]{2,1,0:T(8,128)S(1)}, f32[3,16,128]{2,1,0:T(8,128)S(1)}, u32[]{:S(2)}, u32[]{:S(2)}) collective-permute-start(f32[3,16,128]{2,1,0:T(8,128)S(1)} %get-tuple-element.76), channel_id=1, source_target_pairs={{0,8},{1,9},{2,10},{3,11},{4,12},{5,13},{6,14},{7,15},{8,0},{9,1},... | collective-permute-start | bytes 73736 | tf_op jit(solution)/shard_map/ppermute | solution.py:34
  135.1 4.0 %collective-permute-start.17 = (f32[3,16,128]{2,1,0:T(8,128)S(1)}, f32[3,16,128]{2,1,0:T(8,128)S(1)}, u32[]{:S(2)}, u32[]{:S(2)}) collective-permute-start(f32[3,16,128]{2,1,0:T(8,128)S(1)} %get-tuple-element.78), channel_id=1, source_target_pairs={{0,6},{1,7},{2,4},{3,5},{4,2},{5,3},{6,0},{7,1},{8,14},{9,15},{10,... | collective-permute-start | bytes 73736 | tf_op jit(solution)/shard_map/ppermute | solution.py:34
  139.2 8.8 %collective-permute-start.18 = (f32[3,2,2,4,128]{4,3,2,1,0:T(4,128)S(1)}, f32[3,2,2,4,128]{4,3,2,1,0:T(4,128)S(1)}, u32[]{:S(2)}, u32[]{:S(2)}) collective-permute-start(f32[3,2,2,4,128]{4,3,2,1,0:T(4,128)S(1)} %shard_map.54.own), channel_id=1, source_target_pairs={{0,0},{1,2},{2,1},{3,4},{4,3},{5,6},{6,5},{7,8},{8,7},{9,10},{10,9... | collective-permute-start | bytes 73736 | tf_op jit(solution)/shard_map/ppermute | solution.py:34
  145.8 2.2 %collective-permute-start.19 = (f32[3,2,2,4,128]{4,3,2,1,0:T(4,128)S(1)}, f32[3,2,2,4,128]{4,3,2,1,0:T(4,128)S(1)}, u32[]{:S(2)}, u32[]{:S(2)}) collective-permute-start(f32[3,2,2,4,128]{4,3,2,1,0:T(4,128)S(1)} %shard_map.54.own), channel_id=1, source_target_pairs={{0,1},{1,0},{2,3},{3,2},{4,5},{5,4},{6,7},{7,6},{8,9},{9,8},{10,11... | collective-permute-start | bytes 73736 | tf_op jit(solution)/shard_map/ppermute | solution.py:34

commit v7 on v6

--- a/solution.py
+++ b/solution.py
@@ -567,16 +567,16 @@
                 out[p, d, i] = cur[i][base : base + band_rows]
 
 
-def refine(weight, bias, chip, own, core):
+def refine(weight, bias, chip, own, core, layers):
     pairs, ways, comps, band_rows, width = own.shape
     return pl.pallas_call(
-        functools.partial(refine_kernel, layers=weight.shape[0]),
+        functools.partial(refine_kernel, layers=layers),
         out_shape=jax.ShapeDtypeStruct(own.shape, jnp.float32),
         in_specs=[SMEM, SMEM, VMEM, VMEM, VMEM],
         out_specs=VMEM,
         scratch_shapes=[pltpu.VMEM((pairs * ways * 3 * band_rows, width), jnp.float32)] * (comps + 1),
         compiler_params=pltpu.CompilerParams(vmem_limit_bytes=4 << 20),
-    )(weight.reshape(-1), bias.reshape(-1), chip, own, core)
+    )(weight, bias, chip, own, core)
 
 
 def split_kernel(whole, first, second):
@@ -596,7 +596,7 @@
     )(whole)
 
 
-def gather_frames(blocks, table):
+def gather_frames(blocks, table, extra):
     orders = (
         (by_core(flip_y, flip_b), by_core(flip_a, flip_y), by_core(flip_b, flip_a)),
         (flip_a, flip_b, flip_y),
@@ -605,10 +605,10 @@
     send = [jnp.concatenate(both, axis=0) for both in zip(blocks, first)]
     second = [hop(part, order[1]) for part, order in zip(send, orders)]
     tables = [hop(table, order[2]) for order in orders]
-    second, tables = lax.optimization_barrier((second, tables))
+    second, tables, extra = lax.optimization_barrier((second, tables, extra))
     held = [[part, piece] for part, piece in zip(send, second)]
     sent = [hop(part, order[2]) for part, order in zip(offer(tables, held), orders)]
-    return pick(table, [have + [piece] for have, piece in zip(held, sent)])
+    return (*pick(table, [have + [piece] for have, piece in zip(held, sent)]), *extra)
 
 
 def matched(src0, tgt0):
@@ -629,13 +629,16 @@
     frames, band_rows, width, chans = features.shape
     cells = band_rows * width
     flat_features = features.reshape(frames, cells, chans)
-    src0, tgt0 = gather_frames(split(flat_features, cells * 11 // 16), frame_pairs)
+    weight = conv_weight.reshape(-1)
+    bias = conv_bias.reshape(-1)
+    flat_conv = (weight, bias)
+    src0, tgt0, weight, bias = gather_frames(split(flat_features, cells * 11 // 16), frame_pairs, flat_conv)
     fwd_keep, fwd_send, rev_keep, rev_send = matched(src0, tgt0)
     fwd0, fwd1, rev0, rev1 = half(fwd_keep, hop(fwd_send, flip_c), rev_keep, hop(rev_send, flip_za), band_rows)
     flows = merge(fwd0, hop(fwd1, flip_h), rev0, hop(rev1, flip_zb), band_rows, width)
+    chip = hop(flows, next_chip)
     core = hop(flows, flip_c)
-    chip = hop(flows, next_chip)
-    return refine(conv_weight, conv_bias, chip, flows, core)
+    return refine(weight, bias, chip, flows, core, conv_weight.shape[0])
 
 
 def solution(mesh):

time: 153 us -> 153 us (level)
  no operation moved by 1% of the time
where the time goes in v7:
time: 153 us; the launch traced here: 150 us
  starting transfers between devices  99.1 us (65%)
  waiting for transfers between devices  29.5 us (19%)
  Pallas kernels  19.3 us (13%)
  local copies, waits for them, and re-layouts  1.69 us (1%)
    ppermute x20, starting transfers between devices, hop(): return lax.ppermute(value, AXES, route)  99.1 us
    ppermute x20, waiting for transfers between devices, hop(): return lax.ppermute(value, AXES, route)  29.5 us
    pallas_call x3, Pallas kernels, match_early(): pl.pallas_call(functools.partial(early_kernel, which=which, bands=bands,...  10.1 us
    pallas_call x1, Pallas kernels, match_late(): pl.pallas_call(functools.partial(late_kernel, nsrc=nsrc, ntgt=ntgt, cells...  5.21 us
  transfers between devices with their start and end apart: 20, of which 11 were waited for; matrix products, arithmetic and copies ran while one was open for 0% of the time, Pallas kernels for 7%

profile of v7, /device:TPU:97, one launch (start us, length us, event | category | flops | bytes accessed | tf_op | source)
XLA Modules:
  0.0 149.8 jit_solution(636050414656243309)
XLA Ops:
  0.0 1.0 copy-done
  1.0 2.6 %collective-permute-start = (bf16[3,352,128]{2,1,0:T(8,128)(2,1)S(1)}, bf16[3,352,128]{2,1,0:T(8,128)(2,1)S(1)}, u32[]{:S(2)}, u32[]{:S(2)}) collective-permute-start(bf16[3,352,128]{2,1,0:T(8,128)(2,1)S(1)} %get-tuple-element.44), channel_id=1, source_target_pairs={{0,16},{1,97},{2,18},{3,99},{4,20},{5,101},{6,22},{7,103},{8,24},{... | collective-permute-start | bytes 811016 | tf_op jit(solution)/shard_map/ppermute | solution.py:34
  3.6 5.1 %collective-permute-done.1 = bf16[3,160,128]{2,1,0:T(8,128)(2,1)S(1)} collective-permute-done((bf16[3,160,128]{2,1,0:T(8,128)(2,1)S(1)}, bf16[3,160,128]{2,1,0:T(8,128)(2,1)S(1)}, u32[]{:S(2)}, u32[]{:S(2)}) %collective-permute-start.1) | collective-permute-done | bytes 122912 | tf_op jit(solution)/shard_map/ppermute | solution.py:34
  8.8 0.5 collective-permute-start.2
  9.3 2.3 %collective-permute-start.3 = (bf16[6,160,128]{2,1,0:T(8,128)(2,1)S(1)}, bf16[6,160,128]{2,1,0:T(8,128)(2,1)S(1)}, u32[]{:S(2)}, u32[]{:S(2)}) collective-permute-start(bf16[6,160,128]{2,1,0:T(8,128)(2,1)S(1)} %constant_dynamic-update-slice_fusion.2.refs_4_.refs_3_), channel_id=1, source_target_pairs={{0,96},{1,97},{2,98},{3,99},{4,100},{5,101},{6,102},{7,103},{8,104... | collective-permute-start | bytes 737288 | tf_op jit(solution)/shard_map/ppermute | solution.py:34
  11.8 0.2 collective-permute-start.5
  12.0 0.2 copy.11
  12.5 2.0 %collective-permute-done.4.refs_0_ = s32[3,2]{1,0:T(4,128)S(1)} collective-permute-done((s32[3,2]{1,0:T(4,128)S(1)}, s32[3,2]{1,0:T(4,128)S(1)}, u32[]{:S(2)}, u32[]{:S(2)}) %collective-permute-start.4) | collective-permute-done | bytes 56 | tf_op jit(solution)/shard_map/ppermute | solution.py:34
  14.5 2.9 %collective-permute-done.5.refs_1_ = s32[3,2]{1,0:T(4,128)S(1)} collective-permute-done((s32[3,2]{1,0:T(4,128)S(1)}, s32[3,2]{1,0:T(4,128)S(1)}, u32[]{:S(2)}, u32[]{:S(2)}) %collective-permute-start.5) | collective-permute-done | bytes 56 | tf_op jit(solution)/shard_map/ppermute | solution.py:34
  17.5 1.0 shard_map.47
  18.7 1.0 collective-permute-start.7
  19.7 4.1 %collective-permute-done.7.refs_5_ = bf16[6,160,128]{2,1,0:T(8,128)(2,1)S(1)} collective-permute-done((bf16[6,160,128]{2,1,0:T(8,128)(2,1)S(1)}, bf16[6,160,128]{2,1,0:T(8,128)(2,1)S(1)}, u32[]{:S(2)}, u32[]{:S(2)}) %collective-permute-start.7) | collective-permute-done | bytes 245792 | tf_op jit(solution)/shard_map/ppermute | solution.py:34
  23.8 3.4 %collective-permute-done.6.refs_2_ = bf16[6,352,128]{2,1,0:T(8,128)(2,1)S(1)} collective-permute-done((bf16[6,352,128]{2,1,0:T(8,128)(2,1)S(1)}, bf16[6,352,128]{2,1,0:T(8,128)(2,1)S(1)}, u32[]{:S(2)}, u32[]{:S(2)}) %collective-permute-start.6) | collective-permute-done | bytes 540704 | tf_op jit(solution)/shard_map/ppermute | solution.py:34
  27.2 0.9 shard_map.48
  28.1 2.9 %collective-permute-start.8 = (bf16[3,512,128]{2,1,0:T(8,128)(2,1)S(1)}, bf16[3,512,128]{2,1,0:T(8,128)(2,1)S(1)}, u32[]{:S(2)}, u32[]{:S(2)}) collective-permute-start(bf16[3,512,128]{2,1,0:T(8,128)(2,1)S(1)} %get-tuple-element.56.refs_0_), channel_id=1, source_target_pairs={{0,8},{1,9},{2,10},{3,11},{4,12},{5,13},{6,14},{7,15},{8,0},{9,1},... | collective-permute-start | bytes 1179656 | tf_op jit(solution)/shard_map/ppermute | solution.py:34
  31.2 3.6 %collective-permute-start.9 = (bf16[3,512,128]{2,1,0:T(8,128)(2,1)S(1)}, bf16[3,512,128]{2,1,0:T(8,128)(2,1)S(1)}, u32[]{:S(2)}, u32[]{:S(2)}) collective-permute-start(bf16[3,512,128]{2,1,0:T(8,128)(2,1)S(1)} %get-tuple-element.56.refs_0_), channel_id=1, source_target_pairs={{0,1},{1,0},{2,3},{3,2},{4,5},{5,4},{6,7},{7,6},{8,9},{9,8},{10,11... | collective-permute-start | bytes 1179656 | tf_op jit(solution)/shard_map/ppermute | solution.py:34
  34.8 0.8 collective-permute-start.12
  35.6 1.2 collective-permute-done.8.refs_0_.refs_1_
  36.8 4.4 %collective-permute-start.10 = (bf16[3,512,128]{2,1,0:T(8,128)(2,1)S(1)}, bf16[3,512,128]{2,1,0:T(8,128)(2,1)S(1)}, u32[]{:S(2)}, u32[]{:S(2)}) collective-permute-start(bf16[3,512,128]{2,1,0:T(8,128)(2,1)S(1)} %collective-permute-done.8.refs_0_.refs_1_), channel_id=1, source_target_pairs={{0,1},{1,0},{2,3},{3,2},{4,5},{5,4},{6,7},{7,6},{8,9},{9,8},{10,11... | collective-permute-start | bytes 1179656 | tf_op jit(solution)/shard_map/ppermute | solution.py:34
  41.4 1.9 %shard_map.49 = (f32[3,1024,128]{2,1,0:T(8,128)S(1)}, f32[3,1024,128]{2,1,0:T(8,128)S(1)}, f32[3,1,8,512]{3,2,1,0:T(8,128)S(1)}, f32[3,1,8,512]{3,2,1,0:T(8,128)...) custom-call(bf16[3,512,128]{2,1,0:T(8,128)(2,1)S(1)} %get-tuple-element.56.refs_0_, ...), custom_call_target="tpu_custom_call" | custom-call | flops 804000000 | bytes 600000 | tf_op jit(solution)/shard_map/pallas_call | solution.py:439
  43.3 2.8 %collective-permute-done.12.refs_3_.refs_6_ = bf16[3,512,128]{2,1,0:T(8,128)(2,1)S(1)} collective-permute-done((bf16[3,512,128]{2,1,0:T(8,128)(2,1)S(1)}, bf16[3,512,128]{2,1,0:T(8,128)(2,1)S(1)}, u32[]{:S(2)}, u32[]{:S(2)}) %collective-permute-start.12) | collective-permute-done | bytes 393248 | tf_op jit(solution)/shard_map/ppermute | solution.py:34
  46.0 3.4 %shard_map.50 = (f32[3,1024,128]{2,1,0:T(8,128)S(1)}, f32[3,1024,128]{2,1,0:T(8,128)S(1)}, f32[3,2,8,512]{3,2,1,0:T(8,128)S(1)}, f32[3,2,8,512]{3,2,1,0:T(8,128)...) custom-call(bf16[3,512,128]{2,1,0:T(8,128)(2,1)S(1)} %get-tuple-element.56.refs_0_, ...), custom_call_target="tpu_custom_call" | custom-call | flops 1608000000 | bytes 1200000 | tf_op jit(solution)/shard_map/pallas_call | solution.py:439
  49.5 4.8 %shard_map.51 = (f32[3,1024,128]{2,1,0:T(8,128)S(1)}, f32[3,1024,128]{2,1,0:T(8,128)S(1)}, f32[3,3,8,512]{3,2,1,0:T(8,128)S(1)}, f32[3,3,8,512]{3,2,1,0:T(8,128)S(1)}, f32[3,3,8,512]{3,2,1,0:T(8,128)S(1)}) custom-call(bf16[3,512,128]{2,1,0:T(8,128)(2,1)S(1)} %collective-permute-done.8.refs_0_.refs_1_, ...), custom_call_target="tpu_custom_call" | custom-call | flops 2412000000 | bytes 1800000 | tf_op jit(solution)/shard_map/pallas_call | solution.py:439
  54.3 5.2 %shard_map.52 = (f32[2,3,16,128]{3,2,1,0:T(8,128)S(1)}, f32[2,3,16,128]{3,2,1,0:T(8,128)S(1)}, f32[2,3,16,128]{3,2,1,0:T(8,128)S(1)}, f32[2,3,16,128]{3,2,1,0:T(8,128)S(1)}) custom-call(bf16[3,512,128]{2,1,0:T(8,128)(2,1)S(1)} %get-tuple-element.56.refs_0_, bf16[3,512,128]{2,1,0:T(8,128)(2,1)S(1)} %collective-permute-done.8.refs_0_.refs_1_, ...), custom_call_target="tpu_custom_call" | custom-call | flops 1608000000 | bytes 1200000 | tf_op jit(solution)/shard_map/pallas_call | solution.py:454
  59.5 72.4 %collective-permute-start.14 = (f32[2,3,16,128]{3,2,1,0:T(8,128)S(1)}, f32[2,3,16,128]{3,2,1,0:T(8,128)S(1)}, u32[]{:S(2)}, u32[]{:S(2)}) collective-permute-start(f32[2,3,16,128]{3,2,1,0:T(8,128)S(1)} %get-tuple-element.76), channel_id=1, source_target_pairs={{0,1},{1,0},{2,3},{3,2},{4,5},{5,4},{6,7},{7,6},{8,9},{9,8},{10,11... | collective-permute-start | bytes 147464 | tf_op jit(solution)/shard_map/ppermute | solution.py:34
  131.9 1.0 collective-permute-start.15
  132.9 1.9 %collective-permute-done.15.rev_in = f32[2,3,16,128]{3,2,1,0:T(8,128)S(1)} collective-permute-done((f32[2,3,16,128]{3,2,1,0:T(8,128)S(1)}, f32[2,3,16,128]{3,2,1,0:T(8,128)S(1)}, u32[]{:S(2)}, u32[]{:S(2)}) %collective-permute-start.15) | collective-permute-done | bytes 49184 | tf_op jit(solution)/shard_map/ppermute | solution.py:34
  134.9 0.2 collective-permute-start.16
  135.1 4.0 %collective-permute-done.16.fwd_in = f32[3,16,128]{2,1,0:T(8,128)S(1)} collective-permute-done((f32[3,16,128]{2,1,0:T(8,128)S(1)}, f32[3,16,128]{2,1,0:T(8,128)S(1)}, u32[]{:S(2)}, u32[]{:S(2)}) %collective-permute-start.16) | collective-permute-done | bytes 24608 | tf_op jit(solution)/shard_map/ppermute | solution.py:34
  139.2 6.6 %collective-permute-start.18 = (f32[3,2,2,4,128]{4,3,2,1,0:T(4,128)S(1)}, f32[3,2,2,4,128]{4,3,2,1,0:T(4,128)S(1)}, u32[]{:S(2)}, u32[]{:S(2)}) collective-permute-start(f32[3,2,2,4,128]{4,3,2,1,0:T(4,128)S(1)} %shard_map.54.own), channel_id=1, source_target_pairs={{0,0},{1,2},{2,1},{3,4},{4,3},{5,6},{6,5},{7,8},{8,7},{9,10},{10,9... | collective-permute-start | bytes 73736 | tf_op jit(solution)/shard_map/ppermute | solution.py:34
  145.8 2.1 %collective-permute-done.18.chip = f32[3,2,2,4,128]{4,3,2,1,0:T(4,128)S(1)} collective-permute-done((f32[3,2,2,4,128]{4,3,2,1,0:T(4,128)S(1)}, f32[3,2,2,4,128]{4,3,2,1,0:T(4,128)S(1)}, u32[]{:S(2)}, u32[]{:S(2)}) %collective-permute-start.18) | collective-permute-done | bytes 24608 | tf_op jit(solution)/shard_map/ppermute | solution.py:34
  147.9 1.9 %shard_map.55 = f32[3,2,2,4,128]{4,3,2,1,0:T(4,128)} custom-call(f32[144]{0:T(256)S(1)} %reshape.10.weight, f32[8]{0:T(128)S(1)} %reshape.11.bias, f32[3,2,2,4,128]{4,3,2,1,0:T(4,128)S(1)} %collective-permute-done.18.chip, f32[3,2,2,4,128]{4,3,2,1,0:T(4,128)S(1)} %shard_map.54.own, f32[3,2,2,4,128]{4,3,2,1,0:T(4,128)S(1)} %collective-permute-done.19.core), custom_call_target="tpu_custom_call" | custom-call | tf_op jit(solution)/shard_map/pallas_call | solution.py:572
  (35 shorter events, 1.2 us)
Async XLA Ops:
  0.0 11.7 %copy-start.2 = (s32[3,2]{0,1:T(2,128)S(1)}, s32[3,2]{0,1:T(2,128)}, u32[]{:S(2)}) copy-start(s32[3,2]{0,1:T(2,128)} %param.5) | copy-start | bytes 76
  0.0 1.0 copy-start
  1.0 11.0 %copy-start.1 = (f32[4,2,2,3,3]{0,2,4,3,1:T(2,128)S(1)}, f32[4,2,2,3,3]{0,2,4,3,1:T(2,128)}, u32[]{:S(2)}) copy-start(f32[4,2,2,3,3]{0,2,4,3,1:T(2,128)} %param.6) | copy-start | bytes 1732
  1.0 11.3 %copy-start.3 = (f32[4,2]{0,1:T(2,128)S(1)}, f32[4,2]{0,1:T(2,128)}, u32[]{:S(2)}) copy-start(f32[4,2]{0,1:T(2,128)} %param.7) | copy-start | bytes 100
  1.0 7.7 %collective-permute-start = (bf16[3,352,128]{2,1,0:T(8,128)(2,1)S(1)}, bf16[3,352,128]{2,1,0:T(8,128)(2,1)S(1)}, u32[]{:S(2)}, u32[]{:S(2)}) collective-permute-start(bf16[3,352,128]{2,1,0:T(8,128)(2,1)S(1)} %get-tuple-element.44), channel_id=1, source_target_pairs={{0,16},{1,97},{2,18},{3,99},{4,20},{5,101},{6,22},{7,103},{8,24},{... | collective-permute-start | bytes 811016 | tf_op jit(solution)/shard_map/ppermute | solution.py:34
  3.6 5.1 %collective-permute-start.1 = (bf16[3,160,128]{2,1,0:T(8,128)(2,1)S(1)}, bf16[3,160,128]{2,1,0:T(8,128)(2,1)S(1)}, u32[]{:S(2)}, u32[]{:S(2)}) collective-permute-start(bf16[3,160,128]{2,1,0:T(8,128)(2,1)S(1)} %get-tuple-element.45), channel_id=1, source_target_pairs={{0,32},{1,33},{2,34},{3,35},{4,36},{5,37},{6,38},{7,39},{8,40},{9,... | collective-permute-start | bytes 368648 | tf_op jit(solution)/shard_map/ppermute | solution.py:34
  8.8 8.8 %collective-permute-start.2 = (bf16[6,352,128]{2,1,0:T(8,128)(2,1)S(1)}, bf16[6,352,128]{2,1,0:T(8,128)(2,1)S(1)}, u32[]{:S(2)}, u32[]{:S(2)}) collective-permute-start(bf16[6,352,128]{2,1,0:T(8,128)(2,1)S(1)} %constant_dynamic-update-slice_fusion.refs_2_.refs_0_), channel_id=1, source_target_pairs={{0,32},{1,17},{2,34},{3,19},{4,36},{5,21},{6,38},{7,23},{8,40},{9,... | collective-permute-start | bytes 1622024 | tf_op jit(solution)/shard_map/ppermute | solution.py:34
  9.3 8.2 %collective-permute-start.3 = (bf16[6,160,128]{2,1,0:T(8,128)(2,1)S(1)}, bf16[6,160,128]{2,1,0:T(8,128)(2,1)S(1)}, u32[]{:S(2)}, u32[]{:S(2)}) collective-permute-start(bf16[6,160,128]{2,1,0:T(8,128)(2,1)S(1)} %constant_dynamic-update-slice_fusion.2.refs_4_.refs_3_), channel_id=1, source_target_pairs={{0,96},{1,97},{2,98},{3,99},{4,100},{5,101},{6,102},{7,103},{8,104... | collective-permute-start | bytes 737288 | tf_op jit(solution)/shard_map/ppermute | solution.py:34
  11.8 2.7 %collective-permute-start.4 = (s32[3,2]{1,0:T(4,128)S(1)}, s32[3,2]{1,0:T(4,128)S(1)}, u32[]{:S(2)}, u32[]{:S(2)}) collective-permute-start(s32[3,2]{1,0:T(4,128)S(1)} %copy.9.table), channel_id=1, source_target_pairs={{0,96},{1,33},{2,98},{3,35},{4,100},{5,37},{6,102},{7,39},{8,104},... | collective-permute-start | bytes 80 | tf_op jit(solution)/shard_map/ppermute | solution.py:34
  11.8 5.6 %collective-permute-start.5 = (s32[3,2]{1,0:T(4,128)S(1)}, s32[3,2]{1,0:T(4,128)S(1)}, u32[]{:S(2)}, u32[]{:S(2)}) collective-permute-start(s32[3,2]{1,0:T(4,128)S(1)} %copy.9.table), channel_id=1, source_target_pairs={{0,16},{1,17},{2,18},{3,19},{4,20},{5,21},{6,22},{7,23},{8,24},{9,... | collective-permute-start | bytes 80 | tf_op jit(solution)/shard_map/ppermute | solution.py:34
  18.6 8.6 %collective-permute-start.6 = (bf16[6,352,128]{2,1,0:T(8,128)(2,1)S(1)}, bf16[6,352,128]{2,1,0:T(8,128)(2,1)S(1)}, u32[]{:S(2)}, u32[]{:S(2)}) collective-permute-start(bf16[6,352,128]{2,1,0:T(8,128)(2,1)S(1)} %get-tuple-element.54), channel_id=1, source_target_pairs={{0,96},{1,33},{2,98},{3,35},{4,100},{5,37},{6,102},{7,39},{8,104},... | collective-permute-start | bytes 1622024 | tf_op jit(solution)/shard_map/ppermute | solution.py:34
  18.7 5.1 %collective-permute-start.7 = (bf16[6,160,128]{2,1,0:T(8,128)(2,1)S(1)}, bf16[6,160,128]{2,1,0:T(8,128)(2,1)S(1)}, u32[]{:S(2)}, u32[]{:S(2)}) collective-permute-start(bf16[6,160,128]{2,1,0:T(8,128)(2,1)S(1)} %get-tuple-element.55), channel_id=1, source_target_pairs={{0,16},{1,17},{2,18},{3,19},{4,20},{5,21},{6,22},{7,23},{8,24},{9,... | collective-permute-start | bytes 737288 | tf_op jit(solution)/shard_map/ppermute | solution.py:34
  28.1 8.7 %collective-permute-start.8 = (bf16[3,512,128]{2,1,0:T(8,128)(2,1)S(1)}, bf16[3,512,128]{2,1,0:T(8,128)(2,1)S(1)}, u32[]{:S(2)}, u32[]{:S(2)}) collective-permute-start(bf16[3,512,128]{2,1,0:T(8,128)(2,1)S(1)} %get-tuple-element.56.refs_0_), channel_id=1, source_target_pairs={{0,8},{1,9},{2,10},{3,11},{4,12},{5,13},{6,14},{7,15},{8,0},{9,1},... | collective-permute-start | bytes 1179656 | tf_op jit(solution)/shard_map/ppermute | solution.py:34
  31.1 10.2 %collective-permute-start.11 = (bf16[3,512,128]{2,1,0:T(8,128)(2,1)S(1)}, bf16[3,512,128]{2,1,0:T(8,128)(2,1)S(1)}, u32[]{:S(2)}, u32[]{:S(2)}) collective-permute-start(bf16[3,512,128]{2,1,0:T(8,128)(2,1)S(1)} %get-tuple-element.57.refs_2_.refs_4_), channel_id=1, source_target_pairs={{0,2},{1,7},{2,4},{3,1},{4,6},{5,3},{6,0},{7,5},{8,10},{9,15},{10,... | collective-permute-start | bytes 1179656 | tf_op jit(solution)/shard_map/ppermute | solution.py:34
  31.2 10.2 %collective-permute-start.9 = (bf16[3,512,128]{2,1,0:T(8,128)(2,1)S(1)}, bf16[3,512,128]{2,1,0:T(8,128)(2,1)S(1)}, u32[]{:S(2)}, u32[]{:S(2)}) collective-permute-start(bf16[3,512,128]{2,1,0:T(8,128)(2,1)S(1)} %get-tuple-element.56.refs_0_), channel_id=1, source_target_pairs={{0,1},{1,0},{2,3},{3,2},{4,5},{5,4},{6,7},{7,6},{8,9},{9,8},{10,11... | collective-permute-start | bytes 1179656 | tf_op jit(solution)/shard_map/ppermute | solution.py:34
  34.8 11.2 %collective-permute-start.12 = (bf16[3,512,128]{2,1,0:T(8,128)(2,1)S(1)}, bf16[3,512,128]{2,1,0:T(8,128)(2,1)S(1)}, u32[]{:S(2)}, u32[]{:S(2)}) collective-permute-start(bf16[3,512,128]{2,1,0:T(8,128)(2,1)S(1)} %get-tuple-element.57.refs_2_.refs_4_), channel_id=1, source_target_pairs={{0,6},{1,3},{2,0},{3,5},{4,2},{5,7},{6,4},{7,1},{8,14},{9,11},{10,... | collective-permute-start | bytes 1179656 | tf_op jit(solution)/shard_map/ppermute | solution.py:34
  36.8 12.6 %collective-permute-start.10 = (bf16[3,512,128]{2,1,0:T(8,128)(2,1)S(1)}, bf16[3,512,128]{2,1,0:T(8,128)(2,1)S(1)}, u32[]{:S(2)}, u32[]{:S(2)}) collective-permute-start(bf16[3,512,128]{2,1,0:T(8,128)(2,1)S(1)} %collective-permute-done.8.refs_0_.refs_1_), channel_id=1, source_target_pairs={{0,1},{1,0},{2,3},{3,2},{4,5},{5,4},{6,7},{7,6},{8,9},{9,8},{10,11... | collective-permute-start | bytes 1179656 | tf_op jit(solution)/shard_map/ppermute | solution.py:34
  41.2 13.1 %collective-permute-start.13 = (bf16[3,512,128]{2,1,0:T(8,128)(2,1)S(1)}, bf16[3,512,128]{2,1,0:T(8,128)(2,1)S(1)}, u32[]{:S(2)}, u32[]{:S(2)}) collective-permute-start(bf16[3,512,128]{2,1,0:T(8,128)(2,1)S(1)} %collective-permute-done.11.refs_2_.refs_5_), channel_id=1, source_target_pairs={{0,2},{1,7},{2,4},{3,1},{4,6},{5,3},{6,0},{7,5},{8,10},{9,15},{10,... | collective-permute-start | bytes 1179656 | tf_op jit(solution)/shard_map/ppermute | solution.py:34
  59.5 73.4 %collective-permute-start.14 = (f32[2,3,16,128]{3,2,1,0:T(8,128)S(1)}, f32[2,3,16,128]{3,2,1,0:T(8,128)S(1)}, u32[]{:S(2)}, u32[]{:S(2)}) collective-permute-start(f32[2,3,16,128]{3,2,1,0:T(8,128)S(1)} %get-tuple-element.76), channel_id=1, source_target_pairs={{0,1},{1,0},{2,3},{3,2},{4,5},{5,4},{6,7},{7,6},{8,9},{9,8},{10,11... | collective-permute-start | bytes 147464 | tf_op jit(solution)/shard_map/ppermute | solution.py:34
  131.9 2.9 %collective-permute-start.15 = (f32[2,3,16,128]{3,2,1,0:T(8,128)S(1)}, f32[2,3,16,128]{3,2,1,0:T(8,128)S(1)}, u32[]{:S(2)}, u32[]{:S(2)}) collective-permute-start(f32[2,3,16,128]{3,2,1,0:T(8,128)S(1)} %get-tuple-element.78), channel_id=1, source_target_pairs={{0,2},{1,3},{2,0},{3,1},{4,6},{5,7},{6,4},{7,5},{8,10},{9,11},{10,... | collective-permute-start | bytes 147464 | tf_op jit(solution)/shard_map/ppermute | solution.py:34
  134.9 4.3 %collective-permute-start.16 = (f32[3,16,128]{2,1,0:T(8,128)S(1)}, f32[3,16,128]{2,1,0:T(8,128)S(1)}, u32[]{:S(2)}, u32[]{:S(2)}) collective-permute-start(f32[3,16,128]{2,1,0:T(8,128)S(1)} %get-tuple-element.80), channel_id=1, source_target_pairs={{0,8},{1,9},{2,10},{3,11},{4,12},{5,13},{6,14},{7,15},{8,0},{9,1},... | collective-permute-start | bytes 73736 | tf_op jit(solution)/shard_map/ppermute | solution.py:34
  135.1 4.0 %collective-permute-start.17 = (f32[3,16,128]{2,1,0:T(8,128)S(1)}, f32[3,16,128]{2,1,0:T(8,128)S(1)}, u32[]{:S(2)}, u32[]{:S(2)}) collective-permute-start(f32[3,16,128]{2,1,0:T(8,128)S(1)} %get-tuple-element.82), channel_id=1, source_target_pairs={{0,6},{1,7},{2,4},{3,5},{4,2},{5,3},{6,0},{7,1},{8,14},{9,15},{10,... | collective-permute-start | bytes 73736 | tf_op jit(solution)/shard_map/ppermute | solution.py:34
  139.2 8.8 %collective-permute-start.18 = (f32[3,2,2,4,128]{4,3,2,1,0:T(4,128)S(1)}, f32[3,2,2,4,128]{4,3,2,1,0:T(4,128)S(1)}, u32[]{:S(2)}, u32[]{:S(2)}) collective-permute-start(f32[3,2,2,4,128]{4,3,2,1,0:T(4,128)S(1)} %shard_map.54.own), channel_id=1, source_target_pairs={{0,0},{1,2},{2,1},{3,4},{4,3},{5,6},{6,5},{7,8},{8,7},{9,10},{10,9... | collective-permute-start | bytes 73736 | tf_op jit(solution)/shard_map/ppermute | solution.py:34
  145.7 2.2 %collective-permute-start.19 = (f32[3,2,2,4,128]{4,3,2,1,0:T(4,128)S(1)}, f32[3,2,2,4,128]{4,3,2,1,0:T(4,128)S(1)}, u32[]{:S(2)}, u32[]{:S(2)}) collective-permute-start(f32[3,2,2,4,128]{4,3,2,1,0:T(4,128)S(1)} %shard_map.54.own), channel_id=1, source_target_pairs={{0,1},{1,0},{2,3},{3,2},{4,5},{5,4},{6,7},{7,6},{8,9},{9,8},{10,11... | collective-permute-start | bytes 73736 | tf_op jit(solution)/shard_map/ppermute | solution.py:34
